TPU v7x, 512 devices: a whole 4x8x8 slice. The times are simulated.
512 devices in a mesh: dp: 128 (over y, z, core), mp: 4 (over x).
Axes of the slice: x: 4, y: 8, z: 8, core: 2. Of those that a mesh axis runs over, the one named last changes fastest.
Arguments:
- frames: bfloat16 [32768, 1024], P('dp'), may hold values from -24 to 24
- proj_in: bfloat16 [1024, 2, 1024], P(None, None, 'mp'), may hold values from -0.1875 to 0.1875
- depthwise: float32 [31, 1024], P(None, 'mp'), may hold values from -1 to 1
- bn_gain: float32 [1024], P('mp'), may hold values from 0.5 to 1.5
- bn_shift: float32 [1024], P('mp'), may hold values from -3 to 3
- proj_out: bfloat16 [1024, 1024], P(None, 'mp'), may hold values from -0.1875 to 0.1875
- grad_out: bfloat16 [32768, 1024], P('dp'), may hold values from -24 to 24
- counts: int32 [128], replicated, may hold values from 1 to 2, as said below
- lengths: int32 [128, 2], P('dp'), may hold values from 1 to 255, as said below
Outputs:
- frame_grad: bfloat16 [32768, 1024], P('dp', 'mp')
- in_grad: float32 [1024, 2, 1024], P('dp', None, 'mp')
- out_grad: float32 [1024, 1024], P('dp', 'mp')
- depth_grad: float32 [31, 1024], P(None, 'mp')
- gain_grad: float32 [1024], P('mp')
- shift_grad: float32 [1024], P('mp')
Inputs may be any that keep to these rules, and one draw needn't show every extreme that they name: `counts`: some device holds 2 live blocks. lengths[d] sums to 128 * counts[d]; on some device with 2 live blocks one utterance holds all frames but one for each other utterance.
All inputs are finite; a program needn't handle non-finite values.
Results may differ from a plain program's by a relative error of at most 0.0095.
Values may be sent and summed in bfloat16 or wider, within the bound.
No kernel may reach another device: no remote copies, remote signals or barrier semaphores. Data moves between devices by JAX's collectives and lax.ppermute only.
A program may use at most 64 MiB of HBM per device.

v0:
```python
import jax
import jax.numpy as jnp
from jax import lax
from jax.sharding import PartitionSpec as P

BLOCK = 128


def time_shift(values, offset, fill_value):
    if offset > 0:
        pad_part = jnp.full((offset,) + values.shape[1:], fill_value, values.dtype)
        return jnp.concatenate([values[offset:], pad_part], axis=0)
    if offset < 0:
        pad_part = jnp.full((-offset,) + values.shape[1:], fill_value, values.dtype)
        return jnp.concatenate([pad_part, values[:offset]], axis=0)
    return values


def tap_term(glu_float, owner_id, live_col, offset):
    same_utt = (time_shift(owner_id, offset, -1) == owner_id).astype(jnp.float32)[
        :, None
    ] * live_col
    return time_shift(glu_float, offset, 0.0) * same_utt


def shards(frames, proj_in, depthwise, bn_gain, bn_shift, proj_out, grad_out, counts, lengths):
    frames_dev = frames.shape[0]
    model_width = frames.shape[1]
    channels = proj_in.shape[2]
    tap_count = depthwise.shape[0]
    radius = tap_count // 2
    rows_dev = model_width // lax.axis_size("dp")
    position = jnp.arange(frames_dev, dtype=jnp.int32)
    utt_ends = jnp.cumsum(lengths[0])
    owner_id = jnp.sum((position[:, None] >= utt_ends[None, :]).astype(jnp.int32), axis=1)
    my_count = counts[lax.axis_index("dp")]
    live_col = (position < my_count * BLOCK).astype(jnp.float32)[:, None]
    frame_total = (jnp.sum(counts) * BLOCK).astype(jnp.float32)
    proj_flat = proj_in.reshape(model_width, 2 * channels)
    pre_act = jnp.dot(frames, proj_flat, preferred_element_type=jnp.float32)
    value_half = pre_act[:, :channels]
    gate_sig = jax.nn.sigmoid(pre_act[:, channels:])
    glu_out = (value_half * gate_sig * live_col).astype(jnp.bfloat16)
    glu_float = lax.optimization_barrier(glu_out).astype(jnp.float32)
    conv_out = jnp.zeros((frames_dev, channels), jnp.float32)
    for tap_index in range(tap_count):
        conv_out = conv_out + depthwise[tap_index] * tap_term(
            glu_float, owner_id, live_col, tap_index - radius
        )
    sum_val, sum_sq = lax.psum(
        (jnp.sum(conv_out, axis=0), jnp.sum(conv_out * conv_out, axis=0)), "dp"
    )
    mean_val = sum_val / frame_total
    square_mean = sum_sq / frame_total
    inv_std = lax.rsqrt(square_mean - mean_val * mean_val + 1e-05)
    normed = (conv_out - mean_val) * inv_std
    scaled = normed * bn_gain + bn_shift
    sig_scaled = jax.nn.sigmoid(scaled)
    hidden = (scaled * sig_scaled * live_col).astype(jnp.bfloat16)
    grad_hidden = jnp.dot(grad_out, proj_out, preferred_element_type=jnp.float32) * live_col
    grad_scaled = grad_hidden * sig_scaled * (1.0 + scaled * (1.0 - sig_scaled))
    local_shift = jnp.sum(grad_scaled, axis=0)
    local_gain = jnp.sum(grad_scaled * normed, axis=0)
    shift_grad, gain_grad = lax.psum((local_shift, local_gain), "dp")
    grad_conv = (
        live_col
        * bn_gain
        * inv_std
        * (grad_scaled - shift_grad / frame_total - normed * gain_grad / frame_total)
    )
    depth_rows = []
    for tap_index in range(tap_count):
        depth_rows.append(
            jnp.sum(grad_conv * tap_term(glu_float, owner_id, live_col, tap_index - radius), axis=0)
        )
    depth_grad = lax.psum(jnp.stack(depth_rows), "dp")
    grad_glu = jnp.zeros((frames_dev, channels), jnp.float32)
    for tap_index in range(tap_count):
        offset = tap_index - radius
        back_same = (time_shift(owner_id, -offset, -1) == owner_id).astype(jnp.float32)[
            :, None
        ] * live_col
        grad_glu = grad_glu + depthwise[tap_index] * time_shift(grad_conv, -offset, 0.0) * back_same
    grad_value = grad_glu * gate_sig
    grad_gate = grad_glu * value_half * gate_sig * (1.0 - gate_sig)
    grad_flat = jnp.concatenate([grad_value, grad_gate], axis=1).astype(jnp.bfloat16)
    frame_term = lax.dot_general(
        grad_flat, proj_flat, (((1,), (1,)), ((), ())), preferred_element_type=jnp.float32
    )
    frame_grad = lax.psum_scatter(
        frame_term.astype(jnp.bfloat16), "mp", scatter_dimension=1, tiled=True
    )
    summed = lax.psum_scatter(
        jnp.concatenate(
            [
                lax.dot_general(
                    frames, grad_flat, (((0,), (0,)), ((), ())), preferred_element_type=jnp.float32
                ),
                lax.dot_general(
                    grad_out, hidden, (((0,), (0,)), ((), ())), preferred_element_type=jnp.float32
                ),
            ],
            axis=1,
        ),
        "dp",
        scatter_dimension=0,
        tiled=True,
    )
    in_flat = summed[:, : 2 * channels]
    out_grad = summed[:, 2 * channels :]
    in_grad = in_flat.reshape(rows_dev, 2, channels)
    return (frame_grad, in_grad, out_grad, depth_grad, gain_grad, shift_grad)


def solution(mesh):
    placed = (
        P("dp", None),
        P(None, None, "mp"),
        P(None, "mp"),
        P("mp"),
        P("mp"),
        P(None, "mp"),
        P("dp", None),
        P(),
        P("dp", None),
    )
    return jax.shard_map(
        shards,
        mesh=mesh,
        in_specs=placed,
        out_specs=(
            P("dp", "mp"),
            P("dp", None, "mp"),
            P("dp", "mp"),
            P(None, "mp"),
            P("mp"),
            P("mp"),
        ),
        check_vma=False,
    )
```

profile of v0, /device:TPU:6, one launch (start us, length us, event | category | flops | bytes accessed | tf_op | source)
XLA Modules:
  0.0 1084.7 jit_solution(16203160187497668343)
XLA Ops:
  7.2 0.9 reduce-window.8
  8.2 0.7 fusion.86
  8.9 0.6 fusion.93
  9.5 0.6 fusion.85
  10.8 0.6 fusion.84
  11.4 0.7 fusion.90
  12.1 0.7 fusion.83
  13.4 0.6 fusion.82
  17.8 1.6 fusion.78
  19.4 1.7 fusion.77
  21.0 1.4 reduce_sum.335
  22.4 1.2 dynamic_slice.3
  24.2 1.4 copy.25
  26.2 0.8 fusion.69
  27.1 0.9 fusion.68
  27.9 0.8 fusion.67
  28.7 0.8 fusion.66
  29.6 0.8 fusion.65
  30.4 0.8 fusion.64
  31.2 0.8 fusion.63
  32.0 0.9 fusion.62
  32.9 0.8 fusion.71
  33.7 0.7 fusion.70
  34.4 0.8 fusion.73
  35.2 0.7 fusion.72
  35.9 0.9 fusion.76
  36.8 0.8 fusion.75
  37.6 0.7 fusion.74
  39.0 0.9 fusion.14
  40.1 0.9 fusion.13
  41.1 6.2 multiply_reduce_fusion.32
  47.6 258.3 %all-reduce.89 = (f32[256]{0:T(256)S(1)}, f32[256]{0:T(256)S(1)}) all-reduce(f32[256]{0:T(256)} %get-tuple-element.58, f32[256]{0:T(256)S(1)} %get-tuple-element.57), channel_id=1, replica_groups=mesh['dp'=128,'mp'=4] {'dp'}, use_global_device_ids=true, to_apply=%region_6.7 | all-reduce | flops 512 | bytes 4096 | tf_op jit(solution)/shard_map/psum | solution.py:50
  306.0 2.3 fusion.46
  308.3 247.3 %all-reduce.88 = (f32[256]{0:T(256)}, f32[256]{0:T(256)S(1)}) all-reduce(f32[256]{0:T(256)S(1)} %get-tuple-element.56, f32[256]{0:T(256)S(1)} %get-tuple-element.55), channel_id=1, replica_groups=mesh['dp'=128,'mp'=4] {'dp'}, use_global_device_ids=true, to_apply=%region_10.11 | all-reduce | flops 512 | bytes 4096 | tf_op jit(solution)/shard_map/psum | solution.py:64
  556.2 2.9 multiply_reduce_fusion
  560.5 1.5 convolution_bitcast_fusion.1
  562.3 3.4 multiply_convert_fusion.2
  567.0 1.9 pad_maximum_fusion
  568.9 3.5 copy.21
  572.5 2.3 convolution_convert_fusion
  574.8 2.3 multiply_reduce_fusion.27
  577.2 2.5 multiply_reduce_fusion.18
  579.7 1.1 multiply_reduce_fusion.9
  580.9 2.8 stack.127
  583.7 491.3 %psum.39 = f32[31,256]{1,0:T(8,128)} all-reduce(f32[31,256]{1,0:T(8,128)S(1)} %stack.127), channel_id=1, replica_groups=mesh['dp'=128,'mp'=4] {'dp'}, use_global_device_ids=true, to_apply=%region_44.45 | all-reduce | flops 7936 | bytes 63488 | tf_op jit(solution)/shard_map/psum | solution.py:76
  1075.0 0.7 slice.683
  1075.9 0.7 copy.19
  1076.6 1.3 slice.684
  (210 shorter events, 8.8 us)
Async XLA Ops:
  7.2 18.5 %copy-start = (bf16[256,1024]{1,0:T(8,128)(2,1)S(1)}, bf16[256,1024]{1,0:T(8,128)(2,1)}, u32[]{:S(2)}) copy-start(bf16[256,1024]{1,0:T(8,128)(2,1)} %param.9) | copy-start | bytes 1572868
  7.2 1067.8 %reduce-scatter.7.cloned.1.call-start = ((), (), s32[]{:S(2)}) async-start(), calls=%async_computation.3 | async-start | bytes 3170304
  38.4 9.0 copy-start.1
  39.9 7.4 copy-start.28
  39.9 7.4 copy-start.30
  40.0 7.4 copy-start.33
  40.0 7.4 copy-start.36
  40.0 7.4 copy-start.38
  40.0 7.4 copy-start.40
  40.0 7.4 copy-start.42
  40.0 7.4 copy-start.44
  40.0 7.4 copy-start.46
  40.0 7.4 copy-start.48
  40.0 7.4 copy-start.50
  40.0 7.4 copy-start.52
  40.1 7.4 copy-start.54
  40.1 7.4 copy-start.56
  41.0 6.5 copy-start.14
  41.0 6.5 copy-start.16
  41.0 6.5 copy-start.18
  41.0 6.5 copy-start.20
  41.0 6.5 copy-start.22
  41.0 6.5 copy-start.24
  41.0 6.5 copy-start.26
  41.0 6.5 copy-start.58
  41.0 6.5 copy-start.60
  41.1 6.5 copy-start.62
  41.1 6.5 copy-start.64
  41.1 6.5 copy-start.66
  41.1 6.5 copy-start.68
  41.1 6.5 copy-start.70
  305.9 249.7 %copy-start.84 = (f32[256]{0:T(256)}, f32[256]{0:T(256)S(1)}, u32[]{:S(2)}) copy-start(f32[256]{0:T(256)S(1)} %get-tuple-element.67) | copy-start | bytes 3076
  305.9 253.2 %copy-start.83 = (f32[256]{0:T(256)}, f32[256]{0:T(256)S(1)}, u32[]{:S(2)}) copy-start(f32[256]{0:T(256)S(1)} %get-tuple-element.66) | copy-start | bytes 3076
  559.6 2.3 copy-start.15
  559.6 2.3 copy-start.17
  559.6 2.3 copy-start.19
  572.4 4.8 copy-start.2
  572.4 4.8 copy-start.35
  572.4 7.3 copy-start.3
  572.4 7.3 copy-start.32
  572.4 505.4 %reduce-scatter.5.cloned.1.call-start = ((), (), s32[]{:S(2)}) async-start(), calls=%async_computation.2 | async-start | bytes 655360 | tf_op jit(solution)/shard_map/reduce_scatter | solution.py:90
  574.8 4.9 copy-start.4
  574.8 4.9 copy-start.5
  574.8 4.9 copy-start.6
  574.8 4.9 copy-start.7
  574.8 4.9 copy-start.8
  574.8 4.9 copy-start.9
  574.8 4.9 copy-start.10
  (40 other events, 87.0 us)
Sparse Core Ops, SparseCore 0:
  572.5 194.4 reduce-scatter.6
  770.4 22.5 reduce-scatter.4
where the time goes:
time: 1090 us; the launch traced here: 1080 us
  blocking collectives  997 us (91%)
  local copies, waits for them, and re-layouts  39.2 us (4%)
  other arithmetic  24.7 us (2%)
  between operations  16.7 us (2%)
    psum x1, blocking collectives, shards(): depth_grad = lax.psum(jnp.stack(depth_rows), 'dp')  491 us
    psum x1, blocking collectives, shards(): lax.psum((jnp.sum(conv_out, axis=0), jnp.sum(conv_out * conv_out, axis=0)...  258 us
    psum x1, blocking collectives, shards(): shift_grad, gain_grad = lax.psum((local_shift, local_gain), 'dp')  247 us
  transfers between devices with their start and end apart: 2, of which 0 were waited for; matrix products, arithmetic and copies ran while one was open for 1% of the time, Pallas kernels for 0%

commit v1 on v0

--- a/solution.py
+++ b/solution.py
@@ -1,9 +1,10 @@
 import jax
 import jax.numpy as jnp
 from jax import lax
-from jax.sharding import PartitionSpec as P
+from jax.sharding import Mesh, PartitionSpec as P
 
 BLOCK = 128
+DP = ("y", "z", "core")
 
 
 def time_shift(values, offset, fill_value):
@@ -23,17 +24,38 @@
     return time_shift(glu_float, offset, 0.0) * same_utt
 
 
+def small_sum(x):
+    x = lax.psum(x, "core")
+    peers = lax.axis_size("y") * lax.axis_size("z")
+    every = jnp.broadcast_to(x[None], (peers,) + x.shape)
+    return jnp.sum(lax.all_to_all(every, ("y", "z"), 0, 0), axis=0)
+
+
+def scatter_sum(partial):
+    peers = lax.axis_size("y") * lax.axis_size("z")
+    rows = partial.shape[0] // (2 * peers)
+    parts = partial.reshape(peers, 2, rows, partial.shape[1])
+    core = lax.axis_index("core")
+    keep = lax.dynamic_index_in_dim(parts, core, 1, keepdims=False)
+    send = lax.dynamic_index_in_dim(parts, 1 - core, 1, keepdims=False).astype(jnp.bfloat16)
+    got = lax.ppermute(send, "core", [(0, 1), (1, 0)])
+    both = (keep + got.astype(jnp.float32)).astype(jnp.bfloat16)
+    every = lax.all_to_all(both, ("y", "z"), 0, 0)
+    return jnp.sum(every.astype(jnp.float32), axis=0)
+
+
 def shards(frames, proj_in, depthwise, bn_gain, bn_shift, proj_out, grad_out, counts, lengths):
     frames_dev = frames.shape[0]
     model_width = frames.shape[1]
     channels = proj_in.shape[2]
     tap_count = depthwise.shape[0]
     radius = tap_count // 2
-    rows_dev = model_width // lax.axis_size("dp")
+    rows_dev = model_width // lax.axis_size(DP)
+    groups = lax.axis_size("mp")
     position = jnp.arange(frames_dev, dtype=jnp.int32)
     utt_ends = jnp.cumsum(lengths[0])
     owner_id = jnp.sum((position[:, None] >= utt_ends[None, :]).astype(jnp.int32), axis=1)
-    my_count = counts[lax.axis_index("dp")]
+    my_count = counts[lax.axis_index(DP)]
     live_col = (position < my_count * BLOCK).astype(jnp.float32)[:, None]
     frame_total = (jnp.sum(counts) * BLOCK).astype(jnp.float32)
     proj_flat = proj_in.reshape(model_width, 2 * channels)
@@ -47,8 +69,8 @@
         conv_out = conv_out + depthwise[tap_index] * tap_term(
             glu_float, owner_id, live_col, tap_index - radius
         )
-    sum_val, sum_sq = lax.psum(
-        (jnp.sum(conv_out, axis=0), jnp.sum(conv_out * conv_out, axis=0)), "dp"
+    sum_val, sum_sq = small_sum(
+        jnp.stack([jnp.sum(conv_out, axis=0), jnp.sum(conv_out * conv_out, axis=0)])
     )
     mean_val = sum_val / frame_total
     square_mean = sum_sq / frame_total
@@ -61,7 +83,7 @@
     grad_scaled = grad_hidden * sig_scaled * (1.0 + scaled * (1.0 - sig_scaled))
     local_shift = jnp.sum(grad_scaled, axis=0)
     local_gain = jnp.sum(grad_scaled * normed, axis=0)
-    shift_grad, gain_grad = lax.psum((local_shift, local_gain), "dp")
+    shift_grad, gain_grad = small_sum(jnp.stack([local_shift, local_gain]))
     grad_conv = (
         live_col
         * bn_gain
@@ -73,7 +95,7 @@
         depth_rows.append(
             jnp.sum(grad_conv * tap_term(glu_float, owner_id, live_col, tap_index - radius), axis=0)
         )
-    depth_grad = lax.psum(jnp.stack(depth_rows), "dp")
+    depth_grad = lax.psum(lax.psum(lax.psum(jnp.stack(depth_rows), "core"), "y"), "z")
     grad_glu = jnp.zeros((frames_dev, channels), jnp.float32)
     for tap_index in range(tap_count):
         offset = tap_index - radius
@@ -85,12 +107,12 @@
     grad_gate = grad_glu * value_half * gate_sig * (1.0 - gate_sig)
     grad_flat = jnp.concatenate([grad_value, grad_gate], axis=1).astype(jnp.bfloat16)
     frame_term = lax.dot_general(
-        grad_flat, proj_flat, (((1,), (1,)), ((), ())), preferred_element_type=jnp.float32
-    )
-    frame_grad = lax.psum_scatter(
-        frame_term.astype(jnp.bfloat16), "mp", scatter_dimension=1, tiled=True
-    )
-    summed = lax.psum_scatter(
+        proj_flat, grad_flat, (((1,), (1,)), ((), ())), preferred_element_type=jnp.float32
+    ).T.astype(jnp.bfloat16)
+    frame_parts = frame_term.reshape(frames_dev, groups, model_width // groups)
+    frame_parts = lax.all_to_all(jnp.swapaxes(frame_parts, 0, 1), "mp", 0, 0)
+    frame_grad = jnp.sum(frame_parts.astype(jnp.float32), axis=0).astype(jnp.bfloat16)
+    summed = scatter_sum(
         jnp.concatenate(
             [
                 lax.dot_general(
@@ -101,10 +123,7 @@
                 ),
             ],
             axis=1,
-        ),
-        "dp",
-        scatter_dimension=0,
-        tiled=True,
+        )
     )
     in_flat = summed[:, : 2 * channels]
     out_grad = summed[:, 2 * channels :]
@@ -113,25 +132,26 @@
 
 
 def solution(mesh):
+    grid = Mesh(mesh.devices.reshape(8, 8, 2, 4), ("y", "z", "core", "mp"))
     placed = (
-        P("dp", None),
+        P(DP, None),
         P(None, None, "mp"),
         P(None, "mp"),
         P("mp"),
         P("mp"),
         P(None, "mp"),
-        P("dp", None),
+        P(DP, None),
         P(),
-        P("dp", None),
+        P(DP, None),
     )
     return jax.shard_map(
         shards,
-        mesh=mesh,
+        mesh=grid,
         in_specs=placed,
         out_specs=(
-            P("dp", "mp"),
-            P("dp", None, "mp"),
-            P("dp", "mp"),
+            P(DP, "mp"),
+            P(DP, None, "mp"),
+            P(DP, "mp"),
             P(None, "mp"),
             P("mp"),
             P("mp"),

time: 1090 us -> 198 us (0.18)
  blocking collectives: 997 us -> 69.7 us
  starting transfers between devices: 0.08 us -> 33.8 us
  waiting for transfers between devices: 0.04 us -> 26.9 us
  local copies, waits for them, and re-layouts: 39.2 us -> 23.4 us
  between operations: 16.7 us -> 3.18 us
    psum x3 -> x5, blocking collectives: 997 us -> 69.7 us  [the longest x1 30.2 us: shards(): lax.psum(lax.psum(lax.psum(jnp.stack(depth_rows), 'core'), 'y'), 'z')]
    all_to_all x0 -> x4, starting transfers between devices: none -> 31.9 us  [the longest x2 22.3 us: small_sum(): return jnp.sum(lax.all_to_all(every, ('y', 'z'), 0, 0), axis=0)]
    all_to_all x0 -> x4, waiting for transfers between devices: none -> 26.9 us  [the longest x2 21.6 us: small_sum(): return jnp.sum(lax.all_to_all(every, ('y', 'z'), 0, 0), axis=0)]
    slice x29, local copies, waits for them, and re-layouts: 21 us -> 1.56 us  [time_shift(): return jnp.concatenate([pad_part, values[:offset]], axis=0)]
  transfers between devices with their start and end apart: 2 -> 5, of which waited for: 0 -> 3; matrix products, arithmetic and copies ran while one was open for 1% -> 9% of each run, Pallas kernels for 0% -> 0%
where the time goes in v1:
time: 198 us; the launch traced here: 197 us
  blocking collectives  69.7 us (35%)
  starting transfers between devices  33.8 us (17%)
  other arithmetic  32.5 us (16%)
  waiting for transfers between devices  26.9 us (14%)
  local copies, waits for them, and re-layouts  23.4 us (12%)
  matrix products  7.04 us (4%)
  between operations  3.18 us (2%)
    psum x1, blocking collectives, shards(): lax.psum(lax.psum(lax.psum(jnp.stack(depth_rows), 'core'), 'y'), 'z')  30.2 us
    psum x1, blocking collectives, shards(): lax.psum(lax.psum(jnp.stack(depth_rows), 'core'), 'y')  29.8 us
    all_to_all x2, starting transfers between devices, small_sum(): return jnp.sum(lax.all_to_all(every, ('y', 'z'), 0, 0), axis=0)  22.3 us
    all_to_all x2, waiting for transfers between devices, small_sum(): return jnp.sum(lax.all_to_all(every, ('y', 'z'), 0, 0), axis=0)  21.6 us
    reduce_sum x4, other arithmetic, shards(): jnp.sum(grad_conv * tap_term(glu_float, owner_id, live_col, tap_index - r...  8.92 us
    psum x2, blocking collectives, small_sum(): x = lax.psum(x, 'core')  6.29 us
    all_to_all x1, waiting for transfers between devices, shards(): frame_parts = lax.all_to_all(jnp.swapaxes(frame_parts, 0, 1), 'mp', 0, 0)  5.33 us
    another operation x3, other arithmetic  4.9 us
  transfers between devices with their start and end apart: 5, of which 3 were waited for; matrix products, arithmetic and copies ran while one was open for 9% of the time, Pallas kernels for 0%

profile of v1, /device:TPU:6, one launch (start us, length us, event | category | flops | bytes accessed | tf_op | source)
XLA Modules:
  0.0 196.5 jit_solution(1703413751848722447)
XLA Ops:
  0.7 0.9 reduce-window.8
  2.7 1.2 dynamic_slice.10
  4.6 1.5 copy.31
  8.0 1.1 fusion.80
  9.1 0.6 fusion.81
  9.7 0.7 fusion.16
  10.5 0.7 fusion.15
  11.3 3.9 %fusion.49 = (f32[256]{0:T(256)S(1)}, f32[256]{0:T(256)S(1)}, f32[256,256]{1,0:T(8,128)S(1)}) fusion(f32[256]{0:T(256)S(1)} %get-tuple-element.142, f32[241,256]{1,0:T(8,128)S(1)} %get-tuple-element.78, f32[256]{0:T(256)} %bitcast.33, f32[256]{0:T(256)S(1)} %get-tuple-element.143, f32[242,256]{1,0:T(8,128)S(1)} %get-tuple-element.80, f32[256]{0:T(256)} %bitcast.32, ...), kind=kLoop, calls=%fused_computation.171 | loop fusion | flops 6290944 | bytes 8077312 | tf_op jit(solution)/shard_map/reduce_sum | solution.py:73
  15.5 0.6 pad_maximum_fusion.4
  16.1 3.1 %psum.35 = f32[2,256]{1,0:T(2,128)} all-reduce(f32[2,256]{1,0:T(2,128)} %pad_maximum_fusion.4), channel_id=1, replica_groups=mesh['y'=8,'z'=8,'core'=2,'mp'=4] {'core'}, use_global_device_ids=true, to_apply=%region_4.5 | all-reduce | flops 512 | bytes 4096 | tf_op jit(solution)/shard_map/psum | solution.py:28
  19.2 1.4 broadcast_in_dim.4
  20.6 16.9 %all-to-all-start = ((f32[64,2,256]{2,1,0:T(2,128)}), f32[64,2,256]{2,1,0:T(2,128)}, u32[]{:S(2)}, u32[]{:S(2)}) async-start(f32[64,2,256]{2,1,0:T(2,128)} %broadcast_in_dim.4), calls=%async_computation | async-start | bytes 262144 | tf_op jit(solution)/shard_map/all_to_all | solution.py:31
  37.5 1.3 reduce_sum.376
  39.4 10.9 %all-to-all-done = f32[64,2,256]{2,1,0:T(2,128)} async-done(((f32[64,2,256]{2,1,0:T(2,128)}), f32[64,2,256]{2,1,0:T(2,128)}, u32[]{:S(2)}, u32[]{:S(2)}) %all-to-all-start) | async-done | bytes 131104 | tf_op jit(solution)/shard_map/all_to_all | solution.py:31
  50.3 1.6 reduce_sum.375
  51.8 0.8 add_rsqrt_fusion
  53.2 2.2 %fusion.48 = (f32[256]{0:T(256)S(1)}, f32[256]{0:T(256)S(1)}, f32[256,256]{1,0:T(8,128)}) fusion(f32[256]{0:T(256)S(1)} %bitcast.118, f32[256,256]{1,0:T(8,128)S(1)} %get-tuple-element.46, f32[256]{0:T(256)S(1)} %bitcast.121, f32[256]{0:T(256)} %param.13, f32[256]{0:T(256)} %param.12, f32[256]{0:T(256)S(1)} %fusion.44, bf16[256,1024]{1,0:T(8,128)(2,1)} %param.15, ...), kind=kOutput, calls=%fused_computation.170 | convolution fusion | flops 135265792 | bytes 1580032 | tf_op jit(solution)/shard_map/dot_general | solution.py:82
  55.4 0.6 pad_maximum_fusion.5
  56.0 3.1 %psum.36 = f32[2,256]{1,0:T(2,128)} all-reduce(f32[2,256]{1,0:T(2,128)} %pad_maximum_fusion.5), channel_id=1, replica_groups=mesh['y'=8,'z'=8,'core'=2,'mp'=4] {'core'}, use_global_device_ids=true, to_apply=%region_9.10 | all-reduce | flops 512 | bytes 4096 | tf_op jit(solution)/shard_map/psum | solution.py:28
  59.2 1.4 broadcast_in_dim.5
  60.5 5.4 %all-to-all-start.1 = ((f32[64,2,256]{2,1,0:T(2,128)}), f32[64,2,256]{2,1,0:T(2,128)}, u32[]{:S(2)}, u32[]{:S(2)}) async-start(f32[64,2,256]{2,1,0:T(2,128)} %broadcast_in_dim.5), calls=%async_computation.1 | async-start | bytes 262144 | tf_op jit(solution)/shard_map/all_to_all | solution.py:31
  66.0 2.5 %convolution_bitcast_fusion.1 = f32[1024,256]{0,1:T(8,128)} fusion(bf16[256,1024]{1,0:T(8,128)(2,1)} %param.15, f32[256,256]{1,0:T(8,128)S(1)} %get-tuple-element.46, f32[256]{0:T(256)} %param.13, f32[256]{0:T(256)} %bitcast.122, f32[256]{0:T(256)} %bitcast.119, f32[256]{0:T(256)} %param.12, f32[256]{0:T(256)S(1)} %fusion.44), kind=kOutput, calls=%fused_computation.6 | convolution fusion | flops 134873088 | bytes 1840128 | tf_op jit(solution)/shard_map/dot_general | solution.py:121
  68.5 10.7 %all-to-all-done.1 = f32[64,2,256]{2,1,0:T(2,128)} async-done(((f32[64,2,256]{2,1,0:T(2,128)}), f32[64,2,256]{2,1,0:T(2,128)}, u32[]{:S(2)}, u32[]{:S(2)}) %all-to-all-start.1) | async-done | bytes 131104 | tf_op jit(solution)/shard_map/all_to_all | solution.py:31
  79.2 1.6 reduce_sum.379
  80.8 1.3 fusion.82
  82.1 2.9 %multiply_reduce_fusion = (f32[256]{0:T(256)}, f32[256]{0:T(256)}, f32[256]{0:T(256)}, f32[256]{0:T(256)}, f32[256]{0:T(256)}, /*index=5*/f32[256]{0:T(256)}, f3...) fusion(f32[241,256]{1,0:T(8,128)} %copy-done.28, f32[256]{0:T(256)S(1)} %get-tuple-element.142, ...), kind=kLoop, calls=%fused_computation.18 | loop fusion | flops 2356992 | bytes 3068932 | tf_op jit(solution)/shard_map/reduce_sum | solution.py:96
  86.2 3.9 %multiply_convert_fusion.2 = (bf16[256,256]{1,0:T(8,128)(2,1)S(1)}, f32[256,256]{1,0:T(8,128)S(1)}) fusion(f32[256,512]{1,0:T(8,128)S(1)} %fusion.98, f32[256]{0:T(256)} %get-tuple-element.172, f32[241,256]{1,0:T(8,128)S(1)} %get-tuple-element.48, f32[256]{0:T(256)} %bitcast.33, f32[256]{0:T(256)} %get-tuple-element.141, ...), kind=kLoop, calls=%fused_computation.51 | loop fusion | flops 6356992 | bytes 8599552 | tf_op jit(solution)/shard_map/convert.1
  91.4 1.9 pad_maximum_fusion
  93.3 3.5 %copy.23 = f32[1024,768]{1,0:T(8,128)} copy(f32[1024,768]{0,1:T(8,128)} %pad_maximum_fusion) | data formatting | bytes 6291456 | tf_op jit(solution)/shard_map/concatenate | solution.py:116
  96.9 2.4 %fusion.3 = bf16[64,8,768]{2,1,0:T(8,128)(2,1)} fusion(f32[64,2,8,768]{3,2,1,0:T(8,128)} %bitcast.101, s32[]{:T(128)S(6)} %select_n.12), kind=kLoop, calls=%fused_computation.11 | loop fusion | bytes 1572868 | tf_op jit(solution)/shard_map/convert_element_type | solution.py:40
  99.3 1.9 collective-permute-start
  101.2 1.4 convolution_convert_fusion
  102.6 0.9 copy.33
  103.5 4.8 %all-to-all-start.2 = ((bf16[4,256,256]{2,1,0:T(8,128)(2,1)}), bf16[4,256,256]{2,1,0:T(8,128)(2,1)S(1)}, u32[]{:S(2)}, u32[]{:S(2)}) async-start(bf16[4,256,256]{2,1,0:T(8,128)(2,1)} %bitcast.100), calls=%async_computation.2 | async-start | bytes 1048576 | tf_op jit(solution)/shard_map/all_to_all | solution.py:113
  108.2 2.7 %fusion = bf16[64,8,768]{2,1,0:T(8,128)(2,1)} fusion(bf16[64,8,768]{2,1,0:T(8,128)(2,1)} %collective-permute-done, f32[64,2,8,768]{3,2,1,0:T(8,128)} %bitcast.102, s32[]{:T(128)S(6)} %select_n.11), kind=kLoop, calls=%fused_computation.3 | loop fusion | flops 1179648 | bytes 3145732 | tf_op jit(solution)/shard_map/convert_element_type | solution.py:42
  111.0 5.3 %all-to-all-done.2 = bf16[4,256,256]{2,1,0:T(8,128)(2,1)S(1)} async-done(((bf16[4,256,256]{2,1,0:T(8,128)(2,1)}), bf16[4,256,256]{2,1,0:T(8,128)(2,1)S(1)}, u32[]{:S(2)}, u32[]{:S(2)}) %all-to-all-start.2) | async-done | bytes 524320 | tf_op jit(solution)/shard_map/all_to_all | solution.py:113
  116.3 0.8 copy-done.36
  117.1 4.8 %all-to-all-start.3 = ((bf16[64,8,768]{2,1,0:T(8,128)(2,1)}), bf16[64,8,768]{2,1,0:T(8,128)(2,1)S(1)}, u32[]{:S(2)}, u32[]{:S(2)}) async-start(bf16[64,8,768]{2,1,0:T(8,128)(2,1)} %fusion), calls=%async_computation.3 | async-start | bytes 1572864 | tf_op jit(solution)/shard_map/all_to_all | solution.py:43
  122.0 2.3 %multiply_reduce_fusion.27 = (f32[256]{0:T(256)}, f32[256]{0:T(256)}, f32[256]{0:T(256)}, f32[256]{0:T(256)}) fusion(f32[256,256]{1,0:T(8,128)S(1)} %get-tuple-element.41, f32[244,256]{1,0:T(8,128)} %copy-done.23, f32[256]{0:T(256)} %get-tuple-element.171, f32[256]{0:T(256)} %get-tuple-element.159, f32[243,256]{1,0:T(8,128)} %copy-done.22, ...), kind=kLoop, calls=%fused_computation.45 | loop fusion | flops 785408 | bytes 1263616 | tf_op jit(solution)/shard_map/reduce_sum | solution.py:96
  124.3 2.5 %multiply_reduce_fusion.18 = (f32[256]{0:T(256)}, f32[256]{0:T(256)}, f32[256]{0:T(256)}, f32[256]{0:T(256)}, f32[256]{0:T(256)}, /*index=5*/f32[256]{0:T(256)}, f32[256]{0:T(256)}, f32[256]{0:T(256)}, f32[256]{0:T(256)}) fusion(f32[256,256]{1,0:T(8,128)S(1)} %get-tuple-element.41, f32[253,256]{1,0:T(8,128)S(1)} %get-tuple-element.101, ...), kind=kLoop, calls=%fused_computation.36 | loop fusion | flops 1767168 | bytes 2575360 | tf_op jit(solution)/shard_map/reduce_sum | solution.py:96
  126.9 1.2 multiply_reduce_fusion.9
  128.1 2.9 %stack.151 = f32[31,256]{1,0:T(8,128)S(1)} concatenate(f32[1,256]{1,0:T(1,128)} %bitcast.128, f32[1,256]{1,0:T(1,128)} %bitcast.127, f32[1,256]{1,0:T(1,128)} %bitcast.126, f32[1,256]{1,0:T(1,128)} %bitcast.125, f32[1,256]{1,0:T(1,128)} %bitcast.137, f32[1,256]{1,0:T(1,128)} %bitcast.136, f32[1,256]{1,0:T(1,128)} %bitcast.135, f32[1,256]{1,0:T(1,128)} %bitcast.134, ...), dimensions={0} | concatenate | bytes 63488 | tf_op jit(solution)/shard_map/stack | solution.py:98
  131.0 3.4 %psum.37 = f32[31,256]{1,0:T(8,128)S(1)} all-reduce(f32[31,256]{1,0:T(8,128)S(1)} %stack.151), channel_id=1, replica_groups=mesh['y'=8,'z'=8,'core'=2,'mp'=4] {'core'}, use_global_device_ids=true, to_apply=%region_44.45 | all-reduce | flops 7936 | bytes 63488 | tf_op jit(solution)/shard_map/psum | solution.py:98
  134.4 29.8 %psum.38 = f32[31,256]{1,0:T(8,128)S(1)} all-reduce(f32[31,256]{1,0:T(8,128)S(1)} %psum.37), channel_id=1, replica_groups=mesh['y'=8,'z'=8,'core'=2,'mp'=4] {'y'}, use_global_device_ids=true, to_apply=%region_45.46 | all-reduce | flops 7936 | bytes 63488 | tf_op jit(solution)/shard_map/psum | solution.py:98
  164.2 30.2 %psum.39 = f32[31,256]{1,0:T(8,128)} all-reduce(f32[31,256]{1,0:T(8,128)S(1)} %psum.38), channel_id=1, replica_groups=mesh['y'=8,'z'=8,'core'=2,'mp'=4] {'z'}, use_global_device_ids=true, to_apply=%region_46.47 | all-reduce | flops 7936 | bytes 63488 | tf_op jit(solution)/shard_map/psum | solution.py:98
  194.4 0.7 reduce_sum.380
  195.3 0.6 slice.684
  195.9 0.6 reshape.163
  (200 shorter events, 5.9 us)
Async XLA Ops:
  0.6 5.4 %copy-start = (bf16[256,1024]{1,0:T(8,128)(2,1)S(1)}, bf16[256,1024]{1,0:T(8,128)(2,1)}, u32[]{:S(2)}) copy-start(bf16[256,1024]{1,0:T(8,128)(2,1)} %param.9) | copy-start | bytes 1572868
  6.7 4.5 %copy-start.4 = (f32[252,256]{1,0:T(8,128)}, f32[252,256]{1,0:T(8,128)S(1)}, u32[]{:S(2)}) copy-start(f32[252,256]{1,0:T(8,128)S(1)} %get-tuple-element.100) | copy-start | bytes 774148
  6.7 4.5 %copy-start.6 = (f32[253,256]{1,0:T(8,128)}, f32[253,256]{1,0:T(8,128)S(1)}, u32[]{:S(2)}) copy-start(f32[253,256]{1,0:T(8,128)S(1)} %get-tuple-element.102) | copy-start | bytes 777220
  6.8 4.4 %copy-start.8 = (f32[254,256]{1,0:T(8,128)}, f32[254,256]{1,0:T(8,128)S(1)}, u32[]{:S(2)}) copy-start(f32[254,256]{1,0:T(8,128)S(1)} %get-tuple-element.103) | copy-start | bytes 780292
  6.8 4.4 %copy-start.10 = (f32[254,256]{1,0:T(8,128)}, f32[254,256]{1,0:T(8,128)S(1)}, u32[]{:S(2)}) copy-start(f32[254,256]{1,0:T(8,128)S(1)} %get-tuple-element.104) | copy-start | bytes 780292
  6.8 4.4 %copy-start.12 = (f32[255,256]{1,0:T(8,128)}, f32[255,256]{1,0:T(8,128)S(1)}, u32[]{:S(2)}) copy-start(f32[255,256]{1,0:T(8,128)S(1)} %get-tuple-element.105) | copy-start | bytes 783364
  6.9 4.4 %copy-start.14 = (f32[255,256]{1,0:T(8,128)}, f32[255,256]{1,0:T(8,128)S(1)}, u32[]{:S(2)}) copy-start(f32[255,256]{1,0:T(8,128)S(1)} %get-tuple-element.106) | copy-start | bytes 783364
  6.9 4.3 %copy-start.3 = (f32[249,256]{1,0:T(8,128)}, f32[249,256]{1,0:T(8,128)S(1)}, u32[]{:S(2)}) copy-start(f32[249,256]{1,0:T(8,128)S(1)} %get-tuple-element.94) | copy-start | bytes 764932
  7.0 4.3 %copy-start.16 = (f32[250,256]{1,0:T(8,128)}, f32[250,256]{1,0:T(8,128)S(1)}, u32[]{:S(2)}) copy-start(f32[250,256]{1,0:T(8,128)S(1)} %get-tuple-element.96) | copy-start | bytes 768004
  7.2 8.0 %copy-start.22 = (f32[243,256]{1,0:T(8,128)}, f32[243,256]{1,0:T(8,128)S(1)}, u32[]{:S(2)}) copy-start(f32[243,256]{1,0:T(8,128)S(1)} %get-tuple-element.81) | copy-start | bytes 746500
  7.2 8.0 %copy-start.30 = (f32[243,256]{1,0:T(8,128)}, f32[243,256]{1,0:T(8,128)S(1)}, u32[]{:S(2)}) copy-start(f32[243,256]{1,0:T(8,128)S(1)} %get-tuple-element.82) | copy-start | bytes 746500
  7.3 7.9 %copy-start.23 = (f32[244,256]{1,0:T(8,128)}, f32[244,256]{1,0:T(8,128)S(1)}, u32[]{:S(2)}) copy-start(f32[244,256]{1,0:T(8,128)S(1)} %get-tuple-element.83) | copy-start | bytes 749572
  7.3 7.9 %copy-start.31 = (f32[244,256]{1,0:T(8,128)}, f32[244,256]{1,0:T(8,128)S(1)}, u32[]{:S(2)}) copy-start(f32[244,256]{1,0:T(8,128)S(1)} %get-tuple-element.84) | copy-start | bytes 749572
  7.3 7.9 %copy-start.24 = (f32[245,256]{1,0:T(8,128)}, f32[245,256]{1,0:T(8,128)S(1)}, u32[]{:S(2)}) copy-start(f32[245,256]{1,0:T(8,128)S(1)} %get-tuple-element.85) | copy-start | bytes 752644
  7.4 7.9 %copy-start.32 = (f32[245,256]{1,0:T(8,128)}, f32[245,256]{1,0:T(8,128)S(1)}, u32[]{:S(2)}) copy-start(f32[245,256]{1,0:T(8,128)S(1)} %get-tuple-element.86) | copy-start | bytes 752644
  7.4 7.9 %copy-start.25 = (f32[246,256]{1,0:T(8,128)}, f32[246,256]{1,0:T(8,128)S(1)}, u32[]{:S(2)}) copy-start(f32[246,256]{1,0:T(8,128)S(1)} %get-tuple-element.87) | copy-start | bytes 755716
  7.4 7.9 %copy-start.33 = (f32[246,256]{1,0:T(8,128)}, f32[246,256]{1,0:T(8,128)S(1)}, u32[]{:S(2)}) copy-start(f32[246,256]{1,0:T(8,128)S(1)} %get-tuple-element.88) | copy-start | bytes 755716
  7.5 7.8 %copy-start.26 = (f32[247,256]{1,0:T(8,128)}, f32[247,256]{1,0:T(8,128)S(1)}, u32[]{:S(2)}) copy-start(f32[247,256]{1,0:T(8,128)S(1)} %get-tuple-element.89) | copy-start | bytes 758788
  7.5 7.8 %copy-start.34 = (f32[247,256]{1,0:T(8,128)}, f32[247,256]{1,0:T(8,128)S(1)}, u32[]{:S(2)}) copy-start(f32[247,256]{1,0:T(8,128)S(1)} %get-tuple-element.90) | copy-start | bytes 758788
  8.0 7.3 %copy-start.27 = (f32[248,256]{1,0:T(8,128)}, f32[248,256]{1,0:T(8,128)S(1)}, u32[]{:S(2)}) copy-start(f32[248,256]{1,0:T(8,128)S(1)} %get-tuple-element.91) | copy-start | bytes 761860
  8.0 7.4 %copy-start.35 = (f32[248,256]{1,0:T(8,128)}, f32[248,256]{1,0:T(8,128)S(1)}, u32[]{:S(2)}) copy-start(f32[248,256]{1,0:T(8,128)S(1)} %get-tuple-element.92) | copy-start | bytes 761860
  10.4 4.9 %copy-start.55 = (f32[256]{0:T(256)}, f32[256]{0:T(256)S(1)}, u32[]{:S(2)}) copy-start(f32[256]{0:T(256)S(1)} %get-tuple-element.160) | copy-start | bytes 3076
  10.4 4.9 %copy-start.58 = (f32[256]{0:T(256)}, f32[256]{0:T(256)S(1)}, u32[]{:S(2)}) copy-start(f32[256]{0:T(256)S(1)} %get-tuple-element.161) | copy-start | bytes 3076
  10.4 4.9 %copy-start.61 = (f32[256]{0:T(256)}, f32[256]{0:T(256)S(1)}, u32[]{:S(2)}) copy-start(f32[256]{0:T(256)S(1)} %get-tuple-element.162) | copy-start | bytes 3076
  10.4 4.9 %copy-start.64 = (f32[256]{0:T(256)}, f32[256]{0:T(256)S(1)}, u32[]{:S(2)}) copy-start(f32[256]{0:T(256)S(1)} %get-tuple-element.163) | copy-start | bytes 3076
  10.5 4.9 %copy-start.66 = (f32[256]{0:T(256)}, f32[256]{0:T(256)S(1)}, u32[]{:S(2)}) copy-start(f32[256]{0:T(256)S(1)} %get-tuple-element.164) | copy-start | bytes 3076
  10.5 4.9 %copy-start.68 = (f32[256]{0:T(256)}, f32[256]{0:T(256)S(1)}, u32[]{:S(2)}) copy-start(f32[256]{0:T(256)S(1)} %get-tuple-element.165) | copy-start | bytes 3076
  11.1 4.3 %copy-start.49 = (f32[256]{0:T(256)}, f32[256]{0:T(256)S(1)}, u32[]{:S(2)}) copy-start(f32[256]{0:T(256)S(1)} %get-tuple-element.148) | copy-start | bytes 3076
  11.2 4.3 %copy-start.51 = (f32[256]{0:T(256)}, f32[256]{0:T(256)S(1)}, u32[]{:S(2)}) copy-start(f32[256]{0:T(256)S(1)} %get-tuple-element.149) | copy-start | bytes 3076
  15.4 66.6 %copy-start.40 = (f32[256,256]{1,0:T(8,128)}, f32[256,256]{1,0:T(8,128)S(1)}, u32[]{:S(2)}) copy-start(f32[256,256]{1,0:T(8,128)S(1)} %get-tuple-element.46) | copy-start | bytes 786436
  20.6 29.7 %all-to-all-start = ((f32[64,2,256]{2,1,0:T(2,128)}), f32[64,2,256]{2,1,0:T(2,128)}, u32[]{:S(2)}, u32[]{:S(2)}) async-start(f32[64,2,256]{2,1,0:T(2,128)} %broadcast_in_dim.4), calls=%async_computation | async-start | bytes 262144 | tf_op jit(solution)/shard_map/all_to_all | solution.py:31
  60.5 18.7 %all-to-all-start.1 = ((f32[64,2,256]{2,1,0:T(2,128)}), f32[64,2,256]{2,1,0:T(2,128)}, u32[]{:S(2)}, u32[]{:S(2)}) async-start(f32[64,2,256]{2,1,0:T(2,128)} %broadcast_in_dim.5), calls=%async_computation.1 | async-start | bytes 262144 | tf_op jit(solution)/shard_map/all_to_all | solution.py:31
  99.3 9.0 %collective-permute-start = (bf16[64,8,768]{2,1,0:T(8,128)(2,1)}, bf16[64,8,768]{2,1,0:T(8,128)(2,1)}, u32[]{:S(2)}, u32[]{:S(2)}) collective-permute-start(bf16[64,8,768]{2,1,0:T(8,128)(2,1)} %fusion.3), channel_id=1, source_target_pairs={{0,4},{4,0},{1,5},{5,1},{2,6},{6,2},{3,7},{7,3},{8,12},{12,8},{9,1... | collective-permute-start | bytes 2359304 | tf_op jit(solution)/shard_map/ppermute | solution.py:41
  103.5 12.8 %all-to-all-start.2 = ((bf16[4,256,256]{2,1,0:T(8,128)(2,1)}), bf16[4,256,256]{2,1,0:T(8,128)(2,1)S(1)}, u32[]{:S(2)}, u32[]{:S(2)}) async-start(bf16[4,256,256]{2,1,0:T(8,128)(2,1)} %bitcast.100), calls=%async_computation.2 | async-start | bytes 1048576 | tf_op jit(solution)/shard_map/all_to_all | solution.py:113
  108.2 16.1 %copy-start.2 = (f32[251,256]{1,0:T(8,128)S(1)}, f32[251,256]{1,0:T(8,128)}, u32[]{:S(2)}) copy-start(f32[251,256]{1,0:T(8,128)} %copy-done.1) | copy-start | bytes 771076
  108.2 16.1 %copy-start.63 = (f32[256]{0:T(256)S(1)}, f32[256]{0:T(256)}, u32[]{:S(2)}) copy-start(f32[256]{0:T(256)} %copy-done.61) | copy-start | bytes 3076
  111.0 15.9 %copy-start.5 = (f32[252,256]{1,0:T(8,128)S(1)}, f32[252,256]{1,0:T(8,128)}, u32[]{:S(2)}) copy-start(f32[252,256]{1,0:T(8,128)} %copy-done.4) | copy-start | bytes 774148
  111.0 15.9 %copy-start.7 = (f32[253,256]{1,0:T(8,128)S(1)}, f32[253,256]{1,0:T(8,128)}, u32[]{:S(2)}) copy-start(f32[253,256]{1,0:T(8,128)} %copy-done.6) | copy-start | bytes 777220
  111.0 15.9 %copy-start.57 = (f32[256]{0:T(256)S(1)}, f32[256]{0:T(256)}, u32[]{:S(2)}) copy-start(f32[256]{0:T(256)} %copy-done.55) | copy-start | bytes 3076
  111.0 15.9 %copy-start.60 = (f32[256]{0:T(256)S(1)}, f32[256]{0:T(256)}, u32[]{:S(2)}) copy-start(f32[256]{0:T(256)} %copy-done.58) | copy-start | bytes 3076
  117.1 78.0 %all-to-all-start.3 = ((bf16[64,8,768]{2,1,0:T(8,128)(2,1)}), bf16[64,8,768]{2,1,0:T(8,128)(2,1)S(1)}, u32[]{:S(2)}, u32[]{:S(2)}) async-start(bf16[64,8,768]{2,1,0:T(8,128)(2,1)} %fusion), calls=%async_computation.3 | async-start | bytes 1572864 | tf_op jit(solution)/shard_map/all_to_all | solution.py:43
  121.9 4.9 %copy-start.9 = (f32[254,256]{1,0:T(8,128)S(1)}, f32[254,256]{1,0:T(8,128)}, u32[]{:S(2)}) copy-start(f32[254,256]{1,0:T(8,128)} %copy-done.8) | copy-start | bytes 780292
  121.9 4.9 %copy-start.11 = (f32[254,256]{1,0:T(8,128)S(1)}, f32[254,256]{1,0:T(8,128)}, u32[]{:S(2)}) copy-start(f32[254,256]{1,0:T(8,128)} %copy-done.10) | copy-start | bytes 780292
  122.0 4.9 %copy-start.13 = (f32[255,256]{1,0:T(8,128)S(1)}, f32[255,256]{1,0:T(8,128)}, u32[]{:S(2)}) copy-start(f32[255,256]{1,0:T(8,128)} %copy-done.12) | copy-start | bytes 783364
  122.0 4.9 %copy-start.15 = (f32[255,256]{1,0:T(8,128)S(1)}, f32[255,256]{1,0:T(8,128)}, u32[]{:S(2)}) copy-start(f32[255,256]{1,0:T(8,128)} %copy-done.14) | copy-start | bytes 783364
  122.0 4.9 %copy-start.17 = (f32[250,256]{1,0:T(8,128)S(1)}, f32[250,256]{1,0:T(8,128)}, u32[]{:S(2)}) copy-start(f32[250,256]{1,0:T(8,128)} %copy-done.16) | copy-start | bytes 768004
  122.0 4.9 %copy-start.19 = (f32[251,256]{1,0:T(8,128)S(1)}, f32[251,256]{1,0:T(8,128)}, u32[]{:S(2)}) copy-start(f32[251,256]{1,0:T(8,128)} %copy-done.18) | copy-start | bytes 771076
  126.9 67.5 %copy-start.37 = (bf16[4,256,256]{2,1,0:T(8,128)(2,1)S(1)}, bf16[4,256,256]{2,1,0:T(8,128)(2,1)}, u32[]{:S(2)}) copy-start(bf16[4,256,256]{2,1,0:T(8,128)(2,1)} %copy-done.36) | copy-start | bytes 1572868
  (30 other events, 60.9 us)

commit v2 on v1

v2 whole, which is shorter than its diff:
```python
import functools

import jax
import jax.numpy as jnp
from jax import lax
from jax.experimental import pallas as pl
from jax.experimental.pallas import tpu as pltpu
from jax.sharding import Mesh, PartitionSpec as P

BLOCK = 128
DP = ("y", "z", "core")
YZ = ("y", "z")
LANES = 128
PAD = 16
F32 = jnp.float32
BF16 = jnp.bfloat16
VM = pl.BlockSpec(memory_space=pltpu.VMEM)
SM = pl.BlockSpec(memory_space=pltpu.SMEM)
NT = (((1,), (1,)), ((), ()))


def call(body, outs, ins, scratch=(), name=None):
    return pl.pallas_call(
        body,
        out_shape=outs,
        in_specs=ins,
        out_specs=jax.tree.map(lambda _: VM, outs),
        scratch_shapes=list(scratch),
        name=name,
    )


def shape(dims, dtype=F32):
    return jax.ShapeDtypeStruct(dims, dtype)


def lanes(h):
    return slice(h * LANES, (h + 1) * LANES)


def row_masks(len_ref, rows):
    row = lax.broadcasted_iota(jnp.int32, (rows, LANES), 0)
    split = len_ref[0, 0]
    end = split + len_ref[0, 1]
    return row < split, row < end


def embed(buf, h, x, first):
    rows = x.shape[0]
    zero = jnp.zeros((PAD, LANES), F32)
    head = jnp.where(first, x, 0.0)
    tail = jnp.where(first, 0.0, x)
    buf[h, 0:PAD] = zero
    buf[h, PAD : 2 * PAD] = head[:PAD]
    buf[h, 2 * PAD : PAD + rows] = head[PAD:] + tail[: rows - PAD]
    buf[h, PAD + rows : 2 * PAD + rows] = tail[rows - PAD :]
    buf[h, 2 * PAD + rows : 3 * PAD + rows] = zero


def conv(buf, h, taps, rows, first, sign):
    count = taps.shape[0]
    radius = count // 2
    span = rows + PAD
    total = jnp.zeros((span, LANES), F32)
    for k in range(count):
        total = total + taps[k : k + 1, lanes(h)] * buf[h, pl.ds(PAD + sign * (k - radius), span), :]
    return jnp.where(first, total[:rows], total[PAD:])


def tap_sums(out, values, buf, h, count, rows):
    radius = count // 2
    span = rows + PAD
    for k in range(count):
        prod = values * buf[h, pl.ds(PAD + k - radius, span), :]
        out[k : k + 1, lanes(h)] = jnp.sum(prod, axis=0, keepdims=True)


def forward_kernel(len_ref, frames, proj, taps, value, sig, buf, conv_out, pay):
    rows, channels = value.shape
    first, live = row_masks(len_ref, rows)
    pre = jnp.dot(frames[...], proj[...], preferred_element_type=F32)
    value[...] = pre[:, :channels]
    sig[...] = jax.nn.sigmoid(pre[:, channels:])
    sums = []
    for h in range(channels // LANES):
        glu = jnp.where(live, value[:, lanes(h)] * sig[:, lanes(h)], 0.0)
        embed(buf, h, glu.astype(BF16).astype(F32), first)
        out = jnp.where(live, conv(buf, h, taps, rows, first, 1), 0.0)
        conv_out[:, lanes(h)] = out
        sums.append(
            jnp.concatenate(
                [jnp.sum(out, axis=0, keepdims=True), jnp.sum(out * out, axis=0, keepdims=True)], axis=0
            )
        )
    both = jnp.concatenate(sums, axis=1)
    pay[...] = jnp.broadcast_to(both[None], pay.shape)


def side_kernel(len_ref, grad_out, proj_out, conv_out, buf, grad_hidden, ones_sum, conv_sum, work):
    rows, channels = grad_hidden.shape
    count = 31
    first, live = row_masks(len_ref, rows)
    hid = jnp.dot(grad_out[...], proj_out[...], preferred_element_type=F32)
    for h in range(channels // LANES):
        grad_hidden[:, lanes(h)] = jnp.where(live, hid[:, lanes(h)], 0.0)
        embed(work, h, jnp.where(live, 1.0, 0.0), first)
        tap_sums(ones_sum, work[h, pl.ds(PAD, rows + PAD), :], buf, h, count, rows)
        embed(work, h, conv_out[:, lanes(h)], first)
        tap_sums(conv_sum, work[h, pl.ds(PAD, rows + PAD), :], buf, h, count, rows)
        ones_sum[count : count + 1, lanes(h)] = jnp.zeros((1, LANES), F32)
        conv_sum[count : count + 1, lanes(h)] = jnp.zeros((1, LANES), F32)


def norm_kernel(
    len_ref, counts, got, gain, shift, conv_out, grad_hidden, buf, ones_sum, conv_sum,
    hidden, normed, grad_scaled, stats, pay, work, own_sum,
):
    rows, channels = conv_out.shape
    count = 31
    first, live = row_masks(len_ref, rows)
    total = jnp.sum(counts[...].astype(F32), axis=1, keepdims=True) * BLOCK
    sums = jnp.sum(got[...], axis=0)
    mean = sums[0:1] / total
    inv_std = lax.rsqrt(sums[1:2] / total - mean * mean + 1e-05)
    stats[0:1] = mean
    stats[1:2] = inv_std
    heads = []
    for h in range(channels // LANES):
        cols = lanes(h)
        norm = (conv_out[:, cols] - mean[:, cols]) * inv_std[:, cols]
        scaled = norm * gain[:, cols] + shift[:, cols]
        s = jax.nn.sigmoid(scaled)
        hidden[:, cols] = jnp.where(live, scaled * s, 0.0).astype(BF16)
        grad = grad_hidden[:, cols] * s * (1.0 + scaled * (1.0 - s))
        normed[:, cols] = norm
        grad_scaled[:, cols] = grad
        heads.append((jnp.sum(grad, axis=0, keepdims=True), jnp.sum(grad * norm, axis=0, keepdims=True)))
        embed(work, h, grad, first)
        tap_sums(own_sum, work[h, pl.ds(PAD, rows + PAD), :], buf, h, count, rows)
        own_sum[count : count + 1, cols] = jnp.zeros((1, LANES), F32)
    (s0, q0), (s1, q1) = heads
    tile = jnp.concatenate([s0, s1, q0, q1, jnp.zeros((4, LANES), F32)], axis=0)
    pay[...] = jnp.broadcast_to(tile[None], pay.shape)
    for j in range(pay.shape[0] // 2):
        k, cols = j // 2, lanes(j % 2)
        for i, ref in enumerate((own_sum, ones_sum, conv_sum)):
            part = ref[k : k + 1, cols]
            pay[2 * j, 4 + i : 5 + i, :] = part
            pay[2 * j + 1, 4 + i : 5 + i, :] = part


def back_kernel(
    len_ref, half_ref, counts, got, gain, stats, normed, grad_scaled, value, sig, taps,
    grad_pre, shift_grad, gain_grad, slice_out, work,
):
    rows, channels = normed.shape
    first, live = row_masks(len_ref, rows)
    total = jnp.sum(counts[...].astype(F32), axis=1, keepdims=True) * BLOCK
    sums = jnp.sum(got[...], axis=0)
    mean, inv_std = stats[0:1], stats[1:2]
    slices = []
    for h in range(channels // LANES):
        cols = lanes(h)
        s, q = sums[h : h + 1], sums[2 + h : 3 + h]
        shift_grad[:, cols] = s
        gain_grad[:, cols] = q
        scale = gain[:, cols] * inv_std[:, cols]
        grad = scale * (grad_scaled[:, cols] - s / total - normed[:, cols] * (q / total))
        embed(work, h, jnp.where(live, grad, 0.0), first)
        glu = jnp.where(live, conv(work, h, taps, rows, first, -1), 0.0)
        v, g = value[:, cols], sig[:, cols]
        grad_pre[:, cols] = (glu * g).astype(BF16)
        grad_pre[:, channels + h * LANES : channels + (h + 1) * LANES] = (glu * v * g * (1.0 - g)).astype(BF16)
        own, ones, cv = sums[4:5], sums[5:6], sums[6:7]
        slices.append(
            scale * (own - s / total * ones - q / total * inv_std[:, cols] * (cv - mean[:, cols] * ones))
        )
    which = jnp.full((1, LANES), half_ref[0], jnp.int32)
    depth = jnp.where(which == 0, slices[0], slices[1])
    slice_out[...] = jnp.broadcast_to(depth, slice_out.shape)


def frame_kernel(mp_ref, grad_pre, proj, own, one, two, three):
    width = own.shape[1]
    groups = proj.shape[0] // width
    for d, out in enumerate((own, one, two, three)):
        at = pl.multiple_of(lax.rem(mp_ref[0] + d, groups) * width, width)
        term = lax.dot_general(grad_pre[...], proj[pl.ds(at, width), :], NT, preferred_element_type=F32)
        out[...] = term.astype(BF16)


def rows_kernel(left, own, other, out):
    tokens = own.shape[0]
    total = jnp.dot(left[:, :tokens], own[...], preferred_element_type=F32)
    total = total + jnp.dot(left[:, tokens:], other[...], preferred_element_type=F32)
    out[...] = total.astype(BF16)


def bulk_kernel(left, own, other, out_rows, depth, pay):
    tokens, width = own.shape
    peers, rows, _ = pay.shape
    total = jnp.dot(left[:, :tokens], own[...], preferred_element_type=F32)
    total = total + jnp.dot(left[:, tokens:], other[...], preferred_element_type=F32)
    pay[:, :, :width] = total.reshape(peers, rows, width).astype(BF16)
    pay[:, :, width : width + out_rows.shape[2]] = out_rows[...]
    pay[:, :, width + out_rows.shape[2] :] = jnp.broadcast_to(
        depth[...].astype(BF16)[None], (peers, rows, LANES)
    )


def last_kernel(got, in_rows, out_rows, depth):
    width, more = in_rows.shape[1], out_rows.shape[1]
    in_rows[...] = jnp.sum(got[:, :, :width].astype(F32), axis=0)
    out_rows[...] = jnp.sum(got[:, :, width : width + more].astype(F32), axis=0)
    for j in range(2 * depth.shape[0]):
        depth[j // 2 : j // 2 + 1, lanes(j % 2)] = got[j, 0:1, width + more :].astype(F32)


def core_halves(x, core):
    frames, width = x.shape
    parts = x.T.reshape(width // 16, 2, 8, frames)
    keep = lax.dynamic_index_in_dim(parts, core, 1, keepdims=False).reshape(width // 2, frames)
    send = lax.dynamic_index_in_dim(parts, 1 - core, 1, keepdims=False).reshape(width // 2, frames)
    return keep, send


def swap_cores(x):
    return lax.ppermute(x, "core", [(0, 1), (1, 0)])


def after(x, y):
    return lax.optimization_barrier((x, y))[0]


def shards(frames, proj_in, taps, bn_gain, bn_shift, proj_out, grad_out, counts, lengths):
    rows, width = frames.shape
    channels = proj_in.shape[2]
    count = taps.shape[0]
    halves = channels // LANES
    buf_rows = rows + 3 * PAD
    peers = lax.axis_size(DP)
    chips = lax.axis_size(YZ)
    groups = lax.axis_size("mp")
    rows_dev = width // peers
    core = lax.axis_index("core")
    chip = lax.axis_index(YZ)
    mp = lax.axis_index("mp")
    full = shape((rows, channels))
    proj = proj_in.reshape(width, 2 * channels)
    counts_row = counts.reshape(1, -1)
    gain_row = bn_gain.reshape(1, channels)
    shift_row = bn_shift.reshape(1, channels)

    value, sig, buf, conv_out, pay = call(
        forward_kernel,
        (full, full, shape((halves, buf_rows, LANES)), full, shape((peers, 2, channels))),
        [SM, VM, VM, VM],
        name="forward",
    )(lengths, frames, proj, taps)
    got = lax.all_to_all(pay, DP, 0, 0)

    grad_hidden, ones_sum, conv_sum = call(
        side_kernel,
        (full, shape((count + 1, channels)), shape((count + 1, channels))),
        [SM, VM, VM, VM, VM],
        [pltpu.VMEM((halves, buf_rows, LANES), F32)],
        name="side",
    )(lengths, grad_out, proj_out, conv_out, buf)
    left_in = core_halves(frames, core)
    left_out = core_halves(grad_out, core)
    left_in = jnp.concatenate([left_in[0], swap_cores(after(left_in[1], pay))], axis=1)
    left_out = jnp.concatenate([left_out[0], swap_cores(after(left_out[1], pay))], axis=1)

    hidden, normed, grad_scaled, stats, pay = call(
        norm_kernel,
        (
            shape((rows, channels), BF16),
            full,
            full,
            shape((2, channels)),
            shape((peers, 8, LANES)),
        ),
        [SM] + [VM] * 9,
        [pltpu.VMEM((halves, buf_rows, LANES), F32), pltpu.VMEM((count + 1, channels), F32)],
        name="norm",
    )(lengths, counts_row, got, gain_row, shift_row, conv_out, grad_hidden, buf, ones_sum, conv_sum)
    got = lax.all_to_all(pay, DP, 0, 0)

    other = swap_cores(after(hidden, pay))
    out_rows = call(rows_kernel, shape((width // 2, channels), BF16), [VM] * 3, name="out_rows")(
        left_out, hidden, other
    ).reshape(chips, rows_dev, channels)

    half = (chip % 2).astype(jnp.int32).reshape(1)
    grad_pre, shift_grad, gain_grad, depth = call(
        back_kernel,
        (
            shape((rows, 2 * channels), BF16),
            shape((1, channels)),
            shape((1, channels)),
            shape((rows_dev, LANES)),
        ),
        [SM, SM] + [VM] * 9,
        [pltpu.VMEM((halves, buf_rows, LANES), F32)],
        name="back",
    )(lengths, half, counts_row, got, gain_row, stats, normed, grad_scaled, value, sig, taps)

    other = swap_cores(grad_pre)
    term = shape((rows, width // groups), BF16)
    own, one, two, three = call(frame_kernel, (term,) * 4, [SM, VM, VM], name="frame")(
        mp.astype(jnp.int32).reshape(1), grad_pre, proj
    )
    pay = call(
        bulk_kernel,
        shape((chips, rows_dev, 3 * channels + LANES), BF16),
        [VM] * 5,
        name="bulk",
    )(left_in, grad_pre, other, out_rows, depth)
    got = lax.all_to_all(pay, YZ, 0, 0)

    frame_sum = own.astype(F32)
    for d, part in ((1, one), (2, two), (3, three)):
        part = lax.ppermute(after(part, pay), "mp", [(i, (i + d) % groups) for i in range(groups)])
        frame_sum = frame_sum + part.astype(F32)
    frame_grad = frame_sum.astype(BF16)

    in_rows, out_grad, depth_grad = call(
        last_kernel,
        (shape((rows_dev, 2 * channels)), shape((rows_dev, channels)), shape((count, channels))),
        [VM],
        name="last",
    )(got)
    in_grad = in_rows.reshape(rows_dev, 2, channels)
    return (frame_grad, in_grad, out_grad, depth_grad, gain_grad.reshape(channels), shift_grad.reshape(channels))


def solution(mesh):
    grid = Mesh(mesh.devices.reshape(8, 8, 2, 4), ("y", "z", "core", "mp"))
    placed = (
        P(DP, None),
        P(None, None, "mp"),
        P(None, "mp"),
        P("mp"),
        P("mp"),
        P(None, "mp"),
        P(DP, None),
        P(),
        P(DP, None),
    )
    return jax.shard_map(
        shards,
        mesh=grid,
        in_specs=placed,
        out_specs=(
            P(DP, "mp"),
            P(DP, None, "mp"),
            P(DP, "mp"),
            P(None, "mp"),
            P("mp"),
            P("mp"),
        ),
        check_vma=False,
    )
```

time: 198 us -> 124 us (0.63)
  blocking collectives: 69.7 us -> 0 us
  other arithmetic: 32.5 us -> 3.32 us
  Pallas kernels: 0 us -> 22.7 us
  local copies, waits for them, and re-layouts: 23.4 us -> 8.91 us
  starting transfers between devices: 33.8 us -> 47.1 us
  waiting for transfers between devices: 26.9 us -> 39.3 us
  matrix products: 7.04 us -> 0 us
  between operations: 3.18 us -> 0.81 us
    psum x5 -> x0, blocking collectives: 69.7 us -> none  [the longest x1 30.2 us: shards(): lax.psum(lax.psum(lax.psum(jnp.stack(depth_rows), 'core'), 'y'), 'z')]
    pallas_call x0 -> x8, Pallas kernels: none -> 22.7 us  [the longest x1 3.48 us: shards(): call(forward_kernel, (full, full, shape((halves, buf_rows, LANES)), full,...]
    reduce_sum x11 -> x0, other arithmetic: 18.2 us -> none  [the longest x4 8.92 us: shards(): jnp.sum(grad_conv * tap_term(glu_float, owner_id, live_col, tap_index - r...]
    ppermute x1 -> x7, starting transfers between devices: 1.91 us -> 18.4 us  [the longest x3 9.75 us: shards(): lax.ppermute(after(part, pay), 'mp', [(i, (i + d) % groups) for i in rang...]
    all_to_all x4 -> x3, waiting for transfers between devices: 26.9 us -> 35 us  [the longest x2 26.4 us: shards(): got = lax.all_to_all(pay, DP, 0, 0)]
    another operation x6 -> x0, other arithmetic: 7.45 us -> none
    dot_general x5 -> x0, matrix products: 7.04 us -> none  [the longest x1 2.48 us: shards(): lax.dot_general(grad_out, hidden, (((0,), (0,)), ((), ())), preferred_ele...]
    slice x49 -> x0, local copies, waits for them, and re-layouts: 4.53 us -> none  [the longest x29 1.56 us: time_shift(): return jnp.concatenate([pad_part, values[:offset]], axis=0)]
  transfers between devices with their start and end apart: 5 -> 10, of which waited for: 3 -> 5; matrix products, arithmetic and copies ran while one was open for 9% -> 3% of each run, Pallas kernels for 0% -> 9%
where the time goes in v2:
time: 124 us; the launch traced here: 122 us
  starting transfers between devices  47.1 us (38%)
  waiting for transfers between devices  39.3 us (32%)
  Pallas kernels  22.7 us (18%)
  local copies, waits for them, and re-layouts  8.91 us (7%)
  other arithmetic  3.32 us (3%)
    all_to_all x2, waiting for transfers between devices, shards(): got = lax.all_to_all(pay, DP, 0, 0)  26.4 us
    all_to_all x2, starting transfers between devices, shards(): got = lax.all_to_all(pay, DP, 0, 0)  24.1 us
    ppermute x3, starting transfers between devices, shards(): lax.ppermute(after(part, pay), 'mp', [(i, (i + d) % groups) for i in rang...  9.75 us
    unnamed x20, local copies, waits for them, and re-layouts  8.84 us
    ppermute x4, starting transfers between devices, swap_cores(): return lax.ppermute(x, 'core', [(0, 1), (1, 0)])  8.64 us
    all_to_all x1, waiting for transfers between devices, shards(): got = lax.all_to_all(pay, YZ, 0, 0)  8.64 us
    all_to_all x1, starting transfers between devices, shards(): got = lax.all_to_all(pay, YZ, 0, 0)  4.65 us
    ppermute x3, waiting for transfers between devices, shards(): lax.ppermute(after(part, pay), 'mp', [(i, (i + d) % groups) for i in rang...  4.24 us
  transfers between devices with their start and end apart: 10, of which 5 were waited for; matrix products, arithmetic and copies ran while one was open for 3% of the time, Pallas kernels for 9%

profile of v2, /device:TPU:6, one launch (start us, length us, event | category | flops | bytes accessed | tf_op | source)
XLA Modules:
  0.0 122.2 jit_solution(16691803923717541959)
XLA Ops:
  0.6 2.5 %copy.23 = bf16[128,8,2,256]{3,1,2,0:T(8,128)(2,1)} copy(bf16[128,8,2,256]{3,2,1,0:T(2,128)(2,1)} %bitcast.29) | data formatting | bytes 2097152
  3.1 3.5 %forward.1 = (f32[256,256]{1,0:T(8,128)}, f32[256,256]{1,0:T(8,128)}, f32[2,304,128]{2,1,0:T(8,128)}, f32[256,256]{1,0:T(8,128)}, f32[128,2,256]{2,1,0:T(2,128)}) custom-call(s32[1,2]{1,0:T(1,128)} %len_ref.7, bf16[256,1024]{1,0:T(8,128)(2,1)} %frames.1, bf16[1024,512]{1,0:T(8,128)(2,1)} %bitcast.25, f32[31,256]{1,0:T(8,128)} %taps.3), custom_call_target="tpu_custom_call" | custom-call | tf_op jit(solution)/shard_map/forward/pallas_call | solution.py:254
  6.6 17.8 %all-to-all-start = ((f32[128,2,256]{2,1,0:T(2,128)}), f32[128,2,256]{2,1,0:T(2,128)S(1)}, u32[]{:S(2)}, u32[]{:S(2)}) async-start(f32[128,2,256]{2,1,0:T(2,128)} %get-tuple-element.36), calls=%async_computation | async-start | bytes 524288 | tf_op jit(solution)/shard_map/all_to_all | solution.py:260
  24.4 3.5 %side.1 = (f32[256,256]{1,0:T(8,128)}, f32[32,256]{1,0:T(8,128)}, f32[32,256]{1,0:T(8,128)}) custom-call(s32[1,2]{1,0:T(1,128)} %len_ref.7, bf16[256,1024]{1,0:T(8,128)(2,1)} %grad_out.1, bf16[1024,256]{1,0:T(8,128)(2,1)} %proj_out.1, f32[256,256]{1,0:T(8,128)} %get-tuple-element.37.conv_out, f32[2,304,128]{2,1,0:T(8,128)} %get-tuple-element.38.buf), custom_call_target="tpu_custom_call" | custom-call | tf_op jit(solution)/shard_map/side/pallas_call | solution.py:262
  27.9 11.6 %all-to-all-done.got = f32[128,2,256]{2,1,0:T(2,128)S(1)} async-done(((f32[128,2,256]{2,1,0:T(2,128)}), f32[128,2,256]{2,1,0:T(2,128)S(1)}, u32[]{:S(2)}, u32[]{:S(2)}) %all-to-all-start) | async-done | bytes 262176 | tf_op jit(solution)/shard_map/all_to_all | solution.py:260
  39.5 0.0 copy-start.4
  39.5 0.7 copy-done.4
  40.2 3.4 %norm.1 = (bf16[256,256]{1,0:T(8,128)(2,1)}, f32[256,256]{1,0:T(8,128)}, f32[256,256]{1,0:T(8,128)}, f32[2,256]{1,0:T(2,128)}, f32[128,8,128]{2,1,0:T(8,128)}) custom-call(s32[1,2]{1,0:T(1,128)} %len_ref.7, s32[1,128]{1,0:T(1,128)} %bitcast.34, f32[128,2,256]{2,1,0:T(2,128)} %copy-done.4, f32[1,256]{1,0:T(1,128)} %bitcast.32, f32[1,256]{1,0:T(1,128)} %bitcast.36, ...), custom_call_target="tpu_custom_call" | custom-call | tf_op jit(solution)/shard_map/norm/pallas_call | solution.py:274
  43.6 0.0 copy-start.1
  43.6 6.3 %all-to-all-start.1 = ((f32[128,8,128]{2,1,0:T(8,128)}), f32[128,8,128]{2,1,0:T(8,128)S(1)}, u32[]{:S(2)}, u32[]{:S(2)}) async-start(f32[128,8,128]{2,1,0:T(8,128)} %get-tuple-element.42), calls=%async_computation.1 | async-start | bytes 1048576 | tf_op jit(solution)/shard_map/all_to_all | solution.py:287
  49.9 0.0 copy-done.1
  49.9 0.0 copy-start.2
  49.9 0.2 copy.21
  50.1 0.8 copy-done.2
  50.9 0.2 copy.20
  51.1 0.1 dynamic-slice_bitcast_fusion.1
  51.2 1.9 %collective-permute-start = (bf16[512,256]{1,0:T(8,128)(2,1)S(1)}, bf16[512,256]{1,0:T(8,128)(2,1)S(1)}, u32[]{:S(2)}, u32[]{:S(2)}) collective-permute-start(bf16[512,256]{1,0:T(8,128)(2,1)S(1)} %get-tuple-element.51), channel_id=1, source_target_pairs={{0,4},{4,0},{1,5},{5,1},{2,6},{6,2},{3,7},{7,3},{8,12},{12,8},{9,1... | collective-permute-start | bytes 786440 | tf_op jit(solution)/shard_map/ppermute | solution.py:228
  53.1 2.4 %collective-permute-start.2 = (bf16[512,256]{1,0:T(8,128)(2,1)S(1)}, bf16[512,256]{1,0:T(8,128)(2,1)S(1)}, u32[]{:S(2)}, u32[]{:S(2)}) collective-permute-start(bf16[512,256]{1,0:T(8,128)(2,1)S(1)} %get-tuple-element.52), channel_id=1, source_target_pairs={{0,4},{4,0},{1,5},{5,1},{2,6},{6,2},{3,7},{7,3},{8,12},{12,8},{9,1... | collective-permute-start | bytes 786440 | tf_op jit(solution)/shard_map/ppermute | solution.py:228
  55.6 14.8 %all-to-all-done.1.got = f32[128,8,128]{2,1,0:T(8,128)S(1)} async-done(((f32[128,8,128]{2,1,0:T(8,128)}), f32[128,8,128]{2,1,0:T(8,128)S(1)}, u32[]{:S(2)}, u32[]{:S(2)}) %all-to-all-start.1) | async-done | bytes 524320 | tf_op jit(solution)/shard_map/all_to_all | solution.py:287
  70.4 0.0 copy-start.3
  70.4 0.8 copy-done.3
  71.2 3.2 %back.1 = (bf16[256,512]{1,0:T(8,128)(2,1)}, f32[1,256]{1,0:T(1,128)}, f32[1,256]{1,0:T(1,128)}, f32[8,128]{1,0:T(8,128)}) custom-call(s32[1,2]{1,0:T(1,128)} %len_ref.7, s32[1]{0:T(128)} %bitcast.1.half_ref, s32[1,128]{1,0:T(1,128)} %bitcast.35, f32[128,8,128]{2,1,0:T(8,128)} %copy-done.3, f32[1,256]{1,0:T(1,128)} %bitcast.33, ...), custom_call_target="tpu_custom_call" | custom-call | tf_op jit(solution)/shard_map/back/pallas_call | solution.py:295
  74.4 1.9 %collective-permute-start.1 = (bf16[256,512]{1,0:T(8,128)(2,1)}, bf16[256,512]{1,0:T(8,128)(2,1)S(1)}, u32[]{:S(2)}, u32[]{:S(2)}) collective-permute-start(bf16[256,512]{1,0:T(8,128)(2,1)} %get-tuple-element.48.grad_pre.own), channel_id=1, source_target_pairs={{0,4},{4,0},{1,5},{5,1},{2,6},{6,2},{3,7},{7,3},{8,12},{12,8},{9,1... | collective-permute-start | bytes 786440 | tf_op jit(solution)/shard_map/ppermute | solution.py:228
  76.3 0.0 copy-done.6
  76.3 2.4 %collective-permute-start.3 = (bf16[256,256]{1,0:T(8,128)(2,1)S(1)}, bf16[256,256]{1,0:T(8,128)(2,1)S(1)}, u32[]{:S(2)}, u32[]{:S(2)}) collective-permute-start(bf16[256,256]{1,0:T(8,128)(2,1)S(1)} %copy-done.6), channel_id=1, source_target_pairs={{0,4},{4,0},{1,5},{5,1},{2,6},{6,2},{3,7},{7,3},{8,12},{12,8},{9,1... | collective-permute-start | bytes 393224 | tf_op jit(solution)/shard_map/ppermute | solution.py:228
  78.7 0.0 collective-permute-done
  78.7 0.9 pad_maximum_fusion.left
  79.6 0.0 collective-permute-done.2
  79.6 0.8 pad_maximum_fusion.1.left
  80.4 0.0 collective-permute-done.3.other
  80.4 0.7 copy-done.7
  81.1 2.1 %out_rows.1 = bf16[512,256]{1,0:T(8,128)(2,1)} custom-call(bf16[512,512]{1,0:T(8,128)(2,1)} %pad_maximum_fusion.1.left, bf16[256,256]{1,0:T(8,128)(2,1)} %get-tuple-element.54.own, bf16[256,256]{1,0:T(8,128)(2,1)} %copy-done.7), custom_call_target="tpu_custom_call" | custom-call | tf_op jit(solution)/shard_map/out_rows/pallas_call | solution.py:290
  83.2 0.0 collective-permute-done.1.other
  83.2 0.7 copy-done.5
  83.9 2.6 %bulk.1 = bf16[64,8,896]{2,1,0:T(8,128)(2,1)} custom-call(bf16[512,512]{1,0:T(8,128)(2,1)} %pad_maximum_fusion.left, bf16[256,512]{1,0:T(8,128)(2,1)} %get-tuple-element.48.grad_pre.own, bf16[256,512]{1,0:T(8,128)(2,1)} %copy-done.5, bf16[64,8,256]{2,1,0:T(8,128)(2,1)} %bitcast.30, f32[8,128]{1,0:T(8,128)} %get-tuple-element.55.depth), custom_call_target="tpu_custom_call" | custom-call | tf_op jit(solution)/shard_map/bulk/pallas_call | solution.py:313
  86.5 4.6 %all-to-all-start.2 = ((bf16[64,8,896]{2,1,0:T(8,128)(2,1)}), bf16[64,8,896]{2,1,0:T(8,128)(2,1)S(1)}, u32[]{:S(2)}, u32[]{:S(2)}) async-start(bf16[64,8,896]{2,1,0:T(8,128)(2,1)} %bulk.1), calls=%async_computation.2 | async-start | bytes 1835008 | tf_op jit(solution)/shard_map/all_to_all | solution.py:319
  91.2 2.5 %frame.1 = (bf16[256,256]{1,0:T(8,128)(2,1)}, bf16[256,256]{1,0:T(8,128)(2,1)}, bf16[256,256]{1,0:T(8,128)(2,1)}, bf16[256,256]{1,0:T(8,128)(2,1)}) custom-call(s32[1]{0:T(128)} %bitcast.mp_ref, bf16[256,512]{1,0:T(8,128)(2,1)} %get-tuple-element.48.grad_pre.own, bf16[1024,512]{1,0:T(8,128)(2,1)} %bitcast.26), custom_call_target="tpu_custom_call" | custom-call | tf_op jit(solution)/shard_map/frame/pallas_call | solution.py:310
  93.6 2.7 %collective-permute-start.6 = (bf16[256,256]{1,0:T(8,128)(2,1)}, bf16[256,256]{1,0:T(8,128)(2,1)S(1)}, u32[]{:S(2)}, u32[]{:S(2)}) collective-permute-start(bf16[256,256]{1,0:T(8,128)(2,1)} %get-tuple-element.60), channel_id=1, source_target_pairs={{0,3},{1,0},{2,1},{3,2},{4,7},{5,4},{6,5},{7,6},{8,11},{9,8},{10,9... | collective-permute-start | bytes 393224 | tf_op jit(solution)/shard_map/ppermute | solution.py:323
  96.4 3.0 %collective-permute-start.5 = (bf16[256,256]{1,0:T(8,128)(2,1)}, bf16[256,256]{1,0:T(8,128)(2,1)S(1)}, u32[]{:S(2)}, u32[]{:S(2)}) collective-permute-start(bf16[256,256]{1,0:T(8,128)(2,1)} %get-tuple-element.58), channel_id=1, source_target_pairs={{0,2},{1,3},{2,0},{3,1},{4,6},{5,7},{6,4},{7,5},{8,10},{9,11},{10,... | collective-permute-start | bytes 393224 | tf_op jit(solution)/shard_map/ppermute | solution.py:323
  99.4 4.0 %collective-permute-start.4 = (bf16[256,256]{1,0:T(8,128)(2,1)}, bf16[256,256]{1,0:T(8,128)(2,1)S(1)}, u32[]{:S(2)}, u32[]{:S(2)}) collective-permute-start(bf16[256,256]{1,0:T(8,128)(2,1)} %get-tuple-element.56), channel_id=1, source_target_pairs={{0,1},{1,2},{2,3},{3,0},{4,5},{5,6},{6,7},{7,4},{8,9},{9,10},{10,1... | collective-permute-start | bytes 393224 | tf_op jit(solution)/shard_map/ppermute | solution.py:323
  103.4 0.0 collective-permute-done.6
  103.4 1.7 %collective-permute-done.5 = bf16[256,256]{1,0:T(8,128)(2,1)S(1)} collective-permute-done((bf16[256,256]{1,0:T(8,128)(2,1)}, bf16[256,256]{1,0:T(8,128)(2,1)S(1)}, u32[]{:S(2)}, u32[]{:S(2)}) %collective-permute-start.5) | collective-permute-done | bytes 131104 | tf_op jit(solution)/shard_map/ppermute | solution.py:323
  105.2 2.5 %collective-permute-done.4 = bf16[256,256]{1,0:T(8,128)(2,1)S(1)} collective-permute-done((bf16[256,256]{1,0:T(8,128)(2,1)}, bf16[256,256]{1,0:T(8,128)(2,1)S(1)}, u32[]{:S(2)}, u32[]{:S(2)}) %collective-permute-start.4) | collective-permute-done | bytes 131104 | tf_op jit(solution)/shard_map/ppermute | solution.py:323
  107.7 1.6 %add_convert_fusion = bf16[256,256]{1,0:T(8,128)(2,1)} fusion(bf16[256,256]{1,0:T(8,128)(2,1)S(1)} %collective-permute-done.6, bf16[256,256]{1,0:T(8,128)(2,1)S(1)} %collective-permute-done.5, bf16[256,256]{1,0:T(8,128)(2,1)S(1)} %collective-permute-done.4, bf16[256,256]{1,0:T(8,128)(2,1)} %get-tuple-element.49), kind=kLoop, calls=%fused_computation.2 | loop fusion | flops 524288 | bytes 655360 | tf_op jit(solution)/shard_map/convert_element_type | solution.py:325
  109.3 8.6 %all-to-all-done.2.got = bf16[64,8,896]{2,1,0:T(8,128)(2,1)S(1)} async-done(((bf16[64,8,896]{2,1,0:T(8,128)(2,1)}), bf16[64,8,896]{2,1,0:T(8,128)(2,1)S(1)}, u32[]{:S(2)}, u32[]{:S(2)}) %all-to-all-start.2) | async-done | bytes 917536 | tf_op jit(solution)/shard_map/all_to_all | solution.py:319
  117.9 0.9 copy-done
  118.9 1.9 %last.1 = (f32[8,512]{1,0:T(8,128)}, f32[8,256]{1,0:T(8,128)}, f32[31,256]{1,0:T(8,128)}) custom-call(bf16[64,8,896]{2,1,0:T(8,128)(2,1)} %copy-done), custom_call_target="tpu_custom_call" | custom-call | tf_op jit(solution)/shard_map/last/pallas_call | solution.py:327
  120.8 1.3 %copy.22 = f32[8,2,256]{2,1,0:T(2,128)} copy(f32[8,2,256]{2,0,1:T(8,128)} %bitcast.31) | data formatting | bytes 32768
  (4 shorter events, 0.0 us)
Async XLA Ops:
  6.6 32.9 %all-to-all-start = ((f32[128,2,256]{2,1,0:T(2,128)}), f32[128,2,256]{2,1,0:T(2,128)S(1)}, u32[]{:S(2)}, u32[]{:S(2)}) async-start(f32[128,2,256]{2,1,0:T(2,128)} %get-tuple-element.36), calls=%async_computation | async-start | bytes 524288 | tf_op jit(solution)/shard_map/all_to_all | solution.py:260
  39.5 0.7 copy-start.4
  43.6 6.3 %copy-start.1 = (bf16[256,1024]{1,0:T(8,128)(2,1)S(1)}, bf16[256,1024]{1,0:T(8,128)(2,1)}, u32[]{:S(2)}) copy-start(bf16[256,1024]{1,0:T(8,128)(2,1)} %grad_out.1) | copy-start | bytes 1572868
  43.6 26.8 %all-to-all-start.1 = ((f32[128,8,128]{2,1,0:T(8,128)}), f32[128,8,128]{2,1,0:T(8,128)S(1)}, u32[]{:S(2)}, u32[]{:S(2)}) async-start(f32[128,8,128]{2,1,0:T(8,128)} %get-tuple-element.42), calls=%async_computation.1 | async-start | bytes 1048576 | tf_op jit(solution)/shard_map/all_to_all | solution.py:287
  49.9 1.0 copy-start.2
  51.2 27.5 %collective-permute-start = (bf16[512,256]{1,0:T(8,128)(2,1)S(1)}, bf16[512,256]{1,0:T(8,128)(2,1)S(1)}, u32[]{:S(2)}, u32[]{:S(2)}) collective-permute-start(bf16[512,256]{1,0:T(8,128)(2,1)S(1)} %get-tuple-element.51), channel_id=1, source_target_pairs={{0,4},{4,0},{1,5},{5,1},{2,6},{6,2},{3,7},{7,3},{8,12},{12,8},{9,1... | collective-permute-start | bytes 786440 | tf_op jit(solution)/shard_map/ppermute | solution.py:228
  53.1 26.4 %collective-permute-start.2 = (bf16[512,256]{1,0:T(8,128)(2,1)S(1)}, bf16[512,256]{1,0:T(8,128)(2,1)S(1)}, u32[]{:S(2)}, u32[]{:S(2)}) collective-permute-start(bf16[512,256]{1,0:T(8,128)(2,1)S(1)} %get-tuple-element.52), channel_id=1, source_target_pairs={{0,4},{4,0},{1,5},{5,1},{2,6},{6,2},{3,7},{7,3},{8,12},{12,8},{9,1... | collective-permute-start | bytes 786440 | tf_op jit(solution)/shard_map/ppermute | solution.py:228
  70.4 0.8 copy-start.3
  71.2 5.1 %copy-start.6 = (bf16[256,256]{1,0:T(8,128)(2,1)S(1)}, bf16[256,256]{1,0:T(8,128)(2,1)}, u32[]{:S(2)}) copy-start(bf16[256,256]{1,0:T(8,128)(2,1)} %get-tuple-element.54.own) | copy-start | bytes 393220
  74.4 8.8 %collective-permute-start.1 = (bf16[256,512]{1,0:T(8,128)(2,1)}, bf16[256,512]{1,0:T(8,128)(2,1)S(1)}, u32[]{:S(2)}, u32[]{:S(2)}) collective-permute-start(bf16[256,512]{1,0:T(8,128)(2,1)} %get-tuple-element.48.grad_pre.own), channel_id=1, source_target_pairs={{0,4},{4,0},{1,5},{5,1},{2,6},{6,2},{3,7},{7,3},{8,12},{12,8},{9,1... | collective-permute-start | bytes 786440 | tf_op jit(solution)/shard_map/ppermute | solution.py:228
  76.3 4.1 %collective-permute-start.3 = (bf16[256,256]{1,0:T(8,128)(2,1)S(1)}, bf16[256,256]{1,0:T(8,128)(2,1)S(1)}, u32[]{:S(2)}, u32[]{:S(2)}) collective-permute-start(bf16[256,256]{1,0:T(8,128)(2,1)S(1)} %copy-done.6), channel_id=1, source_target_pairs={{0,4},{4,0},{1,5},{5,1},{2,6},{6,2},{3,7},{7,3},{8,12},{12,8},{9,1... | collective-permute-start | bytes 393224 | tf_op jit(solution)/shard_map/ppermute | solution.py:228
  80.4 0.7 copy-start.7
  83.2 0.7 copy-start.5
  86.5 31.4 %all-to-all-start.2 = ((bf16[64,8,896]{2,1,0:T(8,128)(2,1)}), bf16[64,8,896]{2,1,0:T(8,128)(2,1)S(1)}, u32[]{:S(2)}, u32[]{:S(2)}) async-start(bf16[64,8,896]{2,1,0:T(8,128)(2,1)} %bulk.1), calls=%async_computation.2 | async-start | bytes 1835008 | tf_op jit(solution)/shard_map/all_to_all | solution.py:319
  93.6 9.8 %collective-permute-start.6 = (bf16[256,256]{1,0:T(8,128)(2,1)}, bf16[256,256]{1,0:T(8,128)(2,1)S(1)}, u32[]{:S(2)}, u32[]{:S(2)}) collective-permute-start(bf16[256,256]{1,0:T(8,128)(2,1)} %get-tuple-element.60), channel_id=1, source_target_pairs={{0,3},{1,0},{2,1},{3,2},{4,7},{5,4},{6,5},{7,6},{8,11},{9,8},{10,9... | collective-permute-start | bytes 393224 | tf_op jit(solution)/shard_map/ppermute | solution.py:323
  96.4 8.8 %collective-permute-start.5 = (bf16[256,256]{1,0:T(8,128)(2,1)}, bf16[256,256]{1,0:T(8,128)(2,1)S(1)}, u32[]{:S(2)}, u32[]{:S(2)}) collective-permute-start(bf16[256,256]{1,0:T(8,128)(2,1)} %get-tuple-element.58), channel_id=1, source_target_pairs={{0,2},{1,3},{2,0},{3,1},{4,6},{5,7},{6,4},{7,5},{8,10},{9,11},{10,... | collective-permute-start | bytes 393224 | tf_op jit(solution)/shard_map/ppermute | solution.py:323
  99.4 8.3 %collective-permute-start.4 = (bf16[256,256]{1,0:T(8,128)(2,1)}, bf16[256,256]{1,0:T(8,128)(2,1)S(1)}, u32[]{:S(2)}, u32[]{:S(2)}) collective-permute-start(bf16[256,256]{1,0:T(8,128)(2,1)} %get-tuple-element.56), channel_id=1, source_target_pairs={{0,1},{1,2},{2,3},{3,0},{4,5},{5,6},{6,7},{7,4},{8,9},{9,10},{10,1... | collective-permute-start | bytes 393224 | tf_op jit(solution)/shard_map/ppermute | solution.py:323
  117.9 0.9 copy-start

commit v3 on v2

--- a/solution.py
+++ b/solution.py
@@ -20,18 +20,38 @@
 
 
 def call(body, outs, ins, scratch=(), name=None):
-    return pl.pallas_call(
+    kernel = pl.pallas_call(
         body,
         out_shape=outs,
         in_specs=ins,
-        out_specs=jax.tree.map(lambda _: VM, outs),
+        out_specs=tuple(VM for _ in outs),
         scratch_shapes=list(scratch),
         name=name,
     )
 
+    def run(*args):
+        held = [
+            pltpu.with_memory_space_constraint(a, pltpu.VMEM) if spec is VM else a
+            for a, spec in zip(args, ins)
+        ]
+        return kernel(*held)
+
+    return run
+
 
 def shape(dims, dtype=F32):
+    return pltpu.VMEM(dims, dtype)
+
+
+def hbm_shape(dims, dtype=F32):
     return jax.ShapeDtypeStruct(dims, dtype)
+
+
+def tree_sum(x):
+    while x.shape[0] > 1:
+        half = x.shape[0] // 2
+        x = x[:half] + x[half:]
+    return x[0]
 
 
 def lanes(h):
@@ -113,13 +133,13 @@
 
 def norm_kernel(
     len_ref, counts, got, gain, shift, conv_out, grad_hidden, buf, ones_sum, conv_sum,
-    hidden, normed, grad_scaled, stats, pay, work, own_sum,
+    hidden, normed, grad_scaled, stats, sums_out, work,
 ):
     rows, channels = conv_out.shape
     count = 31
     first, live = row_masks(len_ref, rows)
     total = jnp.sum(counts[...].astype(F32), axis=1, keepdims=True) * BLOCK
-    sums = jnp.sum(got[...], axis=0)
+    sums = tree_sum(got[...])
     mean = sums[0:1] / total
     inv_std = lax.rsqrt(sums[1:2] / total - mean * mean + 1e-05)
     stats[0:1] = mean
@@ -136,17 +156,31 @@
         grad_scaled[:, cols] = grad
         heads.append((jnp.sum(grad, axis=0, keepdims=True), jnp.sum(grad * norm, axis=0, keepdims=True)))
         embed(work, h, grad, first)
-        tap_sums(own_sum, work[h, pl.ds(PAD, rows + PAD), :], buf, h, count, rows)
-        own_sum[count : count + 1, cols] = jnp.zeros((1, LANES), F32)
+        tap_sums(sums_out, work[h, pl.ds(PAD, rows + PAD), :], buf, h, count, rows)
+        sums_out[count : count + 1, cols] = jnp.zeros((1, LANES), F32)
     (s0, q0), (s1, q1) = heads
-    tile = jnp.concatenate([s0, s1, q0, q1, jnp.zeros((4, LANES), F32)], axis=0)
+    base = 3 * (count + 1)
+    for i, ref in enumerate((ones_sum, conv_sum)):
+        sums_out[(i + 1) * (count + 1) : (i + 2) * (count + 1)] = ref[...]
+    sums_out[base : base + 1] = jnp.concatenate([s0, s1], axis=1)
+    sums_out[base + 1 : base + 2] = jnp.concatenate([q0, q1], axis=1)
+    sums_out[base + 2 :] = jnp.zeros((6, channels), F32)
+
+
+def spread_kernel(own, other, pay, sums):
+    sums[...] = own[...] + other[...]
+    count = pay.shape[0] // 2
+    base = 3 * count
+    tile = jnp.concatenate(
+        [sums[base + i : base + i + 1, lanes(h)] for i in range(2) for h in range(2)]
+        + [jnp.zeros((4, LANES), F32)],
+        axis=0,
+    )
     pay[...] = jnp.broadcast_to(tile[None], pay.shape)
-    for j in range(pay.shape[0] // 2):
-        k, cols = j // 2, lanes(j % 2)
-        for i, ref in enumerate((own_sum, ones_sum, conv_sum)):
-            part = ref[k : k + 1, cols]
-            pay[2 * j, 4 + i : 5 + i, :] = part
-            pay[2 * j + 1, 4 + i : 5 + i, :] = part
+    for j in range(pay.shape[0]):
+        for i in range(3):
+            at = i * count + j // 2
+            pay[j, 4 + i : 5 + i, :] = sums[at : at + 1, lanes(j % 2)]
 
 
 def back_kernel(
@@ -156,7 +190,7 @@
     rows, channels = normed.shape
     first, live = row_masks(len_ref, rows)
     total = jnp.sum(counts[...].astype(F32), axis=1, keepdims=True) * BLOCK
-    sums = jnp.sum(got[...], axis=0)
+    sums = tree_sum(got[...])
     mean, inv_std = stats[0:1], stats[1:2]
     slices = []
     for h in range(channels // LANES):
@@ -189,18 +223,17 @@
         out[...] = term.astype(BF16)
 
 
-def rows_kernel(left, own, other, out):
-    tokens = own.shape[0]
-    total = jnp.dot(left[:, :tokens], own[...], preferred_element_type=F32)
-    total = total + jnp.dot(left[:, tokens:], other[...], preferred_element_type=F32)
+def rows_kernel(left_own, left_other, own, other, out):
+    total = jnp.dot(left_own[...], own[...], preferred_element_type=F32)
+    total = total + jnp.dot(left_other[...], other[...], preferred_element_type=F32)
     out[...] = total.astype(BF16)
 
 
-def bulk_kernel(left, own, other, out_rows, depth, pay):
-    tokens, width = own.shape
+def bulk_kernel(left_own, left_other, own, other, out_rows, depth, pay):
+    width = own.shape[1]
     peers, rows, _ = pay.shape
-    total = jnp.dot(left[:, :tokens], own[...], preferred_element_type=F32)
-    total = total + jnp.dot(left[:, tokens:], other[...], preferred_element_type=F32)
+    total = jnp.dot(left_own[...], own[...], preferred_element_type=F32)
+    total = total + jnp.dot(left_other[...], other[...], preferred_element_type=F32)
     pay[:, :, :width] = total.reshape(peers, rows, width).astype(BF16)
     pay[:, :, width : width + out_rows.shape[2]] = out_rows[...]
     pay[:, :, width + out_rows.shape[2] :] = jnp.broadcast_to(
@@ -209,9 +242,17 @@
 
 
 def last_kernel(got, in_rows, out_rows, depth):
-    width, more = in_rows.shape[1], out_rows.shape[1]
-    in_rows[...] = jnp.sum(got[:, :, :width].astype(F32), axis=0)
-    out_rows[...] = jnp.sum(got[:, :, width : width + more].astype(F32), axis=0)
+    more = out_rows.shape[1]
+    width = 2 * more
+    for g in range(2):
+        total = jnp.zeros((in_rows.shape[0], more), F32)
+        for j in range(got.shape[0]):
+            total = total + got[j, :, g * more : (g + 1) * more].astype(F32)
+        in_rows[:, g, :] = total
+    total = jnp.zeros((in_rows.shape[0], more), F32)
+    for j in range(got.shape[0]):
+        total = total + got[j, :, width : width + more].astype(F32)
+    out_rows[...] = total
     for j in range(2 * depth.shape[0]):
         depth[j // 2 : j // 2 + 1, lanes(j % 2)] = got[j, 0:1, width + more :].astype(F32)
 
@@ -253,7 +294,7 @@
 
     value, sig, buf, conv_out, pay = call(
         forward_kernel,
-        (full, full, shape((halves, buf_rows, LANES)), full, shape((peers, 2, channels))),
+        (full, full, shape((halves, buf_rows, LANES)), full, hbm_shape((peers, 2, channels))),
         [SM, VM, VM, VM],
         name="forward",
     )(lengths, frames, proj, taps)
@@ -266,30 +307,40 @@
         [pltpu.VMEM((halves, buf_rows, LANES), F32)],
         name="side",
     )(lengths, grad_out, proj_out, conv_out, buf)
-    left_in = core_halves(frames, core)
-    left_out = core_halves(grad_out, core)
-    left_in = jnp.concatenate([left_in[0], swap_cores(after(left_in[1], pay))], axis=1)
-    left_out = jnp.concatenate([left_out[0], swap_cores(after(left_out[1], pay))], axis=1)
-
-    hidden, normed, grad_scaled, stats, pay = call(
+    left_in, send_in = core_halves(frames, core)
+    left_out, send_out = core_halves(grad_out, core)
+    other_in = swap_cores(after(send_in, pay))
+    other_out = swap_cores(after(send_out, pay))
+
+    tap_rows = 3 * (count + 1)
+    hidden, normed, grad_scaled, stats, sums = call(
         norm_kernel,
         (
             shape((rows, channels), BF16),
             full,
             full,
             shape((2, channels)),
-            shape((peers, 8, LANES)),
+            shape((tap_rows + 8, channels)),
         ),
         [SM] + [VM] * 9,
-        [pltpu.VMEM((halves, buf_rows, LANES), F32), pltpu.VMEM((count + 1, channels), F32)],
+        [pltpu.VMEM((halves, buf_rows, LANES), F32)],
         name="norm",
     )(lengths, counts_row, got, gain_row, shift_row, conv_out, grad_hidden, buf, ones_sum, conv_sum)
-    got = lax.all_to_all(pay, DP, 0, 0)
+    (pay,) = call(
+        spread_kernel,
+        (hbm_shape((chips, 8, LANES)),),
+        [VM, VM],
+        [pltpu.VMEM((tap_rows + 8, channels), F32)],
+        name="spread",
+    )(sums, swap_cores(sums))
+    got = lax.all_to_all(pay, YZ, 0, 0)
 
     other = swap_cores(after(hidden, pay))
-    out_rows = call(rows_kernel, shape((width // 2, channels), BF16), [VM] * 3, name="out_rows")(
-        left_out, hidden, other
-    ).reshape(chips, rows_dev, channels)
+    (out_rows,) = call(rows_kernel, (shape((width // 2, channels), BF16),), [VM] * 4, name="out_rows")(
+        left_out, other_out, hidden, other
+    )
+    got, out_rows, other_in = lax.optimization_barrier((got, out_rows, other_in))
+    out_rows = out_rows.reshape(chips, rows_dev, channels)
 
     half = (chip % 2).astype(jnp.int32).reshape(1)
     grad_pre, shift_grad, gain_grad, depth = call(
@@ -310,12 +361,12 @@
     own, one, two, three = call(frame_kernel, (term,) * 4, [SM, VM, VM], name="frame")(
         mp.astype(jnp.int32).reshape(1), grad_pre, proj
     )
-    pay = call(
+    (pay,) = call(
         bulk_kernel,
-        shape((chips, rows_dev, 3 * channels + LANES), BF16),
-        [VM] * 5,
+        (hbm_shape((chips, rows_dev, 3 * channels + LANES), BF16),),
+        [VM] * 6,
         name="bulk",
-    )(left_in, grad_pre, other, out_rows, depth)
+    )(left_in, other_in, grad_pre, other, out_rows, depth)
     got = lax.all_to_all(pay, YZ, 0, 0)
 
     frame_sum = own.astype(F32)
@@ -324,13 +375,12 @@
         frame_sum = frame_sum + part.astype(F32)
     frame_grad = frame_sum.astype(BF16)
 
-    in_rows, out_grad, depth_grad = call(
+    in_grad, out_grad, depth_grad = call(
         last_kernel,
-        (shape((rows_dev, 2 * channels)), shape((rows_dev, channels)), shape((count, channels))),
+        (hbm_shape((rows_dev, 2, channels)), hbm_shape((rows_dev, channels)), hbm_shape((count, channels))),
         [VM],
         name="last",
     )(got)
-    in_grad = in_rows.reshape(rows_dev, 2, channels)
     return (frame_grad, in_grad, out_grad, depth_grad, gain_grad.reshape(channels), shift_grad.reshape(channels))
 
 

time: 124 us -> 111 us (0.90)
  Pallas kernels: 22.7 us -> 12.4 us
  waiting for transfers between devices: 39.3 us -> 35.3 us
  starting transfers between devices: 47.1 us -> 49.9 us
  other arithmetic: 3.32 us -> 0.73 us
    all_to_all x2 -> x1, waiting for transfers between devices: 26.4 us -> 11.6 us  [shards(): got = lax.all_to_all(pay, DP, 0, 0)]
    pallas_call x8 -> x9, Pallas kernels: 22.7 us -> 12.4 us  [run(): return kernel(*held)]
    all_to_all x1 -> x2, starting transfers between devices: 4.65 us -> 13.3 us  [shards(): got = lax.all_to_all(pay, YZ, 0, 0)]
    all_to_all x1 -> x2, waiting for transfers between devices: 8.64 us -> 15.5 us  [shards(): got = lax.all_to_all(pay, YZ, 0, 0)]
    all_to_all x2 -> x1, starting transfers between devices: 24.1 us -> 17.8 us  [shards(): got = lax.all_to_all(pay, DP, 0, 0)]
    ppermute x4 -> x5, waiting for transfers between devices: 0.01 us -> 3.23 us  [swap_cores(): return lax.ppermute(x, 'core', [(0, 1), (1, 0)])]
    concatenate x2 -> x0, other arithmetic: 1.69 us -> none  [the longest x1 0.85 us: shards(): jnp.concatenate([left_in[0], swap_cores(after(left_in[1], pay))], axis=1)]
    ppermute x4 -> x5, starting transfers between devices: 8.64 us -> 10.2 us  [swap_cores(): return lax.ppermute(x, 'core', [(0, 1), (1, 0)])]
  transfers between devices with their start and end apart: 10 -> 11, of which waited for: 5 -> 8; matrix products, arithmetic and copies ran while one was open for 3% -> 2% of each run, Pallas kernels for 9% -> 3%
where the time goes in v3:
time: 111 us; the launch traced here: 109 us
  starting transfers between devices  49.9 us (45%)
  waiting for transfers between devices  35.3 us (32%)
  Pallas kernels  12.4 us (11%)
  local copies, waits for them, and re-layouts  9.56 us (9%)
    all_to_all x1, starting transfers between devices, shards(): got = lax.all_to_all(pay, DP, 0, 0)  17.8 us
    all_to_all x2, waiting for transfers between devices, shards(): got = lax.all_to_all(pay, YZ, 0, 0)  15.5 us
    all_to_all x2, starting transfers between devices, shards(): got = lax.all_to_all(pay, YZ, 0, 0)  13.3 us
    pallas_call x9, Pallas kernels, run(): return kernel(*held)  12.4 us
    all_to_all x1, waiting for transfers between devices, shards(): got = lax.all_to_all(pay, DP, 0, 0)  11.6 us
    ppermute x5, starting transfers between devices, swap_cores(): return lax.ppermute(x, 'core', [(0, 1), (1, 0)])  10.2 us
    unnamed x47, local copies, waits for them, and re-layouts  9.47 us
    ppermute x3, starting transfers between devices, shards(): lax.ppermute(after(part, pay), 'mp', [(i, (i + d) % groups) for i in rang...  8.64 us
  transfers between devices with their start and end apart: 11, of which 8 were waited for; matrix products, arithmetic and copies ran while one was open for 2% of the time, Pallas kernels for 3%

profile of v3, /device:TPU:6, one launch (start us, length us, event | category | flops | bytes accessed | tf_op | source)
XLA Modules:
  0.0 108.8 jit_solution(7525915733074735898)
XLA Ops:
  0.7 1.5 %copy.21 = bf16[128,8,2,256]{3,1,2,0:T(8,128)(2,1)S(1)} copy(bf16[128,8,2,256]{3,2,1,0:T(2,128)(2,1)} %bitcast.36) | data formatting | bytes 2097152
  2.2 2.7 %forward.1 = (f32[256,256]{1,0:T(8,128)S(1)}, f32[256,256]{1,0:T(8,128)S(1)}, f32[2,304,128]{2,1,0:T(8,128)S(1)}, f32[256,256]{1,0:T(8,128)S(1)}, f32[128,2,256]{2,1,0:T(2,128)}) custom-call(s32[1,2]{1,0:T(1,128)} %len_ref.7, bf16[256,1024]{1,0:T(8,128)(2,1)S(1)} %copy-done.3, bf16[1024,512]{1,0:T(8,128)(2,1)S(1)} %bitcast.26, f32[31,256]{1,0:T(8,128)S(1)} %copy-done.15), custom_call_target="tpu_custom_call" | custom-call | tf_op jit(solution)/shard_map/forward/pallas_call | solution.py:37
  4.9 0.7 copy-done.5
  5.6 0.7 copy-done.7
  6.3 17.8 %all-to-all-start = ((f32[128,2,256]{2,1,0:T(2,128)}), f32[128,2,256]{2,1,0:T(2,128)S(1)}, u32[]{:S(2)}, u32[]{:S(2)}) async-start(f32[128,2,256]{2,1,0:T(2,128)} %get-tuple-element.39), calls=%async_computation | async-start | bytes 524288 | tf_op jit(solution)/shard_map/all_to_all | solution.py:301
  24.1 0.0 copy-start.4
  24.1 1.0 copy-done.4
  25.1 2.5 %side.1 = (f32[256,256]{1,0:T(8,128)S(1)}, f32[32,256]{1,0:T(8,128)S(1)}, f32[32,256]{1,0:T(8,128)S(1)}) custom-call(s32[1,2]{1,0:T(1,128)} %len_ref.7, bf16[256,1024]{1,0:T(8,128)(2,1)S(1)} %copy-done.2, bf16[1024,256]{1,0:T(8,128)(2,1)S(1)} %copy-done.4, f32[256,256]{1,0:T(8,128)S(1)} %get-tuple-element.40.conv_out, f32[2,304,128]{2,1,0:T(8,128)S(1)} %get-tuple-element.41.buf), custom_call_target="tpu_custom_call" | custom-call | tf_op jit(solution)/shard_map/side/pallas_call | solution.py:37
  27.6 11.6 %all-to-all-done.got = f32[128,2,256]{2,1,0:T(2,128)S(1)} async-done(((f32[128,2,256]{2,1,0:T(2,128)}), f32[128,2,256]{2,1,0:T(2,128)S(1)}, u32[]{:S(2)}, u32[]{:S(2)}) %all-to-all-start) | async-done | bytes 262176 | tf_op jit(solution)/shard_map/all_to_all | solution.py:301
  39.2 0.7 copy-done.18
  39.9 0.0 copy-done.19
  39.9 1.9 %norm.1 = (bf16[256,256]{1,0:T(8,128)(2,1)S(1)}, f32[256,256]{1,0:T(8,128)S(1)}, f32[256,256]{1,0:T(8,128)S(1)}, f32[2,256]{1,0:T(2,128)S(1)}, f32[104,256]{1,0:T(8,128)S(1)}) custom-call(s32[1,2]{1,0:T(1,128)} %len_ref.7, s32[1,128]{1,0:T(1,128)S(1)} %bitcast.31, f32[128,2,256]{2,1,0:T(2,128)S(1)} %all-to-all-done.got, f32[1,256]{1,0:T(1,128)S(1)} %bitcast.29, ...), custom_call_target="tpu_custom_call" | custom-call | tf_op jit(solution)/shard_map/norm/pallas_call | solution.py:37
  41.7 0.7 copy-done.11
  42.5 1.9 %collective-permute-start = (f32[104,256]{1,0:T(8,128)S(1)}, f32[104,256]{1,0:T(8,128)S(1)}, u32[]{:S(2)}, u32[]{:S(2)}) collective-permute-start(f32[104,256]{1,0:T(8,128)S(1)} %get-tuple-element.45.own), channel_id=1, source_target_pairs={{0,4},{4,0},{1,5},{5,1},{2,6},{6,2},{3,7},{7,3},{8,12},{12,8},{9,1... | collective-permute-start | bytes 319496 | tf_op jit(solution)/shard_map/ppermute | solution.py:269
  44.4 1.3 %collective-permute-done.other = f32[104,256]{1,0:T(8,128)S(1)} collective-permute-done((f32[104,256]{1,0:T(8,128)S(1)}, f32[104,256]{1,0:T(8,128)S(1)}, u32[]{:S(2)}, u32[]{:S(2)}) %collective-permute-start) | collective-permute-done | bytes 106528 | tf_op jit(solution)/shard_map/ppermute | solution.py:269
  45.6 0.8 spread.1
  46.4 0.0 copy-done.9
  46.4 4.6 %all-to-all-start.1 = ((f32[64,8,128]{2,1,0:T(8,128)}), f32[64,8,128]{2,1,0:T(8,128)S(1)}, u32[]{:S(2)}, u32[]{:S(2)}) async-start(f32[64,8,128]{2,1,0:T(8,128)} %spread.1), calls=%async_computation.1 | async-start | bytes 524288 | tf_op jit(solution)/shard_map/all_to_all | solution.py:336
  51.1 0.2 copy.19
  51.3 2.1 %collective-permute-start.1 = (bf16[512,256]{1,0:T(8,128)(2,1)S(1)}, bf16[512,256]{1,0:T(8,128)(2,1)S(1)}, u32[]{:S(2)}, u32[]{:S(2)}) collective-permute-start(bf16[512,256]{1,0:T(8,128)(2,1)S(1)} %get-tuple-element.46), channel_id=1, source_target_pairs={{0,4},{4,0},{1,5},{5,1},{2,6},{6,2},{3,7},{7,3},{8,12},{12,8},{9,1... | collective-permute-start | bytes 786440 | tf_op jit(solution)/shard_map/ppermute | solution.py:269
  53.4 0.2 copy.20
  53.7 2.3 %collective-permute-start.3 = (bf16[512,256]{1,0:T(8,128)(2,1)S(1)}, bf16[512,256]{1,0:T(8,128)(2,1)S(1)}, u32[]{:S(2)}, u32[]{:S(2)}) collective-permute-start(bf16[512,256]{1,0:T(8,128)(2,1)S(1)} %get-tuple-element.49), channel_id=1, source_target_pairs={{0,4},{4,0},{1,5},{5,1},{2,6},{6,2},{3,7},{7,3},{8,12},{12,8},{9,1... | collective-permute-start | bytes 786440 | tf_op jit(solution)/shard_map/ppermute | solution.py:269
  55.9 2.1 %collective-permute-start.2 = (bf16[256,256]{1,0:T(8,128)(2,1)S(1)}, bf16[256,256]{1,0:T(8,128)(2,1)S(1)}, u32[]{:S(2)}, u32[]{:S(2)}) collective-permute-start(bf16[256,256]{1,0:T(8,128)(2,1)S(1)} %get-tuple-element.48.own), channel_id=1, source_target_pairs={{0,4},{4,0},{1,5},{5,1},{2,6},{6,2},{3,7},{7,3},{8,12},{12,8},{9,1... | collective-permute-start | bytes 393224 | tf_op jit(solution)/shard_map/ppermute | solution.py:269
  58.0 0.0 collective-permute-done.1.left_other
  58.0 0.7 copy-done.13
  58.7 0.4 collective-permute-done.2.other
  59.2 0.9 copy-done.14
  60.1 0.9 copy-done.17
  61.1 0.3 out_rows.1
  61.4 0.0 collective-permute-done.3.left_other
  61.4 5.0 %all-to-all-done.1.got = f32[64,8,128]{2,1,0:T(8,128)S(1)} async-done(((f32[64,8,128]{2,1,0:T(8,128)}), f32[64,8,128]{2,1,0:T(8,128)S(1)}, u32[]{:S(2)}, u32[]{:S(2)}) %all-to-all-start.1) | async-done | bytes 262176 | tf_op jit(solution)/shard_map/all_to_all | solution.py:336
  66.4 1.7 %back.1 = (bf16[256,512]{1,0:T(8,128)(2,1)S(1)}, f32[1,256]{1,0:T(1,128)S(1)}, f32[1,256]{1,0:T(1,128)S(1)}, f32[8,128]{1,0:T(8,128)S(1)}) custom-call(s32[1,2]{1,0:T(1,128)} %len_ref.7, s32[1]{0:T(128)} %bitcast.1.half_ref, s32[1,128]{1,0:T(1,128)S(1)} %bitcast.32, f32[64,8,128]{2,1,0:T(8,128)S(1)} %all-to-all-done.1.got, f32[1,256]{1,0:T(1,128)S(1)} %bitcast.30, ...), custom_call_target="tpu_custom_call" | custom-call | tf_op jit(solution)/shard_map/back/pallas_call | solution.py:37
  68.1 1.9 %collective-permute-start.4 = (bf16[256,512]{1,0:T(8,128)(2,1)S(1)}, bf16[256,512]{1,0:T(8,128)(2,1)S(1)}, u32[]{:S(2)}, u32[]{:S(2)}) collective-permute-start(bf16[256,512]{1,0:T(8,128)(2,1)S(1)} %get-tuple-element.56.grad_pre.own), channel_id=1, source_target_pairs={{0,4},{4,0},{1,5},{5,1},{2,6},{6,2},{3,7},{7,3},{8,12},{12,8},{9,1... | collective-permute-start | bytes 786440 | tf_op jit(solution)/shard_map/ppermute | solution.py:269
  70.0 1.5 %collective-permute-done.4.other = bf16[256,512]{1,0:T(8,128)(2,1)S(1)} collective-permute-done((bf16[256,512]{1,0:T(8,128)(2,1)S(1)}, bf16[256,512]{1,0:T(8,128)(2,1)S(1)}, u32[]{:S(2)}, u32[]{:S(2)}) %collective-permute-start.4) | collective-permute-done | bytes 262176 | tf_op jit(solution)/shard_map/ppermute | solution.py:269
  71.5 1.4 %bulk.1 = bf16[64,8,896]{2,1,0:T(8,128)(2,1)} custom-call(bf16[512,256]{1,0:T(8,128)(2,1)S(1)} %get-tuple-element.72.left_own, bf16[512,256]{1,0:T(8,128)(2,1)S(1)} %collective-permute-done.3.left_other, bf16[256,512]{1,0:T(8,128)(2,1)S(1)} %get-tuple-element.56.grad_pre.own, bf16[256,512]{1,0:T(8,128)(2,1)S(1)} %collective-permute-done.4.other, ...), custom_call_target="tpu_custom_call" | custom-call | tf_op jit(solution)/shard_map/bulk/pallas_call | solution.py:37
  72.9 8.7 %all-to-all-start.2 = ((bf16[64,8,896]{2,1,0:T(8,128)(2,1)}), bf16[64,8,896]{2,1,0:T(8,128)(2,1)S(1)}, u32[]{:S(2)}, u32[]{:S(2)}) async-start(bf16[64,8,896]{2,1,0:T(8,128)(2,1)} %bulk.1), calls=%async_computation.2 | async-start | bytes 1835008 | tf_op jit(solution)/shard_map/all_to_all | solution.py:370
  81.6 0.5 frame.1
  82.0 2.4 %collective-permute-start.5 = (bf16[256,256]{1,0:T(8,128)(2,1)S(1)}, bf16[256,256]{1,0:T(8,128)(2,1)S(1)}, u32[]{:S(2)}, u32[]{:S(2)}) collective-permute-start(bf16[256,256]{1,0:T(8,128)(2,1)S(1)} %get-tuple-element.62), channel_id=1, source_target_pairs={{0,1},{1,2},{2,3},{3,0},{4,5},{5,6},{6,7},{7,4},{8,9},{9,10},{10,1... | collective-permute-start | bytes 393224 | tf_op jit(solution)/shard_map/ppermute | solution.py:374
  84.4 4.3 %collective-permute-start.6 = (bf16[256,256]{1,0:T(8,128)(2,1)S(1)}, bf16[256,256]{1,0:T(8,128)(2,1)S(1)}, u32[]{:S(2)}, u32[]{:S(2)}) collective-permute-start(bf16[256,256]{1,0:T(8,128)(2,1)S(1)} %get-tuple-element.64), channel_id=1, source_target_pairs={{0,2},{1,3},{2,0},{3,1},{4,6},{5,7},{6,4},{7,5},{8,10},{9,11},{10,... | collective-permute-start | bytes 393224 | tf_op jit(solution)/shard_map/ppermute | solution.py:374
  88.8 1.9 %collective-permute-start.7 = (bf16[256,256]{1,0:T(8,128)(2,1)S(1)}, bf16[256,256]{1,0:T(8,128)(2,1)S(1)}, u32[]{:S(2)}, u32[]{:S(2)}) collective-permute-start(bf16[256,256]{1,0:T(8,128)(2,1)S(1)} %get-tuple-element.66), channel_id=1, source_target_pairs={{0,3},{1,0},{2,1},{3,2},{4,7},{5,4},{6,5},{7,6},{8,11},{9,8},{10,9... | collective-permute-start | bytes 393224 | tf_op jit(solution)/shard_map/ppermute | solution.py:374
  90.7 0.6 copy.22
  91.3 0.6 copy.23
  91.8 0.0 collective-permute-done.5
  91.8 1.0 collective-permute-done.6
  92.8 4.0 %collective-permute-done.7 = bf16[256,256]{1,0:T(8,128)(2,1)S(1)} collective-permute-done((bf16[256,256]{1,0:T(8,128)(2,1)S(1)}, bf16[256,256]{1,0:T(8,128)(2,1)S(1)}, u32[]{:S(2)}, u32[]{:S(2)}) %collective-permute-start.7) | collective-permute-done | bytes 131104 | tf_op jit(solution)/shard_map/ppermute | solution.py:374
  96.9 0.7 add_convert_fusion
  97.6 10.5 %all-to-all-done.2.got = bf16[64,8,896]{2,1,0:T(8,128)(2,1)S(1)} async-done(((bf16[64,8,896]{2,1,0:T(8,128)(2,1)}), bf16[64,8,896]{2,1,0:T(8,128)(2,1)S(1)}, u32[]{:S(2)}, u32[]{:S(2)}) %all-to-all-start.2) | async-done | bytes 917536 | tf_op jit(solution)/shard_map/all_to_all | solution.py:370
  108.0 0.8 last.1
  (33 shorter events, 0.1 us)
Async XLA Ops:
  0.6 1.5 %copy-start.3 = (bf16[256,1024]{1,0:T(8,128)(2,1)S(1)}, bf16[256,1024]{1,0:T(8,128)(2,1)}, u32[]{:S(2)}) copy-start(bf16[256,1024]{1,0:T(8,128)(2,1)} %frames.1) | copy-start | bytes 1572868
  0.6 1.5 %copy-start.15 = (f32[31,256]{1,0:T(8,128)S(1)}, f32[31,256]{1,0:T(8,128)}, u32[]{:S(2)}) copy-start(f32[31,256]{1,0:T(8,128)} %taps.3) | copy-start | bytes 95236
  2.2 3.4 %copy-start = (bf16[128,8,2,256]{3,1,2,0:T(8,128)(2,1)}, bf16[128,8,2,256]{3,1,2,0:T(8,128)(2,1)S(1)}, u32[]{:S(2)}) copy-start(bf16[128,8,2,256]{3,1,2,0:T(8,128)(2,1)S(1)} %copy.21) | copy-start | bytes 3145732
  4.9 0.7 copy-start.5
  5.6 0.7 copy-start.7
  5.6 18.5 %copy-start.2 = (bf16[256,1024]{1,0:T(8,128)(2,1)S(1)}, bf16[256,1024]{1,0:T(8,128)(2,1)}, u32[]{:S(2)}) copy-start(bf16[256,1024]{1,0:T(8,128)(2,1)} %grad_out.1) | copy-start | bytes 1572868
  6.3 32.9 %all-to-all-start = ((f32[128,2,256]{2,1,0:T(2,128)}), f32[128,2,256]{2,1,0:T(2,128)S(1)}, u32[]{:S(2)}, u32[]{:S(2)}) async-start(f32[128,2,256]{2,1,0:T(2,128)} %get-tuple-element.39), calls=%async_computation | async-start | bytes 524288 | tf_op jit(solution)/shard_map/all_to_all | solution.py:301
  24.1 1.0 copy-start.4
  25.1 14.0 %copy-start.20 = (f32[256]{0:T(256)S(1)}, f32[256]{0:T(256)}, u32[]{:S(2)}) copy-start(f32[256]{0:T(256)} %param.13) | copy-start | bytes 3076
  39.2 0.7 copy-start.18
  39.2 0.7 copy-start.19
  41.7 0.7 copy-start.11
  42.5 4.0 %copy-start.9 = (f32[256,256]{1,0:T(8,128)}, f32[256,256]{1,0:T(8,128)S(1)}, u32[]{:S(2)}) copy-start(f32[256,256]{1,0:T(8,128)S(1)} %get-tuple-element.52.normed) | copy-start | bytes 786436
  42.5 13.5 %copy-start.16 = (bf16[256,256]{1,0:T(8,128)(2,1)}, bf16[256,256]{1,0:T(8,128)(2,1)S(1)}, u32[]{:S(2)}) copy-start(bf16[256,256]{1,0:T(8,128)(2,1)S(1)} %get-tuple-element.48.own) | copy-start | bytes 393220
  42.5 3.2 %collective-permute-start = (f32[104,256]{1,0:T(8,128)S(1)}, f32[104,256]{1,0:T(8,128)S(1)}, u32[]{:S(2)}, u32[]{:S(2)}) collective-permute-start(f32[104,256]{1,0:T(8,128)S(1)} %get-tuple-element.45.own), channel_id=1, source_target_pairs={{0,4},{4,0},{1,5},{5,1},{2,6},{6,2},{3,7},{7,3},{8,12},{12,8},{9,1... | collective-permute-start | bytes 319496 | tf_op jit(solution)/shard_map/ppermute | solution.py:269
  46.4 19.9 %all-to-all-start.1 = ((f32[64,8,128]{2,1,0:T(8,128)}), f32[64,8,128]{2,1,0:T(8,128)S(1)}, u32[]{:S(2)}, u32[]{:S(2)}) async-start(f32[64,8,128]{2,1,0:T(8,128)} %spread.1), calls=%async_computation.1 | async-start | bytes 524288 | tf_op jit(solution)/shard_map/all_to_all | solution.py:336
  51.3 6.7 %collective-permute-start.1 = (bf16[512,256]{1,0:T(8,128)(2,1)S(1)}, bf16[512,256]{1,0:T(8,128)(2,1)S(1)}, u32[]{:S(2)}, u32[]{:S(2)}) collective-permute-start(bf16[512,256]{1,0:T(8,128)(2,1)S(1)} %get-tuple-element.46), channel_id=1, source_target_pairs={{0,4},{4,0},{1,5},{5,1},{2,6},{6,2},{3,7},{7,3},{8,12},{12,8},{9,1... | collective-permute-start | bytes 786440 | tf_op jit(solution)/shard_map/ppermute | solution.py:269
  53.7 7.7 %collective-permute-start.3 = (bf16[512,256]{1,0:T(8,128)(2,1)S(1)}, bf16[512,256]{1,0:T(8,128)(2,1)S(1)}, u32[]{:S(2)}, u32[]{:S(2)}) collective-permute-start(bf16[512,256]{1,0:T(8,128)(2,1)S(1)} %get-tuple-element.49), channel_id=1, source_target_pairs={{0,4},{4,0},{1,5},{5,1},{2,6},{6,2},{3,7},{7,3},{8,12},{12,8},{9,1... | collective-permute-start | bytes 786440 | tf_op jit(solution)/shard_map/ppermute | solution.py:269
  55.9 3.2 %collective-permute-start.2 = (bf16[256,256]{1,0:T(8,128)(2,1)S(1)}, bf16[256,256]{1,0:T(8,128)(2,1)S(1)}, u32[]{:S(2)}, u32[]{:S(2)}) collective-permute-start(bf16[256,256]{1,0:T(8,128)(2,1)S(1)} %get-tuple-element.48.own), channel_id=1, source_target_pairs={{0,4},{4,0},{1,5},{5,1},{2,6},{6,2},{3,7},{7,3},{8,12},{12,8},{9,1... | collective-permute-start | bytes 393224 | tf_op jit(solution)/shard_map/ppermute | solution.py:269
  58.0 0.7 copy-start.13
  59.2 1.0 copy-start.14
  60.1 0.9 copy-start.17
  61.0 5.3 %copy-start.6 = (f32[256,256]{1,0:T(8,128)S(1)}, f32[256,256]{1,0:T(8,128)}, u32[]{:S(2)}) copy-start(f32[256,256]{1,0:T(8,128)} %copy-done.5) | copy-start | bytes 786436
  61.0 5.3 %copy-start.8 = (f32[256,256]{1,0:T(8,128)S(1)}, f32[256,256]{1,0:T(8,128)}, u32[]{:S(2)}) copy-start(f32[256,256]{1,0:T(8,128)} %copy-done.7) | copy-start | bytes 786436
  61.0 5.3 %copy-start.10 = (f32[256,256]{1,0:T(8,128)S(1)}, f32[256,256]{1,0:T(8,128)}, u32[]{:S(2)}) copy-start(f32[256,256]{1,0:T(8,128)} %copy-done.9) | copy-start | bytes 786436
  61.0 5.3 %copy-start.12 = (f32[256,256]{1,0:T(8,128)S(1)}, f32[256,256]{1,0:T(8,128)}, u32[]{:S(2)}) copy-start(f32[256,256]{1,0:T(8,128)} %copy-done.11) | copy-start | bytes 786436
  68.1 3.4 %collective-permute-start.4 = (bf16[256,512]{1,0:T(8,128)(2,1)S(1)}, bf16[256,512]{1,0:T(8,128)(2,1)S(1)}, u32[]{:S(2)}, u32[]{:S(2)}) collective-permute-start(bf16[256,512]{1,0:T(8,128)(2,1)S(1)} %get-tuple-element.56.grad_pre.own), channel_id=1, source_target_pairs={{0,4},{4,0},{1,5},{5,1},{2,6},{6,2},{3,7},{7,3},{8,12},{12,8},{9,1... | collective-permute-start | bytes 786440 | tf_op jit(solution)/shard_map/ppermute | solution.py:269
  72.9 8.7 %copy-start.1 = (bf16[128,8,2,256]{3,1,2,0:T(8,128)(2,1)S(1)}, bf16[128,8,2,256]{3,1,2,0:T(8,128)(2,1)}, u32[]{:S(2)}) copy-start(bf16[128,8,2,256]{3,1,2,0:T(8,128)(2,1)} %copy-done) | copy-start | bytes 3145732
  72.9 35.2 %all-to-all-start.2 = ((bf16[64,8,896]{2,1,0:T(8,128)(2,1)}), bf16[64,8,896]{2,1,0:T(8,128)(2,1)S(1)}, u32[]{:S(2)}, u32[]{:S(2)}) async-start(bf16[64,8,896]{2,1,0:T(8,128)(2,1)} %bulk.1), calls=%async_computation.2 | async-start | bytes 1835008 | tf_op jit(solution)/shard_map/all_to_all | solution.py:370
  82.0 9.8 %collective-permute-start.5 = (bf16[256,256]{1,0:T(8,128)(2,1)S(1)}, bf16[256,256]{1,0:T(8,128)(2,1)S(1)}, u32[]{:S(2)}, u32[]{:S(2)}) collective-permute-start(bf16[256,256]{1,0:T(8,128)(2,1)S(1)} %get-tuple-element.62), channel_id=1, source_target_pairs={{0,1},{1,2},{2,3},{3,0},{4,5},{5,6},{6,7},{7,4},{8,9},{9,10},{10,1... | collective-permute-start | bytes 393224 | tf_op jit(solution)/shard_map/ppermute | solution.py:374
  84.4 8.4 %collective-permute-start.6 = (bf16[256,256]{1,0:T(8,128)(2,1)S(1)}, bf16[256,256]{1,0:T(8,128)(2,1)S(1)}, u32[]{:S(2)}, u32[]{:S(2)}) collective-permute-start(bf16[256,256]{1,0:T(8,128)(2,1)S(1)} %get-tuple-element.64), channel_id=1, source_target_pairs={{0,2},{1,3},{2,0},{3,1},{4,6},{5,7},{6,4},{7,5},{8,10},{9,11},{10,... | collective-permute-start | bytes 393224 | tf_op jit(solution)/shard_map/ppermute | solution.py:374
  88.8 8.1 %collective-permute-start.7 = (bf16[256,256]{1,0:T(8,128)(2,1)S(1)}, bf16[256,256]{1,0:T(8,128)(2,1)S(1)}, u32[]{:S(2)}, u32[]{:S(2)}) collective-permute-start(bf16[256,256]{1,0:T(8,128)(2,1)S(1)} %get-tuple-element.66), channel_id=1, source_target_pairs={{0,3},{1,0},{2,1},{3,2},{4,7},{5,4},{6,5},{7,6},{8,11},{9,8},{10,9... | collective-permute-start | bytes 393224 | tf_op jit(solution)/shard_map/ppermute | solution.py:374

commit v4 on v3

v4 whole, which is shorter than its diff:
```python
import functools

import jax
import jax.numpy as jnp
from jax import lax
from jax.experimental import pallas as pl
from jax.experimental.pallas import tpu as pltpu
from jax.sharding import Mesh, PartitionSpec as P

BLOCK = 128
DP = ("y", "z", "core")
YZ = ("y", "z")
LANES = 128
TAPS = 31
PAD = 16
F32 = jnp.float32
BF16 = jnp.bfloat16
VM = pl.BlockSpec(memory_space=pltpu.VMEM)
HB = pl.BlockSpec(memory_space=pltpu.VMEM)
SM = pl.BlockSpec(memory_space=pltpu.SMEM)
NT = (((1,), (1,)), ((), ()))


def call(body, outs, ins, scratch=(), name=None):
    kernel = pl.pallas_call(
        body,
        out_shape=outs,
        in_specs=ins,
        out_specs=tuple(VM for _ in outs),
        scratch_shapes=list(scratch),
        name=name,
    )

    def run(*args):
        held = [
            pltpu.with_memory_space_constraint(a, pltpu.VMEM) if spec is VM else a
            for a, spec in zip(args, ins)
        ]
        return kernel(*held)

    return run


def shape(dims, dtype=F32):
    return pltpu.VMEM(dims, dtype)


def hbm_shape(dims, dtype=F32):
    return jax.ShapeDtypeStruct(dims, dtype)


def tree_sum(x):
    while x.shape[0] > 1:
        half = x.shape[0] // 2
        x = x[:half] + x[half:]
    return x[0]


def lanes(h):
    return slice(h * LANES, (h + 1) * LANES)


def row_masks(split, end, rows):
    row = lax.broadcasted_iota(jnp.int32, (rows, LANES), 0).astype(F32)
    return row < split, row < end


def own_masks(len_ref, rows):
    split = len_ref[0, 0]
    return row_masks(split.astype(F32), (split + len_ref[0, 1]).astype(F32), rows)


def embed(buf, h, x, first):
    rows = x.shape[0]
    zero = jnp.zeros((PAD, LANES), F32)
    head = jnp.where(first, x, 0.0)
    tail = jnp.where(first, 0.0, x)
    buf[h, 0:PAD] = zero
    buf[h, PAD : 2 * PAD] = head[:PAD]
    buf[h, 2 * PAD : PAD + rows] = head[PAD:] + tail[: rows - PAD]
    buf[h, PAD + rows : 2 * PAD + rows] = tail[rows - PAD :]
    buf[h, 2 * PAD + rows : 3 * PAD + rows] = zero


def conv(buf, h, taps, rows, first, sign):
    count = taps.shape[0]
    radius = count // 2
    span = rows + PAD
    total = jnp.zeros((span, LANES), F32)
    for k in range(count):
        total = total + taps[k : k + 1, lanes(h)] * buf[h, pl.ds(PAD + sign * (k - radius), span), :]
    return jnp.where(first, total[:rows], total[PAD:])


def tap_sums(out, values, buf, h, count, rows):
    radius = count // 2
    span = rows + PAD
    for k in range(count):
        prod = values * buf[h, pl.ds(PAD + k - radius, span), :]
        out[k : k + 1, lanes(h)] = jnp.sum(prod, axis=0, keepdims=True)


def gated(pre, live, h, channels):
    value = pre[:, lanes(h)]
    sig = jax.nn.sigmoid(pre[:, channels + h * LANES : channels + (h + 1) * LANES])
    return value, sig, jnp.where(live, value * sig, 0.0).astype(BF16).astype(F32)


def forward_kernel(len_ref, frames, proj, taps, conv_out, buf, pay, pre):
    rows, channels = conv_out.shape
    first, live = own_masks(len_ref, rows)
    pre[...] = jnp.dot(frames[...], proj[...], preferred_element_type=F32)
    sums = []
    for h in range(channels // LANES):
        _, _, glu = gated(pre, live, h, channels)
        embed(buf, h, glu, first)
        out = jnp.where(live, conv(buf, h, taps, rows, first, 1), 0.0)
        conv_out[:, lanes(h)] = out
        sums.append(
            jnp.concatenate(
                [jnp.sum(out, axis=0, keepdims=True), jnp.sum(out * out, axis=0, keepdims=True)], axis=0
            )
        )
    both = jnp.concatenate(sums, axis=1)
    pay[...] = jnp.broadcast_to(both[None], pay.shape)


def known_sums(ones_sum, conv_sum, conv_out, buf, work, h, rows, first, live):
    count = TAPS
    embed(work, h, jnp.where(live, 1.0, 0.0), first)
    tap_sums(ones_sum, work[h, pl.ds(PAD, rows + PAD), :], buf, h, count, rows)
    embed(work, h, conv_out[:, lanes(h)], first)
    tap_sums(conv_sum, work[h, pl.ds(PAD, rows + PAD), :], buf, h, count, rows)
    ones_sum[count : count + 1, lanes(h)] = jnp.zeros((1, LANES), F32)
    conv_sum[count : count + 1, lanes(h)] = jnp.zeros((1, LANES), F32)


def side_kernel(
    len_ref, frames, proj, grad_out, proj_out, conv_out, buf, gain, shift, counts,
    value, sig, grad_hidden, ones_sum, conv_sum, params, pre, hid, work,
):
    rows, channels = conv_out.shape
    first, live = own_masks(len_ref, rows)
    pre[...] = jnp.dot(frames[...], proj[...], preferred_element_type=F32)
    hid[...] = jnp.dot(grad_out[...], proj_out[...], preferred_element_type=F32)
    for h in range(channels // LANES):
        cols = lanes(h)
        value[:, cols], sig[:, cols], _ = gated(pre, live, h, channels)
        grad_hidden[:, cols] = jnp.where(live, hid[:, cols], 0.0)
        known_sums(ones_sum, conv_sum, conv_out, buf, work, h, rows, first, live)
    total = jnp.sum(counts[...].astype(F32), axis=1, keepdims=True) * BLOCK
    params[0:1] = gain[...]
    params[1:2] = shift[...]
    params[2:3] = jnp.broadcast_to(total, (1, channels))
    params[3:] = jnp.zeros((5, channels), F32)


def mirror_kernel(
    given, proj, proj_out, taps,
    value, sig, grad_hidden, ones_sum, conv_sum, conv_out, buf, ends, pre, hid, work,
):
    rows, channels = conv_out.shape
    spans = given[2 * rows : 2 * rows + 16, :LANES].astype(F32)[0:1]
    split = spans[:, 0:1]
    end = split + spans[:, 1:2]
    ends[0:1] = jnp.broadcast_to(split, (1, LANES))
    ends[1:2] = jnp.broadcast_to(end, (1, LANES))
    ends[2:] = jnp.zeros((6, LANES), F32)
    first, live = row_masks(ends[0:1], ends[1:2], rows)
    pre[...] = jnp.dot(given[:rows], proj[...], preferred_element_type=F32)
    hid[...] = jnp.dot(given[rows : 2 * rows], proj_out[...], preferred_element_type=F32)
    for h in range(channels // LANES):
        cols = lanes(h)
        value[:, cols], sig[:, cols], glu = gated(pre, live, h, channels)
        embed(buf, h, glu, first)
        conv_out[:, cols] = jnp.where(live, conv(buf, h, taps, rows, first, 1), 0.0)
        grad_hidden[:, cols] = jnp.where(live, hid[:, cols], 0.0)
        known_sums(ones_sum, conv_sum, conv_out, buf, work, h, rows, first, live)


def norm_kernel(
    len_ref, ends, got, params, conv_a, conv_b, hid_a, hid_b, buf_a, buf_b,
    ones_a, ones_b, conv_sum_a, conv_sum_b,
    hidden, grad_scaled, stats, pay, work, sums,
):
    rows, channels = conv_a.shape
    count = TAPS
    total = params[2:3]
    found = tree_sum(got[...])
    mean = found[0:1] / total
    inv_std = lax.rsqrt(found[1:2] / total - mean * mean + 1e-05)
    stats[0:1] = mean
    stats[1:2] = inv_std
    heads = []
    for h in range(channels // LANES):
        cols = lanes(h)
        head = []
        for part, (conv_out, grad_hidden, buf) in enumerate(((conv_a, hid_a, buf_a), (conv_b, hid_b, buf_b))):
            masks = own_masks(len_ref, rows) if part == 0 else row_masks(ends[0:1], ends[1:2], rows)
            first, live = masks
            span = slice(part * rows, (part + 1) * rows)
            norm = (conv_out[:, cols] - mean[:, cols]) * inv_std[:, cols]
            scaled = norm * params[0:1, cols] + params[1:2, cols]
            s = jax.nn.sigmoid(scaled)
            hidden[span, cols] = jnp.where(live, scaled * s, 0.0).astype(BF16)
            grad = grad_hidden[:, cols] * s * (1.0 + scaled * (1.0 - s))
            grad_scaled[span, cols] = grad
            head.append((jnp.sum(grad, axis=0, keepdims=True), jnp.sum(grad * norm, axis=0, keepdims=True)))
            embed(work, h, grad, first)
            tap_sums(sums.at[part], work[h, pl.ds(PAD, rows + PAD), :], buf, h, count, rows)
            sums[part, count : count + 1, cols] = jnp.zeros((1, LANES), F32)
        heads.append([a + b for a, b in zip(*head)])
    sums[0] = sums[0] + sums[1]
    sums[1] = ones_a[...] + ones_b[...]
    sums[2] = conv_sum_a[...] + conv_sum_b[...]
    (s0, q0), (s1, q1) = heads
    tile = jnp.concatenate([s0, s1, q0, q1, jnp.zeros((4, LANES), F32)], axis=0)
    pay[...] = jnp.broadcast_to(tile[None], pay.shape)
    for j in range(pay.shape[0]):
        for i in range(3):
            pay[j, 4 + i : 5 + i, :] = sums[i, j // 2 : j // 2 + 1, lanes(j % 2)]


def back_kernel(
    len_ref, half_ref, ends, got, params, stats, conv_a, conv_b, grad_scaled, value_a, value_b, sig_a, sig_b,
    taps, left, out_rows,
    own_pre, shift_grad, gain_grad, pay, work, grad_pre,
):
    rows, channels = conv_a.shape
    width = 2 * channels
    peers, rows_dev, _ = pay.shape
    total = params[2:3]
    sums = tree_sum(got[...])
    mean, inv_std = stats[0:1], stats[1:2]
    slices = []
    for h in range(channels // LANES):
        cols = lanes(h)
        s, q = sums[h : h + 1], sums[2 + h : 3 + h]
        shift_grad[:, cols] = s
        gain_grad[:, cols] = q
        scale = params[0:1, cols] * inv_std[:, cols]
        s, q = s / total[:, cols], q / total[:, cols]
        for part, (conv_out, value, sig) in enumerate(((conv_a, value_a, sig_a), (conv_b, value_b, sig_b))):
            masks = own_masks(len_ref, rows) if part == 0 else row_masks(ends[0:1], ends[1:2], rows)
            first, live = masks
            span = slice(part * rows, (part + 1) * rows)
            norm = (conv_out[:, cols] - mean[:, cols]) * inv_std[:, cols]
            grad = scale * (grad_scaled[span, cols] - s - norm * q)
            embed(work, h, jnp.where(live, grad, 0.0), first)
            glu = jnp.where(live, conv(work, h, taps, rows, first, -1), 0.0)
            v, g = value[:, cols], sig[:, cols]
            grad_pre[span, cols] = (glu * g).astype(BF16)
            grad_pre[span, channels + h * LANES : channels + (h + 1) * LANES] = (
                glu * v * g * (1.0 - g)
            ).astype(BF16)
        own, ones, cv = sums[4:5], sums[5:6], sums[6:7]
        slices.append(scale * (own - s * ones - q * inv_std[:, cols] * (cv - mean[:, cols] * ones)))
    own_pre[...] = grad_pre[:rows]
    which = jnp.full((1, LANES), half_ref[0], jnp.int32)
    depth = jnp.where(which == 0, slices[0], slices[1]).astype(BF16)
    total = jnp.dot(left[...], grad_pre[...], preferred_element_type=F32)
    pay[:, :, :width] = total.reshape(peers, rows_dev, width).astype(BF16)
    pay[:, :, width : width + channels] = out_rows[...]
    pay[:, :, width + channels :] = jnp.broadcast_to(depth[None], (peers, rows_dev, LANES))


def frame_kernel(mp_ref, grad_pre, proj, own, one, two, three):
    width = own.shape[1]
    groups = proj.shape[0] // width
    for d, out in enumerate((own, one, two, three)):
        at = pl.multiple_of(lax.rem(mp_ref[0] + d, groups) * width, width)
        term = lax.dot_general(grad_pre[...], proj[pl.ds(at, width), :], NT, preferred_element_type=F32)
        out[...] = term.astype(BF16)


def rows_kernel(left, right, out):
    out[...] = jnp.dot(left[...], right[...], preferred_element_type=F32).astype(BF16)


def last_kernel(got, in_rows, out_rows, depth):
    more = out_rows.shape[1]
    width = 2 * more
    for g in range(2):
        total = jnp.zeros((in_rows.shape[0], more), F32)
        for j in range(got.shape[0]):
            total = total + got[j, :, g * more : (g + 1) * more].astype(F32)
        in_rows[:, g, :] = total
    total = jnp.zeros((in_rows.shape[0], more), F32)
    for j in range(got.shape[0]):
        total = total + got[j, :, width : width + more].astype(F32)
    out_rows[...] = total
    for j in range(2 * depth.shape[0]):
        depth[j // 2 : j // 2 + 1, lanes(j % 2)] = got[j, 0:1, width + more :].astype(F32)


def core_rows(x, other, core):
    frames, width = x.shape
    halves = []
    for part in (x, other):
        rows = part.T.reshape(width // 16, 2, 8, frames)
        halves.append(lax.dynamic_index_in_dim(rows, core, 1, keepdims=False).reshape(width // 2, frames))
    return jnp.concatenate(halves, axis=1)


def swap_cores(x):
    return lax.ppermute(x, "core", [(0, 1), (1, 0)])


def after(x, y):
    return lax.optimization_barrier((x, y))[0]


def shards(frames, proj_in, taps, bn_gain, bn_shift, proj_out, grad_out, counts, lengths):
    rows, width = frames.shape
    channels = proj_in.shape[2]
    count = taps.shape[0]
    halves = channels // LANES
    buf_rows = rows + 3 * PAD
    peers = lax.axis_size(DP)
    chips = lax.axis_size(YZ)
    groups = lax.axis_size("mp")
    rows_dev = width // peers
    core = lax.axis_index("core")
    chip = lax.axis_index(YZ)
    mp = lax.axis_index("mp")
    full = shape((rows, channels))
    buf_shape = (halves, buf_rows, LANES)
    tap_shape = (count + 1, channels)
    wide = pltpu.VMEM((rows, 2 * channels), F32)
    square = pltpu.VMEM((rows, channels), F32)
    work = pltpu.VMEM(buf_shape, F32)
    proj = proj_in.reshape(width, 2 * channels)
    counts_row = counts.reshape(1, -1)
    gain_row = bn_gain.reshape(1, channels)
    shift_row = bn_shift.reshape(1, channels)

    conv_a, buf_a, pay = call(
        forward_kernel,
        (full, shape(buf_shape), hbm_shape((peers, 2, channels))),
        [SM, VM, VM, VM],
        [wide],
        name="forward",
    )(lengths, frames, proj, taps)
    got = lax.all_to_all(pay, DP, 0, 0)

    spans = jnp.pad(lengths.astype(BF16), ((0, 15), (0, width - lengths.shape[1])))
    given = swap_cores(after(jnp.concatenate([frames, grad_out, spans], axis=0), pay))
    value_a, sig_a, hid_a, ones_a, conv_sum_a, params = call(
        side_kernel,
        (
            hbm_shape((rows, channels)),
            hbm_shape((rows, channels)),
            full,
            shape(tap_shape),
            shape(tap_shape),
            shape((8, channels)),
        ),
        [SM, HB, HB, HB, HB, VM, VM, HB, HB, HB],
        [wide, square, work],
        name="side",
    )(lengths, frames, proj, grad_out, proj_out, conv_a, buf_a, gain_row, shift_row, counts_row)
    value_b, sig_b, hid_b, ones_b, conv_sum_b, conv_b, buf_b, ends = call(
        mirror_kernel,
        (
            hbm_shape((rows, channels)),
            hbm_shape((rows, channels)),
            full,
            shape(tap_shape),
            shape(tap_shape),
            full,
            shape(buf_shape),
            shape((8, LANES)),
        ),
        [HB, HB, HB, HB],
        [wide, square, work],
        name="mirror",
    )(given, proj, proj_out, taps)

    hidden, grad_scaled, stats, pay = call(
        norm_kernel,
        (
            shape((2 * rows, channels), BF16),
            shape((2 * rows, channels)),
            shape((2, channels)),
            hbm_shape((chips, 8, LANES)),
        ),
        [SM] + [VM] * 13,
        [work, pltpu.VMEM((3,) + tap_shape, F32)],
        name="norm",
    )(lengths, ends, got, params, conv_a, conv_b, hid_a, hid_b, buf_a, buf_b, ones_a, ones_b, conv_sum_a, conv_sum_b)
    got = lax.all_to_all(pay, YZ, 0, 0)

    given = after(given, pay)
    left_in = core_rows(frames, given[:rows], core)
    left_out = core_rows(grad_out, given[rows : 2 * rows], core)
    (out_rows,) = call(rows_kernel, (shape((width // 2, channels), BF16),), [HB, VM], name="out_rows")(
        left_out, hidden
    )
    got, out_rows, left_in = lax.optimization_barrier((got, out_rows, left_in))
    out_rows = out_rows.reshape(chips, rows_dev, channels)

    half = (chip % 2).astype(jnp.int32).reshape(1)
    grad_pre, shift_grad, gain_grad, pay = call(
        back_kernel,
        (
            shape((rows, 2 * channels), BF16),
            hbm_shape((1, channels)),
            hbm_shape((1, channels)),
            hbm_shape((chips, rows_dev, 3 * channels + LANES), BF16),
        ),
        [SM, SM] + [VM] * 14,
        [work, pltpu.VMEM((2 * rows, 2 * channels), BF16)],
        name="back",
    )(
        lengths, half, ends, got, params, stats, conv_a, conv_b, grad_scaled, value_a, value_b, sig_a, sig_b,
        taps, left_in, out_rows,
    )
    got = lax.all_to_all(pay, YZ, 0, 0)

    term = shape((rows, width // groups), BF16)
    own, one, two, three = call(frame_kernel, (term,) * 4, [SM, VM, HB], name="frame")(
        mp.astype(jnp.int32).reshape(1), grad_pre, proj
    )

    frame_sum = own.astype(F32)
    for d, part in ((1, one), (2, two), (3, three)):
        part = lax.ppermute(after(part, pay), "mp", [(i, (i + d) % groups) for i in range(groups)])
        frame_sum = frame_sum + part.astype(F32)
    frame_grad = frame_sum.astype(BF16)

    in_grad, out_grad, depth_grad = call(
        last_kernel,
        (hbm_shape((rows_dev, 2, channels)), hbm_shape((rows_dev, channels)), hbm_shape((count, channels))),
        [VM],
        name="last",
    )(got)
    return (frame_grad, in_grad, out_grad, depth_grad, gain_grad.reshape(channels), shift_grad.reshape(channels))


def solution(mesh):
    grid = Mesh(mesh.devices.reshape(8, 8, 2, 4), ("y", "z", "core", "mp"))
    placed = (
        P(DP, None),
        P(None, None, "mp"),
        P(None, "mp"),
        P("mp"),
        P("mp"),
        P(None, "mp"),
        P(DP, None),
        P(),
        P(DP, None),
    )
    return jax.shard_map(
        shards,
        mesh=grid,
        in_specs=placed,
        out_specs=(
            P(DP, "mp"),
            P(DP, None, "mp"),
            P(DP, "mp"),
            P(None, "mp"),
            P("mp"),
            P("mp"),
        ),
        check_vma=False,
    )
```

time: 111 us -> 109 us (0.982)
  Pallas kernels: 12.4 us -> 22.5 us
  starting transfers between devices: 49.9 us -> 41.4 us
  waiting for transfers between devices: 35.3 us -> 29.3 us
  other arithmetic: 0.73 us -> 2.75 us
    pallas_call x9 -> x8, Pallas kernels: 12.4 us -> 22.5 us  [run(): return kernel(*held)]
    ppermute x5 -> x1, starting transfers between devices: 10.2 us -> 1.91 us  [swap_cores(): return lax.ppermute(x, 'core', [(0, 1), (1, 0)])]
    all_to_all x1, waiting for transfers between devices: 11.6 us -> 4.4 us  [shards(): got = lax.all_to_all(pay, DP, 0, 0)]
    all_to_all x2, waiting for transfers between devices: 15.5 us -> 18.7 us  [shards(): got = lax.all_to_all(pay, YZ, 0, 0)]
    ppermute x5 -> x1, waiting for transfers between devices: 3.23 us -> 0.01 us  [swap_cores(): return lax.ppermute(x, 'core', [(0, 1), (1, 0)])]
    unnamed x47 -> x57, local copies, waits for them, and re-layouts: 9.47 us -> 6.28 us
    transpose x0 -> x3, local copies, waits for them, and re-layouts: none -> 2.48 us  [core_rows(): rows = part.T.reshape(width // 16, 2, 8, frames)]
    concatenate x0 -> x3, other arithmetic: none -> 2.02 us  [the longest x1 1.15 us: shards(): jnp.concatenate([frames, grad_out, spans], axis=0)]
  transfers between devices with their start and end apart: 11 -> 7, of which waited for: 8 -> 5; matrix products, arithmetic and copies ran while one was open for 2% -> 6% of each run, Pallas kernels for 3% -> 11%
where the time goes in v4:
time: 109 us; the launch traced here: 107 us
  starting transfers between devices  41.4 us (38%)
  waiting for transfers between devices  29.3 us (27%)
  Pallas kernels  22.5 us (21%)
  local copies, waits for them, and re-layouts  10.2 us (9%)
  other arithmetic  2.75 us (3%)
    pallas_call x8, Pallas kernels, run(): return kernel(*held)  22.5 us
    all_to_all x2, waiting for transfers between devices, shards(): got = lax.all_to_all(pay, YZ, 0, 0)  18.7 us
    all_to_all x1, starting transfers between devices, shards(): got = lax.all_to_all(pay, DP, 0, 0)  17.9 us
    all_to_all x2, starting transfers between devices, shards(): got = lax.all_to_all(pay, YZ, 0, 0)  13 us
    ppermute x3, starting transfers between devices, shards(): lax.ppermute(after(part, pay), 'mp', [(i, (i + d) % groups) for i in rang...  8.64 us
    unnamed x57, local copies, waits for them, and re-layouts  6.28 us
    ppermute x3, waiting for transfers between devices, shards(): lax.ppermute(after(part, pay), 'mp', [(i, (i + d) % groups) for i in rang...  6.14 us
    all_to_all x1, waiting for transfers between devices, shards(): got = lax.all_to_all(pay, DP, 0, 0)  4.4 us
  transfers between devices with their start and end apart: 7, of which 5 were waited for; matrix products, arithmetic and copies ran while one was open for 6% of the time, Pallas kernels for 11%

profile of v4, /device:TPU:6, one launch (start us, length us, event | category | flops | bytes accessed | tf_op | source)
XLA Modules:
  0.0 107.2 jit_solution(2034094264476364870)
XLA Ops:
  0.6 0.0 copy-start.26
  0.6 0.0 copy-start.14
  0.7 0.0 copy-start.1
  0.7 1.5 %copy.23 = bf16[128,8,2,256]{3,1,2,0:T(8,128)(2,1)S(1)} copy(bf16[128,8,2,256]{3,2,1,0:T(2,128)(2,1)} %bitcast.39) | data formatting | bytes 2097152
  2.2 0.0 copy-start.22
  2.2 2.7 %forward.1 = (f32[256,256]{1,0:T(8,128)S(1)}, f32[2,304,128]{2,1,0:T(8,128)S(1)}, f32[128,2,256]{2,1,0:T(2,128)}) custom-call(s32[1,2]{1,0:T(1,128)} %len_ref.7, bf16[256,1024]{1,0:T(8,128)(2,1)S(1)} %copy-done.1, bf16[1024,512]{1,0:T(8,128)(2,1)S(1)} %bitcast.30, f32[31,256]{1,0:T(8,128)S(1)} %copy-done.14), custom_call_target="tpu_custom_call" | custom-call | tf_op jit(solution)/shard_map/forward/pallas_call | solution.py:39
  5.0 1.1 %fusion.1 = bf16[528,1024]{1,0:T(8,128)(2,1)} fusion(bf16[1,2]{1,0:T(2,128)(2,1)S(1)} %convert_element_type.20, bf16[256,1024]{1,0:T(8,128)(2,1)S(1)} %copy-done.22, bf16[256,1024]{1,0:T(8,128)(2,1)S(1)} %copy-done.1), kind=kLoop, calls=%fused_computation.2 | loop fusion | flops 4325376 | bytes 2129924 | tf_op jit(solution)/shard_map/concatenate | solution.py:347
  6.1 1.9 %collective-permute-start = (bf16[528,1024]{1,0:T(8,128)(2,1)}, bf16[528,1024]{1,0:T(8,128)(2,1)}, u32[]{:S(2)}, u32[]{:S(2)}) collective-permute-start(bf16[528,1024]{1,0:T(8,128)(2,1)} %fusion.1), channel_id=1, source_target_pairs={{0,4},{4,0},{1,5},{5,1},{2,6},{6,2},{3,7},{7,3},{8,12},{12,8},{9,1... | collective-permute-start | bytes 3244040 | tf_op jit(solution)/shard_map/ppermute | solution.py:306
  8.0 17.9 %all-to-all-start = ((f32[128,2,256]{2,1,0:T(2,128)}), f32[128,2,256]{2,1,0:T(2,128)S(1)}, u32[]{:S(2)}, u32[]{:S(2)}) async-start(f32[128,2,256]{2,1,0:T(2,128)} %get-tuple-element.46), calls=%async_computation | async-start | bytes 524288 | tf_op jit(solution)/shard_map/all_to_all | solution.py:344
  26.0 0.2 copy.19
  26.2 0.2 copy.21
  26.4 4.2 %side.1 = (f32[256,256]{1,0:T(8,128)}, f32[256,256]{1,0:T(8,128)}, f32[256,256]{1,0:T(8,128)S(1)}, f32[32,256]{1,0:T(8,128)S(1)}, f32[32,256]{1,0:T(8,128)S(1)}, /*index=5*/f32[8,256]{1,0:T(8,128)S(1)}) custom-call(s32[1,2]{1,0:T(1,128)} %len_ref.7, bf16[256,1024]{1,0:T(8,128)(2,1)} %frames.3, bf16[1024,512]{1,0:T(8,128)(2,1)} %bitcast.31, ...), custom_call_target="tpu_custom_call" | custom-call | tf_op jit(solution)/shard_map/side/pallas_call | solution.py:39
  30.6 0.7 dynamic-slice_bitcast_fusion.3
  31.3 0.7 dynamic-slice_bitcast_fusion.1
  32.1 0.0 collective-permute-done.given
  32.1 4.6 %mirror.1 = (f32[256,256]{1,0:T(8,128)}, f32[256,256]{1,0:T(8,128)}, f32[256,256]{1,0:T(8,128)S(1)}, f32[32,256]{1,0:T(8,128)S(1)}, f32[32,256]{1,0:T(8,128)S(1)...) custom-call(bf16[528,1024]{1,0:T(8,128)(2,1)} %collective-permute-done.given, ...), custom_call_target="tpu_custom_call" | custom-call | tf_op jit(solution)/shard_map/mirror/pallas_call | solution.py:39
  36.7 4.4 %all-to-all-done.got = f32[128,2,256]{2,1,0:T(2,128)S(1)} async-done(((f32[128,2,256]{2,1,0:T(2,128)}), f32[128,2,256]{2,1,0:T(2,128)S(1)}, u32[]{:S(2)}, u32[]{:S(2)}) %all-to-all-start) | async-done | bytes 262176 | tf_op jit(solution)/shard_map/all_to_all | solution.py:344
  41.1 0.7 copy-done.8
  41.8 0.0 copy-done.5
  41.8 0.9 copy-done.9
  42.7 3.2 %norm.1 = (bf16[512,256]{1,0:T(8,128)(2,1)S(1)}, f32[512,256]{1,0:T(8,128)S(1)}, f32[2,256]{1,0:T(2,128)S(1)}, f32[64,8,128]{2,1,0:T(8,128)}) custom-call(s32[1,2]{1,0:T(1,128)} %len_ref.7, f32[8,128]{1,0:T(8,128)S(1)} %get-tuple-element.48.ends, f32[128,2,256]{2,1,0:T(2,128)S(1)} %copy-done.9, f32[8,256]{1,0:T(8,128)S(1)} %get-tuple-element.51.params, ...), custom_call_target="tpu_custom_call" | custom-call | tf_op jit(solution)/shard_map/norm/pallas_call | solution.py:39
  46.0 8.3 %all-to-all-start.1 = ((f32[64,8,128]{2,1,0:T(8,128)}), f32[64,8,128]{2,1,0:T(8,128)S(1)}, u32[]{:S(2)}, u32[]{:S(2)}) async-start(f32[64,8,128]{2,1,0:T(8,128)} %get-tuple-element.60), calls=%async_computation.1 | async-start | bytes 524288 | tf_op jit(solution)/shard_map/all_to_all | solution.py:391
  54.3 1.3 %slice_bitcast_fusion = (bf16[1024,256]{0,1:T(8,128)(2,1)S(1)}, bf16[1024,256]{0,1:T(8,128)(2,1)S(1)}) fusion(bf16[528,1024]{1,0:T(8,128)(2,1)} %collective-permute-done.given), kind=kLoop, calls=%fused_computation.5 | loop fusion | bytes 2097152 | tf_op jit(solution)/shard_map/transpose | solution.py:300
  55.6 0.2 copy.20
  55.8 1.0 copy.22
  56.8 0.0 copy-done.25
  56.8 0.0 copy-start.23
  56.9 0.0 copy-start.24
  56.9 0.8 pad_maximum_fusion.left
  57.7 0.0 copy-start.15
  57.8 1.4 %out_rows.1 = bf16[512,256]{1,0:T(8,128)(2,1)S(1)} custom-call(bf16[512,512]{1,0:T(8,128)(2,1)} %pad_maximum_fusion.left, bf16[512,256]{1,0:T(8,128)(2,1)S(1)} %copy-done.21), custom_call_target="tpu_custom_call" | custom-call | tf_op jit(solution)/shard_map/out_rows/pallas_call | solution.py:39
  59.3 10.0 %all-to-all-done.1.got = f32[64,8,128]{2,1,0:T(8,128)S(1)} async-done(((f32[64,8,128]{2,1,0:T(8,128)}), f32[64,8,128]{2,1,0:T(8,128)S(1)}, u32[]{:S(2)}, u32[]{:S(2)}) %all-to-all-start.1) | async-done | bytes 262176 | tf_op jit(solution)/shard_map/all_to_all | solution.py:391
  69.4 0.7 copy-done.10
  70.1 0.0 copy-done.7
  70.1 0.9 copy-done.11
  71.1 0.9 copy-done.16
  72.0 3.8 %back.1 = (bf16[256,512]{1,0:T(8,128)(2,1)S(1)}, f32[1,256]{1,0:T(1,128)}, f32[1,256]{1,0:T(1,128)}, bf16[64,8,896]{2,1,0:T(8,128)(2,1)}) custom-call(s32[1,2]{1,0:T(1,128)} %len_ref.7, s32[1]{0:T(128)} %bitcast.1.half_ref, f32[8,128]{1,0:T(8,128)S(1)} %get-tuple-element.48.ends, f32[64,8,128]{2,1,0:T(8,128)S(1)} %copy-done.11, ...), custom_call_target="tpu_custom_call" | custom-call | tf_op jit(solution)/shard_map/back/pallas_call | solution.py:39
  75.8 4.6 %all-to-all-start.2 = ((bf16[64,8,896]{2,1,0:T(8,128)(2,1)}), bf16[64,8,896]{2,1,0:T(8,128)(2,1)S(1)}, u32[]{:S(2)}, u32[]{:S(2)}) async-start(bf16[64,8,896]{2,1,0:T(8,128)(2,1)} %get-tuple-element.75), calls=%async_computation.2 | async-start | bytes 1835008 | tf_op jit(solution)/shard_map/all_to_all | solution.py:418
  80.5 1.7 %frame.1 = (bf16[256,256]{1,0:T(8,128)(2,1)S(1)}, bf16[256,256]{1,0:T(8,128)(2,1)S(1)}, bf16[256,256]{1,0:T(8,128)(2,1)S(1)}, bf16[256,256]{1,0:T(8,128)(2,1)S(1)}) custom-call(s32[1]{0:T(128)} %bitcast.mp_ref, bf16[256,512]{1,0:T(8,128)(2,1)S(1)} %get-tuple-element.72.grad_pre, bf16[1024,512]{1,0:T(8,128)(2,1)} %bitcast.33), custom_call_target="tpu_custom_call" | custom-call | tf_op jit(solution)/shard_map/frame/pallas_call | solution.py:39
  82.2 2.4 %collective-permute-start.1 = (bf16[256,256]{1,0:T(8,128)(2,1)S(1)}, bf16[256,256]{1,0:T(8,128)(2,1)S(1)}, u32[]{:S(2)}, u32[]{:S(2)}) collective-permute-start(bf16[256,256]{1,0:T(8,128)(2,1)S(1)} %get-tuple-element.76), channel_id=1, source_target_pairs={{0,1},{1,2},{2,3},{3,0},{4,5},{5,6},{6,7},{7,4},{8,9},{9,10},{10,1... | collective-permute-start | bytes 393224 | tf_op jit(solution)/shard_map/ppermute | solution.py:427
  84.6 4.3 %collective-permute-start.2 = (bf16[256,256]{1,0:T(8,128)(2,1)S(1)}, bf16[256,256]{1,0:T(8,128)(2,1)S(1)}, u32[]{:S(2)}, u32[]{:S(2)}) collective-permute-start(bf16[256,256]{1,0:T(8,128)(2,1)S(1)} %get-tuple-element.78), channel_id=1, source_target_pairs={{0,2},{1,3},{2,0},{3,1},{4,6},{5,7},{6,4},{7,5},{8,10},{9,11},{10,... | collective-permute-start | bytes 393224 | tf_op jit(solution)/shard_map/ppermute | solution.py:427
  88.9 1.9 %collective-permute-start.3 = (bf16[256,256]{1,0:T(8,128)(2,1)S(1)}, bf16[256,256]{1,0:T(8,128)(2,1)S(1)}, u32[]{:S(2)}, u32[]{:S(2)}) collective-permute-start(bf16[256,256]{1,0:T(8,128)(2,1)S(1)} %get-tuple-element.80), channel_id=1, source_target_pairs={{0,3},{1,0},{2,1},{3,2},{4,7},{5,4},{6,5},{7,6},{8,11},{9,8},{10,9... | collective-permute-start | bytes 393224 | tf_op jit(solution)/shard_map/ppermute | solution.py:427
  90.8 0.0 collective-permute-done.1
  90.9 2.4 %collective-permute-done.2 = bf16[256,256]{1,0:T(8,128)(2,1)S(1)} collective-permute-done((bf16[256,256]{1,0:T(8,128)(2,1)S(1)}, bf16[256,256]{1,0:T(8,128)(2,1)S(1)}, u32[]{:S(2)}, u32[]{:S(2)}) %collective-permute-start.2) | collective-permute-done | bytes 131104 | tf_op jit(solution)/shard_map/ppermute | solution.py:427
  93.2 3.8 %collective-permute-done.3 = bf16[256,256]{1,0:T(8,128)(2,1)S(1)} collective-permute-done((bf16[256,256]{1,0:T(8,128)(2,1)S(1)}, bf16[256,256]{1,0:T(8,128)(2,1)S(1)}, u32[]{:S(2)}, u32[]{:S(2)}) %collective-permute-start.3) | collective-permute-done | bytes 131104 | tf_op jit(solution)/shard_map/ppermute | solution.py:427
  97.0 0.7 add_convert_fusion
  97.7 8.7 %all-to-all-done.2.got = bf16[64,8,896]{2,1,0:T(8,128)(2,1)S(1)} async-done(((bf16[64,8,896]{2,1,0:T(8,128)(2,1)}), bf16[64,8,896]{2,1,0:T(8,128)(2,1)S(1)}, u32[]{:S(2)}, u32[]{:S(2)}) %all-to-all-start.2) | async-done | bytes 917536 | tf_op jit(solution)/shard_map/all_to_all | solution.py:418
  106.4 0.8 last.1
  (43 shorter events, 0.2 us)
Async XLA Ops:
  0.6 1.6 %copy-start.26 = (s32[1,2]{1,0:T(1,128)S(1)}, s32[1,2]{1,0:T(1,128)}, u32[]{:S(2)}) copy-start(s32[1,2]{1,0:T(1,128)} %len_ref.7) | copy-start | bytes 28
  0.6 1.6 %copy-start.14 = (f32[31,256]{1,0:T(8,128)S(1)}, f32[31,256]{1,0:T(8,128)}, u32[]{:S(2)}) copy-start(f32[31,256]{1,0:T(8,128)} %taps.5) | copy-start | bytes 95236
  0.7 1.6 %copy-start.1 = (bf16[256,1024]{1,0:T(8,128)(2,1)S(1)}, bf16[256,1024]{1,0:T(8,128)(2,1)}, u32[]{:S(2)}) copy-start(bf16[256,1024]{1,0:T(8,128)(2,1)} %frames.3) | copy-start | bytes 1572868
  2.2 3.9 %copy-start = (bf16[128,8,2,256]{3,1,2,0:T(8,128)(2,1)}, bf16[128,8,2,256]{3,1,2,0:T(8,128)(2,1)S(1)}, u32[]{:S(2)}) copy-start(bf16[128,8,2,256]{3,1,2,0:T(8,128)(2,1)S(1)} %copy.23) | copy-start | bytes 3145732
  2.2 2.8 %copy-start.22 = (bf16[256,1024]{1,0:T(8,128)(2,1)S(1)}, bf16[256,1024]{1,0:T(8,128)(2,1)}, u32[]{:S(2)}) copy-start(bf16[256,1024]{1,0:T(8,128)(2,1)} %grad_out.1) | copy-start | bytes 1572868
  5.0 21.4 %copy-start.4 = (f32[2,304,128]{2,1,0:T(8,128)}, f32[2,304,128]{2,1,0:T(8,128)S(1)}, u32[]{:S(2)}) copy-start(f32[2,304,128]{2,1,0:T(8,128)S(1)} %get-tuple-element.50.buf.buf_a) | copy-start | bytes 933892
  5.0 36.8 %copy-start.2 = (f32[256,256]{1,0:T(8,128)}, f32[256,256]{1,0:T(8,128)S(1)}, u32[]{:S(2)}) copy-start(f32[256,256]{1,0:T(8,128)S(1)} %get-tuple-element.49.conv_out.conv_a) | copy-start | bytes 786436
  6.1 25.9 %collective-permute-start = (bf16[528,1024]{1,0:T(8,128)(2,1)}, bf16[528,1024]{1,0:T(8,128)(2,1)}, u32[]{:S(2)}, u32[]{:S(2)}) collective-permute-start(bf16[528,1024]{1,0:T(8,128)(2,1)} %fusion.1), channel_id=1, source_target_pairs={{0,4},{4,0},{1,5},{5,1},{2,6},{6,2},{3,7},{7,3},{8,12},{12,8},{9,1... | collective-permute-start | bytes 3244040 | tf_op jit(solution)/shard_map/ppermute | solution.py:306
  8.0 33.0 %all-to-all-start = ((f32[128,2,256]{2,1,0:T(2,128)}), f32[128,2,256]{2,1,0:T(2,128)S(1)}, u32[]{:S(2)}, u32[]{:S(2)}) async-start(f32[128,2,256]{2,1,0:T(2,128)} %get-tuple-element.46), calls=%async_computation | async-start | bytes 524288 | tf_op jit(solution)/shard_map/all_to_all | solution.py:344
  32.1 9.7 %copy-start.5 = (f32[2,304,128]{2,1,0:T(8,128)S(1)}, f32[2,304,128]{2,1,0:T(8,128)}, u32[]{:S(2)}) copy-start(f32[2,304,128]{2,1,0:T(8,128)} %copy-done.4) | copy-start | bytes 933892
  36.7 9.3 %copy-start.6 = (f32[256,256]{1,0:T(8,128)}, f32[256,256]{1,0:T(8,128)S(1)}, u32[]{:S(2)}) copy-start(f32[256,256]{1,0:T(8,128)S(1)} %get-tuple-element.52.conv_b) | copy-start | bytes 786436
  41.1 0.7 copy-start.8
  41.8 1.0 copy-start.9
  46.0 9.6 %copy-start.12 = (f32[512,256]{1,0:T(8,128)}, f32[512,256]{1,0:T(8,128)S(1)}, u32[]{:S(2)}) copy-start(f32[512,256]{1,0:T(8,128)S(1)} %get-tuple-element.65.grad_scaled) | copy-start | bytes 1572868
  46.0 9.6 %copy-start.20 = (bf16[512,256]{1,0:T(8,128)(2,1)}, bf16[512,256]{1,0:T(8,128)(2,1)S(1)}, u32[]{:S(2)}) copy-start(bf16[512,256]{1,0:T(8,128)(2,1)S(1)} %get-tuple-element.62.right) | copy-start | bytes 786436
  46.0 23.4 %all-to-all-start.1 = ((f32[64,8,128]{2,1,0:T(8,128)}), f32[64,8,128]{2,1,0:T(8,128)S(1)}, u32[]{:S(2)}, u32[]{:S(2)}) async-start(f32[64,8,128]{2,1,0:T(8,128)} %get-tuple-element.60), calls=%async_computation.1 | async-start | bytes 524288 | tf_op jit(solution)/shard_map/all_to_all | solution.py:391
  55.6 1.3 %copy-start.25 = (bf16[512,256]{1,0:T(8,128)(2,1)S(1)}, bf16[512,256]{1,0:T(8,128)(2,1)}, u32[]{:S(2)}) copy-start(bf16[512,256]{1,0:T(8,128)(2,1)} %dynamic-slice_bitcast_fusion.3) | copy-start | bytes 786436
  55.8 1.9 %copy-start.21 = (bf16[512,256]{1,0:T(8,128)(2,1)S(1)}, bf16[512,256]{1,0:T(8,128)(2,1)}, u32[]{:S(2)}) copy-start(bf16[512,256]{1,0:T(8,128)(2,1)} %copy-done.20) | copy-start | bytes 786436
  56.8 2.4 %copy-start.23 = (bf16[1024,256]{1,0:T(8,128)(2,1)S(1)}, bf16[1024,256]{1,0:T(8,128)(2,1)}, u32[]{:S(2)}) copy-start(bf16[1024,256]{1,0:T(8,128)(2,1)} %copy.22) | copy-start | bytes 1572868
  56.9 2.4 %copy-start.24 = (bf16[512,256]{1,0:T(8,128)(2,1)S(1)}, bf16[512,256]{1,0:T(8,128)(2,1)}, u32[]{:S(2)}) copy-start(bf16[512,256]{1,0:T(8,128)(2,1)} %dynamic-slice_bitcast_fusion.1) | copy-start | bytes 786436
  57.7 12.3 %copy-start.3 = (f32[256,256]{1,0:T(8,128)S(1)}, f32[256,256]{1,0:T(8,128)}, u32[]{:S(2)}) copy-start(f32[256,256]{1,0:T(8,128)} %copy-done.2) | copy-start | bytes 786436
  57.7 12.3 %copy-start.7 = (f32[256,256]{1,0:T(8,128)S(1)}, f32[256,256]{1,0:T(8,128)}, u32[]{:S(2)}) copy-start(f32[256,256]{1,0:T(8,128)} %copy-done.6) | copy-start | bytes 786436
  57.7 12.4 %copy-start.13 = (f32[512,256]{1,0:T(8,128)S(1)}, f32[512,256]{1,0:T(8,128)}, u32[]{:S(2)}) copy-start(f32[512,256]{1,0:T(8,128)} %copy-done.12) | copy-start | bytes 1572868
  57.7 12.3 %copy-start.15 = (f32[31,256]{1,0:T(8,128)S(1)}, f32[31,256]{1,0:T(8,128)}, u32[]{:S(2)}) copy-start(f32[31,256]{1,0:T(8,128)} %taps.5) | copy-start | bytes 95236
  57.7 12.3 %copy-start.17 = (f32[256,256]{1,0:T(8,128)S(1)}, f32[256,256]{1,0:T(8,128)}, u32[]{:S(2)}) copy-start(f32[256,256]{1,0:T(8,128)} %get-tuple-element.68.sig_a) | copy-start | bytes 786436
  57.7 12.3 %copy-start.19 = (f32[256,256]{1,0:T(8,128)S(1)}, f32[256,256]{1,0:T(8,128)}, u32[]{:S(2)}) copy-start(f32[256,256]{1,0:T(8,128)} %get-tuple-element.69.sig_b) | copy-start | bytes 786436
  59.2 10.9 %copy-start.18 = (f32[256,256]{1,0:T(8,128)S(1)}, f32[256,256]{1,0:T(8,128)}, u32[]{:S(2)}) copy-start(f32[256,256]{1,0:T(8,128)} %get-tuple-element.67.value_b) | copy-start | bytes 786436
  69.4 0.7 copy-start.10
  70.1 1.0 copy-start.11
  71.1 0.9 copy-start.16
  75.8 30.6 %all-to-all-start.2 = ((bf16[64,8,896]{2,1,0:T(8,128)(2,1)}), bf16[64,8,896]{2,1,0:T(8,128)(2,1)S(1)}, u32[]{:S(2)}, u32[]{:S(2)}) async-start(bf16[64,8,896]{2,1,0:T(8,128)(2,1)} %get-tuple-element.75), calls=%async_computation.2 | async-start | bytes 1835008 | tf_op jit(solution)/shard_map/all_to_all | solution.py:418
  82.2 8.7 %collective-permute-start.1 = (bf16[256,256]{1,0:T(8,128)(2,1)S(1)}, bf16[256,256]{1,0:T(8,128)(2,1)S(1)}, u32[]{:S(2)}, u32[]{:S(2)}) collective-permute-start(bf16[256,256]{1,0:T(8,128)(2,1)S(1)} %get-tuple-element.76), channel_id=1, source_target_pairs={{0,1},{1,2},{2,3},{3,0},{4,5},{5,6},{6,7},{7,4},{8,9},{9,10},{10,1... | collective-permute-start | bytes 393224 | tf_op jit(solution)/shard_map/ppermute | solution.py:427
  84.6 8.6 %collective-permute-start.2 = (bf16[256,256]{1,0:T(8,128)(2,1)S(1)}, bf16[256,256]{1,0:T(8,128)(2,1)S(1)}, u32[]{:S(2)}, u32[]{:S(2)}) collective-permute-start(bf16[256,256]{1,0:T(8,128)(2,1)S(1)} %get-tuple-element.78), channel_id=1, source_target_pairs={{0,2},{1,3},{2,0},{3,1},{4,6},{5,7},{6,4},{7,5},{8,10},{9,11},{10,... | collective-permute-start | bytes 393224 | tf_op jit(solution)/shard_map/ppermute | solution.py:427
  88.9 8.1 %collective-permute-start.3 = (bf16[256,256]{1,0:T(8,128)(2,1)S(1)}, bf16[256,256]{1,0:T(8,128)(2,1)S(1)}, u32[]{:S(2)}, u32[]{:S(2)}) collective-permute-start(bf16[256,256]{1,0:T(8,128)(2,1)S(1)} %get-tuple-element.80), channel_id=1, source_target_pairs={{0,3},{1,0},{2,1},{3,2},{4,7},{5,4},{6,5},{7,6},{8,11},{9,8},{10,9... | collective-permute-start | bytes 393224 | tf_op jit(solution)/shard_map/ppermute | solution.py:427

commit v5 on v4

--- a/solution.py
+++ b/solution.py
@@ -1,11 +1,10 @@
-import functools
-
 import jax
 import jax.numpy as jnp
 from jax import lax
 from jax.experimental import pallas as pl
 from jax.experimental.pallas import tpu as pltpu
 from jax.sharding import Mesh, PartitionSpec as P
+
 
 BLOCK = 128
 DP = ("y", "z", "core")
@@ -17,18 +16,14 @@
 BF16 = jnp.bfloat16
 VM = pl.BlockSpec(memory_space=pltpu.VMEM)
 HB = pl.BlockSpec(memory_space=pltpu.VMEM)
+AN = pl.BlockSpec(memory_space=pl.ANY)
 SM = pl.BlockSpec(memory_space=pltpu.SMEM)
 NT = (((1,), (1,)), ((), ()))
 
 
-def call(body, outs, ins, scratch=(), name=None):
+def call(body, outs, ins, scratch=()):
     kernel = pl.pallas_call(
-        body,
-        out_shape=outs,
-        in_specs=ins,
-        out_specs=tuple(VM for _ in outs),
-        scratch_shapes=list(scratch),
-        name=name,
+        body, out_shape=outs, in_specs=ins, out_specs=tuple(VM for _ in outs), scratch_shapes=list(scratch)
     )
 
     def run(*args):
@@ -98,6 +93,23 @@
     for k in range(count):
         prod = values * buf[h, pl.ds(PAD + k - radius, span), :]
         out[k : k + 1, lanes(h)] = jnp.sum(prod, axis=0, keepdims=True)
+
+
+def fetches(sources, targets, sems):
+    copies = [pltpu.make_async_copy(a, b, sems.at[i]) for i, (a, b) in enumerate(zip(sources, targets))]
+    for copy in copies:
+        copy.start()
+    return copies
+
+
+def batch_norm(conv_out, mean, inv_std, params, cols):
+    norm = (conv_out[:, cols] - mean[:, cols]) * inv_std[:, cols]
+    scaled = norm * params[0:1, cols] + params[1:2, cols]
+    return norm, scaled, jax.nn.sigmoid(scaled)
+
+
+def swish_slope(scaled, s):
+    return s * (1.0 + scaled * (1.0 - s))
 
 
 def gated(pre, live, h, channels):
@@ -181,38 +193,38 @@
 def norm_kernel(
     len_ref, ends, got, params, conv_a, conv_b, hid_a, hid_b, buf_a, buf_b,
     ones_a, ones_b, conv_sum_a, conv_sum_b,
-    hidden, grad_scaled, stats, pay, work, sums,
+    hidden, stats, pay, work, sums, hids, bufs, sems,
 ):
     rows, channels = conv_a.shape
     count = TAPS
+    copies = fetches((hid_a, hid_b, buf_a, buf_b), (hids.at[0], hids.at[1], bufs.at[0], bufs.at[1]), sems)
     total = params[2:3]
     found = tree_sum(got[...])
     mean = found[0:1] / total
     inv_std = lax.rsqrt(found[1:2] / total - mean * mean + 1e-05)
     stats[0:1] = mean
     stats[1:2] = inv_std
+    sums[1] = ones_a[...] + ones_b[...]
+    sums[2] = conv_sum_a[...] + conv_sum_b[...]
+    for copy in copies:
+        copy.wait()
     heads = []
     for h in range(channels // LANES):
         cols = lanes(h)
         head = []
-        for part, (conv_out, grad_hidden, buf) in enumerate(((conv_a, hid_a, buf_a), (conv_b, hid_b, buf_b))):
+        for part, conv_out in enumerate((conv_a, conv_b)):
             masks = own_masks(len_ref, rows) if part == 0 else row_masks(ends[0:1], ends[1:2], rows)
             first, live = masks
-            span = slice(part * rows, (part + 1) * rows)
-            norm = (conv_out[:, cols] - mean[:, cols]) * inv_std[:, cols]
-            scaled = norm * params[0:1, cols] + params[1:2, cols]
-            s = jax.nn.sigmoid(scaled)
-            hidden[span, cols] = jnp.where(live, scaled * s, 0.0).astype(BF16)
-            grad = grad_hidden[:, cols] * s * (1.0 + scaled * (1.0 - s))
-            grad_scaled[span, cols] = grad
+            norm, scaled, s = batch_norm(conv_out, mean, inv_std, params, cols)
+            hidden[part * rows : (part + 1) * rows, cols] = jnp.where(live, scaled * s, 0.0).astype(BF16)
+            grad = hids[part, :, cols] * swish_slope(scaled, s)
             head.append((jnp.sum(grad, axis=0, keepdims=True), jnp.sum(grad * norm, axis=0, keepdims=True)))
             embed(work, h, grad, first)
-            tap_sums(sums.at[part], work[h, pl.ds(PAD, rows + PAD), :], buf, h, count, rows)
-            sums[part, count : count + 1, cols] = jnp.zeros((1, LANES), F32)
+            out = sums.at[0] if part == 0 else sums.at[3]
+            tap_sums(out, work[h, pl.ds(PAD, rows + PAD), :], bufs.at[part], h, count, rows)
+            out[count : count + 1, cols] = jnp.zeros((1, LANES), F32)
         heads.append([a + b for a, b in zip(*head)])
-    sums[0] = sums[0] + sums[1]
-    sums[1] = ones_a[...] + ones_b[...]
-    sums[2] = conv_sum_a[...] + conv_sum_b[...]
+    sums[0] = sums[0] + sums[3]
     (s0, q0), (s1, q1) = heads
     tile = jnp.concatenate([s0, s1, q0, q1, jnp.zeros((4, LANES), F32)], axis=0)
     pay[...] = jnp.broadcast_to(tile[None], pay.shape)
@@ -222,16 +234,23 @@
 
 
 def back_kernel(
-    len_ref, half_ref, ends, got, params, stats, conv_a, conv_b, grad_scaled, value_a, value_b, sig_a, sig_b,
-    taps, left, out_rows,
-    own_pre, shift_grad, gain_grad, pay, work, grad_pre,
+    len_ref, half_ref, ends, got, params, stats, conv_a, conv_b, taps,
+    hid_a, hid_b, value_a, value_b, sig_a, sig_b, left_in, rows_in,
+    own_pre, shift_grad, gain_grad, pay, work, grad_pre, hids, values, sigs, left, out_rows, sems,
 ):
     rows, channels = conv_a.shape
     width = 2 * channels
     peers, rows_dev, _ = pay.shape
+    copies = fetches(
+        (hid_a, hid_b, value_a, value_b, sig_a, sig_b, left_in, rows_in),
+        (hids.at[0], hids.at[1], values.at[0], values.at[1], sigs.at[0], sigs.at[1], left, out_rows),
+        sems,
+    )
     total = params[2:3]
     sums = tree_sum(got[...])
     mean, inv_std = stats[0:1], stats[1:2]
+    copies[0].wait()
+    copies[1].wait()
     slices = []
     for h in range(channels // LANES):
         cols = lanes(h)
@@ -240,15 +259,18 @@
         gain_grad[:, cols] = q
         scale = params[0:1, cols] * inv_std[:, cols]
         s, q = s / total[:, cols], q / total[:, cols]
-        for part, (conv_out, value, sig) in enumerate(((conv_a, value_a, sig_a), (conv_b, value_b, sig_b))):
+        for part, conv_out in enumerate((conv_a, conv_b)):
             masks = own_masks(len_ref, rows) if part == 0 else row_masks(ends[0:1], ends[1:2], rows)
             first, live = masks
             span = slice(part * rows, (part + 1) * rows)
-            norm = (conv_out[:, cols] - mean[:, cols]) * inv_std[:, cols]
-            grad = scale * (grad_scaled[span, cols] - s - norm * q)
+            norm, scaled, swish = batch_norm(conv_out, mean, inv_std, params, cols)
+            grad = scale * (hids[part, :, cols] * swish_slope(scaled, swish) - s - norm * q)
             embed(work, h, jnp.where(live, grad, 0.0), first)
             glu = jnp.where(live, conv(work, h, taps, rows, first, -1), 0.0)
-            v, g = value[:, cols], sig[:, cols]
+            if h == 0:
+                copies[2 + part].wait()
+                copies[4 + part].wait()
+            v, g = values[part, :, cols], sigs[part, :, cols]
             grad_pre[span, cols] = (glu * g).astype(BF16)
             grad_pre[span, channels + h * LANES : channels + (h + 1) * LANES] = (
                 glu * v * g * (1.0 - g)
@@ -258,6 +280,8 @@
     own_pre[...] = grad_pre[:rows]
     which = jnp.full((1, LANES), half_ref[0], jnp.int32)
     depth = jnp.where(which == 0, slices[0], slices[1]).astype(BF16)
+    copies[6].wait()
+    copies[7].wait()
     total = jnp.dot(left[...], grad_pre[...], preferred_element_type=F32)
     pay[:, :, :width] = total.reshape(peers, rows_dev, width).astype(BF16)
     pay[:, :, width : width + channels] = out_rows[...]
@@ -335,67 +359,64 @@
     shift_row = bn_shift.reshape(1, channels)
 
     conv_a, buf_a, pay = call(
-        forward_kernel,
-        (full, shape(buf_shape), hbm_shape((peers, 2, channels))),
-        [SM, VM, VM, VM],
-        [wide],
-        name="forward",
+        forward_kernel, (full, shape(buf_shape), hbm_shape((peers, 2, channels))), [SM, VM, VM, VM], [wide]
     )(lengths, frames, proj, taps)
     got = lax.all_to_all(pay, DP, 0, 0)
 
     spans = jnp.pad(lengths.astype(BF16), ((0, 15), (0, width - lengths.shape[1])))
-    given = swap_cores(after(jnp.concatenate([frames, grad_out, spans], axis=0), pay))
+    given = after(jnp.concatenate([frames, grad_out, spans], axis=0), pay)
+    given = swap_cores(given)
     value_a, sig_a, hid_a, ones_a, conv_sum_a, params = call(
         side_kernel,
         (
             hbm_shape((rows, channels)),
             hbm_shape((rows, channels)),
-            full,
+            hbm_shape((rows, channels)),
             shape(tap_shape),
             shape(tap_shape),
             shape((8, channels)),
         ),
         [SM, HB, HB, HB, HB, VM, VM, HB, HB, HB],
         [wide, square, work],
-        name="side",
     )(lengths, frames, proj, grad_out, proj_out, conv_a, buf_a, gain_row, shift_row, counts_row)
     value_b, sig_b, hid_b, ones_b, conv_sum_b, conv_b, buf_b, ends = call(
         mirror_kernel,
         (
             hbm_shape((rows, channels)),
             hbm_shape((rows, channels)),
-            full,
+            hbm_shape((rows, channels)),
             shape(tap_shape),
             shape(tap_shape),
             full,
-            shape(buf_shape),
+            hbm_shape(buf_shape),
             shape((8, LANES)),
         ),
         [HB, HB, HB, HB],
         [wide, square, work],
-        name="mirror",
     )(given, proj, proj_out, taps)
 
-    hidden, grad_scaled, stats, pay = call(
+    hidden, stats, pay = call(
         norm_kernel,
         (
             shape((2 * rows, channels), BF16),
-            shape((2 * rows, channels)),
             shape((2, channels)),
             hbm_shape((chips, 8, LANES)),
         ),
-        [SM] + [VM] * 13,
-        [work, pltpu.VMEM((3,) + tap_shape, F32)],
-        name="norm",
+        [SM] + [VM] * 5 + [AN] * 4 + [VM] * 4,
+        [
+            work,
+            pltpu.VMEM((4,) + tap_shape, F32),
+            pltpu.VMEM((2, rows, channels), F32),
+            pltpu.VMEM((2,) + buf_shape, F32),
+            pltpu.SemaphoreType.DMA((4,)),
+        ],
     )(lengths, ends, got, params, conv_a, conv_b, hid_a, hid_b, buf_a, buf_b, ones_a, ones_b, conv_sum_a, conv_sum_b)
     got = lax.all_to_all(pay, YZ, 0, 0)
 
-    given = after(given, pay)
+    given, frames, grad_out, _ = lax.optimization_barrier((given, frames, grad_out, pay))
     left_in = core_rows(frames, given[:rows], core)
     left_out = core_rows(grad_out, given[rows : 2 * rows], core)
-    (out_rows,) = call(rows_kernel, (shape((width // 2, channels), BF16),), [HB, VM], name="out_rows")(
-        left_out, hidden
-    )
+    (out_rows,) = call(rows_kernel, (hbm_shape((width // 2, channels), BF16),), [HB, VM])(left_out, hidden)
     got, out_rows, left_in = lax.optimization_barrier((got, out_rows, left_in))
     out_rows = out_rows.reshape(chips, rows_dev, channels)
 
@@ -408,17 +429,25 @@
             hbm_shape((1, channels)),
             hbm_shape((chips, rows_dev, 3 * channels + LANES), BF16),
         ),
-        [SM, SM] + [VM] * 14,
-        [work, pltpu.VMEM((2 * rows, 2 * channels), BF16)],
-        name="back",
+        [SM, SM] + [VM] * 7 + [AN] * 8,
+        [
+            work,
+            pltpu.VMEM((2 * rows, 2 * channels), BF16),
+            pltpu.VMEM((2, rows, channels), F32),
+            pltpu.VMEM((2, rows, channels), F32),
+            pltpu.VMEM((2, rows, channels), F32),
+            pltpu.VMEM((width // 2, 2 * rows), BF16),
+            pltpu.VMEM((chips, rows_dev, channels), BF16),
+            pltpu.SemaphoreType.DMA((8,)),
+        ],
     )(
-        lengths, half, ends, got, params, stats, conv_a, conv_b, grad_scaled, value_a, value_b, sig_a, sig_b,
-        taps, left_in, out_rows,
+        lengths, half, ends, got, params, stats, conv_a, conv_b, taps,
+        hid_a, hid_b, value_a, value_b, sig_a, sig_b, left_in, out_rows,
     )
     got = lax.all_to_all(pay, YZ, 0, 0)
 
     term = shape((rows, width // groups), BF16)
-    own, one, two, three = call(frame_kernel, (term,) * 4, [SM, VM, HB], name="frame")(
+    own, one, two, three = call(frame_kernel, (term,) * 4, [SM, VM, HB])(
         mp.astype(jnp.int32).reshape(1), grad_pre, proj
     )
 
@@ -432,7 +461,6 @@
         last_kernel,
         (hbm_shape((rows_dev, 2, channels)), hbm_shape((rows_dev, channels)), hbm_shape((count, channels))),
         [VM],
-        name="last",
     )(got)
     return (frame_grad, in_grad, out_grad, depth_grad, gain_grad.reshape(channels), shift_grad.reshape(channels))
 

time: 109 us -> 108 us (level)
  local copies, waits for them, and re-layouts: 10.2 us -> 5.74 us
  Pallas kernels: 22.5 us -> 26.7 us
  waiting for transfers between devices: 29.3 us -> 27.9 us
    pallas_call x8, Pallas kernels: 22.5 us -> 26.7 us  [run(): return kernel(*held)]
    unnamed x57 -> x27, local copies, waits for them, and re-layouts: 6.28 us -> 3.19 us
    all_to_all x2, waiting for transfers between devices: 18.7 us -> 17.3 us  [shards(): got = lax.all_to_all(pay, YZ, 0, 0)]
    reshape x4 -> x2, local copies, waits for them, and re-layouts: 1.48 us -> 0.08 us  [core_rows(): lax.dynamic_index_in_dim(rows, core, 1, keepdims=False)]
  transfers between devices with their start and end apart: 7 -> 7, of which waited for: 5 -> 5; matrix products, arithmetic and copies ran while one was open for 6% -> 5% of each run, Pallas kernels for 11% -> 13%
where the time goes in v5:
time: 108 us; the launch traced here: 106 us
  starting transfers between devices  41.4 us (38%)
  waiting for transfers between devices  27.9 us (26%)
  Pallas kernels  26.7 us (25%)
  local copies, waits for them, and re-layouts  5.74 us (5%)
  other arithmetic  3.53 us (3%)
    pallas_call x8, Pallas kernels, run(): return kernel(*held)  26.7 us
    all_to_all x1, starting transfers between devices, shards(): got = lax.all_to_all(pay, DP, 0, 0)  17.9 us
    all_to_all x2, waiting for transfers between devices, shards(): got = lax.all_to_all(pay, YZ, 0, 0)  17.3 us
    all_to_all x2, starting transfers between devices, shards(): got = lax.all_to_all(pay, YZ, 0, 0)  12.9 us
    ppermute x3, starting transfers between devices, shards(): lax.ppermute(after(part, pay), 'mp', [(i, (i + d) % groups) for i in rang...  8.64 us
    ppermute x3, waiting for transfers between devices, shards(): lax.ppermute(after(part, pay), 'mp', [(i, (i + d) % groups) for i in rang...  6.14 us
    all_to_all x1, waiting for transfers between devices, shards(): got = lax.all_to_all(pay, DP, 0, 0)  4.44 us
    unnamed x27, local copies, waits for them, and re-layouts  3.19 us
  transfers between devices with their start and end apart: 7, of which 5 were waited for; matrix products, arithmetic and copies ran while one was open for 5% of the time, Pallas kernels for 13%

profile of v5, /device:TPU:6, one launch (start us, length us, event | category | flops | bytes accessed | tf_op | source)
XLA Modules:
  0.0 106.1 jit_solution(4035162534663734069)
XLA Ops:
  0.6 0.0 copy-start.12
  0.6 0.0 copy-start.4
  0.7 0.0 copy-start.1
  0.7 1.5 %copy.23 = bf16[128,8,2,256]{3,1,2,0:T(8,128)(2,1)S(1)} copy(bf16[128,8,2,256]{3,2,1,0:T(2,128)(2,1)} %bitcast.38) | data formatting | bytes 2097152
  2.2 0.0 copy-done.12
  2.2 0.0 copy-start
  2.2 0.0 copy-start.6
  2.2 0.0 copy-done.4
  2.2 0.0 copy-done.1
  2.2 2.8 %shard_map.136 = (f32[256,256]{1,0:T(8,128)S(1)}, f32[2,304,128]{2,1,0:T(8,128)S(1)}, f32[128,2,256]{2,1,0:T(2,128)}) custom-call(s32[1,2]{1,0:T(1,128)} %len_ref.7, bf16[256,1024]{1,0:T(8,128)(2,1)S(1)} %copy-done.1, bf16[1024,512]{1,0:T(8,128)(2,1)S(1)} %bitcast.30, f32[31,256]{1,0:T(8,128)S(1)} %copy-done.4), custom_call_target="tpu_custom_call" | custom-call | tf_op jit(solution)/shard_map/pallas_call | solution.py:34
  5.0 0.0 copy-done.6
  5.0 1.1 %fusion.1 = bf16[528,1024]{1,0:T(8,128)(2,1)} fusion(bf16[1,2]{1,0:T(2,128)(2,1)S(1)} %convert_element_type.20, bf16[256,1024]{1,0:T(8,128)(2,1)S(1)} %copy-done.6, bf16[256,1024]{1,0:T(8,128)(2,1)S(1)} %copy-done.1), kind=kLoop, calls=%fused_computation.2 | loop fusion | flops 4325376 | bytes 2129924 | tf_op jit(solution)/shard_map/concatenate | solution.py:367
  6.1 0.0 copy-done
  6.1 1.9 %collective-permute-start = (bf16[528,1024]{1,0:T(8,128)(2,1)}, bf16[528,1024]{1,0:T(8,128)(2,1)S(1)}, u32[]{:S(2)}, u32[]{:S(2)}) collective-permute-start(bf16[528,1024]{1,0:T(8,128)(2,1)} %fusion.1), channel_id=1, source_target_pairs={{0,4},{4,0},{1,5},{5,1},{2,6},{6,2},{3,7},{7,3},{8,12},{12,8},{9,1... | collective-permute-start | bytes 3244040 | tf_op jit(solution)/shard_map/ppermute | solution.py:330
  8.1 17.9 %all-to-all-start = ((f32[128,2,256]{2,1,0:T(2,128)}), f32[128,2,256]{2,1,0:T(2,128)S(1)}, u32[]{:S(2)}, u32[]{:S(2)}) async-start(f32[128,2,256]{2,1,0:T(2,128)} %get-tuple-element.47), calls=%async_computation | async-start | bytes 524288 | tf_op jit(solution)/shard_map/all_to_all | solution.py:364
  26.0 0.0 copy-done.3
  26.0 4.6 %shard_map.138 = (f32[256,256]{1,0:T(8,128)}, f32[256,256]{1,0:T(8,128)}, f32[256,256]{1,0:T(8,128)}, f32[32,256]{1,0:T(8,128)S(1)}, f32[32,256]{1,0:T(8,128)S(1)}, /*index=5*/f32[8,256]{1,0:T(8,128)S(1)}) custom-call(s32[1,2]{1,0:T(1,128)} %len_ref.7, bf16[256,1024]{1,0:T(8,128)(2,1)} %frames.3, bf16[1024,512]{1,0:T(8,128)(2,1)} %bitcast.31, ...), custom_call_target="tpu_custom_call" | custom-call | tf_op jit(solution)/shard_map/pallas_call | solution.py:34
  30.6 0.0 collective-permute-done.given
  30.6 1.0 copy-done.8
  31.6 5.1 %shard_map.137 = (f32[256,256]{1,0:T(8,128)}, f32[256,256]{1,0:T(8,128)}, f32[256,256]{1,0:T(8,128)}, f32[32,256]{1,0:T(8,128)S(1)}, f32[32,256]{1,0:T(8,128)S(1...) custom-call(bf16[528,1024]{1,0:T(8,128)(2,1)} %copy-done.8, bf16[1024,512]{1,0:T(8,128)(2,1)} %bitcast.32, ...), custom_call_target="tpu_custom_call" | custom-call | tf_op jit(solution)/shard_map/pallas_call | solution.py:34
  36.6 4.4 %all-to-all-done.got = f32[128,2,256]{2,1,0:T(2,128)S(1)} async-done(((f32[128,2,256]{2,1,0:T(2,128)}), f32[128,2,256]{2,1,0:T(2,128)S(1)}, u32[]{:S(2)}, u32[]{:S(2)}) %all-to-all-start) | async-done | bytes 262176 | tf_op jit(solution)/shard_map/all_to_all | solution.py:364
  41.1 4.6 %shard_map.139 = (bf16[512,256]{1,0:T(8,128)(2,1)S(1)}, f32[2,256]{1,0:T(2,128)S(1)}, f32[64,8,128]{2,1,0:T(8,128)}) custom-call(s32[1,2]{1,0:T(1,128)} %len_ref.7, f32[8,128]{1,0:T(8,128)S(1)} %get-tuple-element.49.ends, f32[128,2,256]{2,1,0:T(2,128)S(1)} %all-to-all-done.got, f32[8,256]{1,0:T(8,128)S(1)} %get-tuple-element.52.params, ...), custom_call_target="tpu_custom_call" | custom-call | tf_op jit(solution)/shard_map/pallas_call | solution.py:34
  45.7 8.3 %all-to-all-start.1 = ((f32[64,8,128]{2,1,0:T(8,128)}), f32[64,8,128]{2,1,0:T(8,128)S(1)}, u32[]{:S(2)}, u32[]{:S(2)}) async-start(f32[64,8,128]{2,1,0:T(8,128)} %get-tuple-element.61), calls=%async_computation.1 | async-start | bytes 524288 | tf_op jit(solution)/shard_map/all_to_all | solution.py:414
  53.9 0.0 copy-done.9
  53.9 0.0 copy-start.2
  54.0 0.9 slice_bitcast_fusion
  54.8 1.0 copy.22
  55.8 0.2 copy.21
  56.0 0.2 copy.20
  56.3 0.6 copy-done.7
  56.9 0.2 copy.19
  57.2 0.8 pad_maximum_fusion.left
  58.0 2.1 %shard_map.140 = bf16[512,256]{1,0:T(8,128)(2,1)} custom-call(bf16[512,512]{1,0:T(8,128)(2,1)} %pad_maximum_fusion.left, bf16[512,256]{1,0:T(8,128)(2,1)S(1)} %get-tuple-element.64.right), custom_call_target="tpu_custom_call" | custom-call | tf_op jit(solution)/shard_map/pallas_call | solution.py:34
  60.1 0.9 pad_maximum_fusion.1.left_in
  61.0 8.0 %all-to-all-done.1.got = f32[64,8,128]{2,1,0:T(8,128)S(1)} async-done(((f32[64,8,128]{2,1,0:T(8,128)}), f32[64,8,128]{2,1,0:T(8,128)S(1)}, u32[]{:S(2)}, u32[]{:S(2)}) %all-to-all-start.1) | async-done | bytes 262176 | tf_op jit(solution)/shard_map/all_to_all | solution.py:414
  69.0 0.0 copy-done.5
  69.0 5.2 %shard_map.141 = (bf16[256,512]{1,0:T(8,128)(2,1)S(1)}, f32[1,256]{1,0:T(1,128)}, f32[1,256]{1,0:T(1,128)}, bf16[64,8,896]{2,1,0:T(8,128)(2,1)}) custom-call(s32[1,2]{1,0:T(1,128)} %len_ref.7, s32[1]{0:T(128)} %bitcast.1.half_ref, f32[8,128]{1,0:T(8,128)S(1)} %get-tuple-element.49.ends, f32[64,8,128]{2,1,0:T(8,128)S(1)} %all-to-all-done.1.got, ...), custom_call_target="tpu_custom_call" | custom-call | tf_op jit(solution)/shard_map/pallas_call | solution.py:34
  74.2 4.7 %all-to-all-start.2 = ((bf16[64,8,896]{2,1,0:T(8,128)(2,1)}), bf16[64,8,896]{2,1,0:T(8,128)(2,1)S(1)}, u32[]{:S(2)}, u32[]{:S(2)}) async-start(bf16[64,8,896]{2,1,0:T(8,128)(2,1)} %get-tuple-element.77), calls=%async_computation.2 | async-start | bytes 1835008 | tf_op jit(solution)/shard_map/all_to_all | solution.py:447
  78.9 1.7 %shard_map.142 = (bf16[256,256]{1,0:T(8,128)(2,1)S(1)}, bf16[256,256]{1,0:T(8,128)(2,1)S(1)}, bf16[256,256]{1,0:T(8,128)(2,1)S(1)}, bf16[256,256]{1,0:T(8,128)(2,1)S(1)}) custom-call(s32[1]{0:T(128)} %bitcast.mp_ref, bf16[256,512]{1,0:T(8,128)(2,1)S(1)} %get-tuple-element.74.grad_pre, bf16[1024,512]{1,0:T(8,128)(2,1)} %bitcast.33), custom_call_target="tpu_custom_call" | custom-call | tf_op jit(solution)/shard_map/pallas_call | solution.py:34
  80.6 2.4 %collective-permute-start.1 = (bf16[256,256]{1,0:T(8,128)(2,1)S(1)}, bf16[256,256]{1,0:T(8,128)(2,1)S(1)}, u32[]{:S(2)}, u32[]{:S(2)}) collective-permute-start(bf16[256,256]{1,0:T(8,128)(2,1)S(1)} %get-tuple-element.78), channel_id=1, source_target_pairs={{0,1},{1,2},{2,3},{3,0},{4,5},{5,6},{6,7},{7,4},{8,9},{9,10},{10,1... | collective-permute-start | bytes 393224 | tf_op jit(solution)/shard_map/ppermute | solution.py:456
  83.0 4.3 %collective-permute-start.2 = (bf16[256,256]{1,0:T(8,128)(2,1)S(1)}, bf16[256,256]{1,0:T(8,128)(2,1)S(1)}, u32[]{:S(2)}, u32[]{:S(2)}) collective-permute-start(bf16[256,256]{1,0:T(8,128)(2,1)S(1)} %get-tuple-element.80), channel_id=1, source_target_pairs={{0,2},{1,3},{2,0},{3,1},{4,6},{5,7},{6,4},{7,5},{8,10},{9,11},{10,... | collective-permute-start | bytes 393224 | tf_op jit(solution)/shard_map/ppermute | solution.py:456
  87.3 1.9 %collective-permute-start.3 = (bf16[256,256]{1,0:T(8,128)(2,1)S(1)}, bf16[256,256]{1,0:T(8,128)(2,1)S(1)}, u32[]{:S(2)}, u32[]{:S(2)}) collective-permute-start(bf16[256,256]{1,0:T(8,128)(2,1)S(1)} %get-tuple-element.82), channel_id=1, source_target_pairs={{0,3},{1,0},{2,1},{3,2},{4,7},{5,4},{6,5},{7,6},{8,11},{9,8},{10,9... | collective-permute-start | bytes 393224 | tf_op jit(solution)/shard_map/ppermute | solution.py:456
  89.2 0.0 collective-permute-done.1
  89.3 2.1 %collective-permute-done.2 = bf16[256,256]{1,0:T(8,128)(2,1)S(1)} collective-permute-done((bf16[256,256]{1,0:T(8,128)(2,1)S(1)}, bf16[256,256]{1,0:T(8,128)(2,1)S(1)}, u32[]{:S(2)}, u32[]{:S(2)}) %collective-permute-start.2) | collective-permute-done | bytes 131104 | tf_op jit(solution)/shard_map/ppermute | solution.py:456
  91.3 4.0 %collective-permute-done.3 = bf16[256,256]{1,0:T(8,128)(2,1)S(1)} collective-permute-done((bf16[256,256]{1,0:T(8,128)(2,1)S(1)}, bf16[256,256]{1,0:T(8,128)(2,1)S(1)}, u32[]{:S(2)}, u32[]{:S(2)}) %collective-permute-start.3) | collective-permute-done | bytes 131104 | tf_op jit(solution)/shard_map/ppermute | solution.py:456
  95.4 0.7 add_convert_fusion
  96.1 9.2 %all-to-all-done.2.got = bf16[64,8,896]{2,1,0:T(8,128)(2,1)S(1)} async-done(((bf16[64,8,896]{2,1,0:T(8,128)(2,1)}), bf16[64,8,896]{2,1,0:T(8,128)(2,1)S(1)}, u32[]{:S(2)}, u32[]{:S(2)}) %all-to-all-start.2) | async-done | bytes 917536 | tf_op jit(solution)/shard_map/all_to_all | solution.py:447
  105.4 0.8 shard_map.143
  (13 shorter events, 0.1 us)
Async XLA Ops:
  0.6 1.6 %copy-start.12 = (s32[1,2]{1,0:T(1,128)S(1)}, s32[1,2]{1,0:T(1,128)}, u32[]{:S(2)}) copy-start(s32[1,2]{1,0:T(1,128)} %len_ref.7) | copy-start | bytes 28
  0.6 1.6 %copy-start.4 = (f32[31,256]{1,0:T(8,128)S(1)}, f32[31,256]{1,0:T(8,128)}, u32[]{:S(2)}) copy-start(f32[31,256]{1,0:T(8,128)} %taps.5) | copy-start | bytes 95236
  0.7 1.6 %copy-start.1 = (bf16[256,1024]{1,0:T(8,128)(2,1)S(1)}, bf16[256,1024]{1,0:T(8,128)(2,1)}, u32[]{:S(2)}) copy-start(bf16[256,1024]{1,0:T(8,128)(2,1)} %frames.3) | copy-start | bytes 1572868
  2.2 3.9 %copy-start = (bf16[128,8,2,256]{3,1,2,0:T(8,128)(2,1)}, bf16[128,8,2,256]{3,1,2,0:T(8,128)(2,1)S(1)}, u32[]{:S(2)}) copy-start(bf16[128,8,2,256]{3,1,2,0:T(8,128)(2,1)S(1)} %copy.23) | copy-start | bytes 3145732
  2.2 2.8 %copy-start.6 = (bf16[256,1024]{1,0:T(8,128)(2,1)S(1)}, bf16[256,1024]{1,0:T(8,128)(2,1)}, u32[]{:S(2)}) copy-start(bf16[256,1024]{1,0:T(8,128)(2,1)} %grad_out.1) | copy-start | bytes 1572868
  5.0 21.0 %copy-start.3 = (f32[2,304,128]{2,1,0:T(8,128)}, f32[2,304,128]{2,1,0:T(8,128)S(1)}, u32[]{:S(2)}) copy-start(f32[2,304,128]{2,1,0:T(8,128)S(1)} %get-tuple-element.51.buf.buf_a) | copy-start | bytes 933892
  6.1 24.4 %collective-permute-start = (bf16[528,1024]{1,0:T(8,128)(2,1)}, bf16[528,1024]{1,0:T(8,128)(2,1)S(1)}, u32[]{:S(2)}, u32[]{:S(2)}) collective-permute-start(bf16[528,1024]{1,0:T(8,128)(2,1)} %fusion.1), channel_id=1, source_target_pairs={{0,4},{4,0},{1,5},{5,1},{2,6},{6,2},{3,7},{7,3},{8,12},{12,8},{9,1... | collective-permute-start | bytes 3244040 | tf_op jit(solution)/shard_map/ppermute | solution.py:330
  8.1 33.0 %all-to-all-start = ((f32[128,2,256]{2,1,0:T(2,128)}), f32[128,2,256]{2,1,0:T(2,128)S(1)}, u32[]{:S(2)}, u32[]{:S(2)}) async-start(f32[128,2,256]{2,1,0:T(2,128)} %get-tuple-element.47), calls=%async_computation | async-start | bytes 524288 | tf_op jit(solution)/shard_map/all_to_all | solution.py:364
  30.6 1.0 copy-start.8
  41.1 12.9 %copy-start.9 = (bf16[528,1024]{1,0:T(8,128)(2,1)S(1)}, bf16[528,1024]{1,0:T(8,128)(2,1)}, u32[]{:S(2)}) copy-start(bf16[528,1024]{1,0:T(8,128)(2,1)} %copy-done.8) | copy-start | bytes 3244036
  45.7 23.3 %all-to-all-start.1 = ((f32[64,8,128]{2,1,0:T(8,128)}), f32[64,8,128]{2,1,0:T(8,128)S(1)}, u32[]{:S(2)}, u32[]{:S(2)}) async-start(f32[64,8,128]{2,1,0:T(8,128)} %get-tuple-element.61), calls=%async_computation.1 | async-start | bytes 524288 | tf_op jit(solution)/shard_map/all_to_all | solution.py:414
  53.9 1.9 %copy-start.2 = (bf16[256,1024]{1,0:T(8,128)(2,1)S(1)}, bf16[256,1024]{1,0:T(8,128)(2,1)}, u32[]{:S(2)}) copy-start(bf16[256,1024]{1,0:T(8,128)(2,1)} %frames.3) | copy-start | bytes 1572868
  54.8 1.2 %copy-start.10 = (bf16[1024,256]{0,1:T(8,128)(2,1)S(1)}, bf16[1024,256]{0,1:T(8,128)(2,1)}, u32[]{:S(2)}) copy-start(bf16[1024,256]{0,1:T(8,128)(2,1)} %get-tuple-element.89) | copy-start | bytes 1572868
  55.8 1.1 %copy-start.7 = (bf16[256,1024]{1,0:T(8,128)(2,1)S(1)}, bf16[256,1024]{1,0:T(8,128)(2,1)}, u32[]{:S(2)}) copy-start(bf16[256,1024]{1,0:T(8,128)(2,1)} %grad_out.1) | copy-start | bytes 1572868
  57.1 2.9 %copy-start.11 = (bf16[1024,256]{1,0:T(8,128)(2,1)S(1)}, bf16[1024,256]{1,0:T(8,128)(2,1)}, u32[]{:S(2)}) copy-start(bf16[1024,256]{1,0:T(8,128)(2,1)} %copy.22) | copy-start | bytes 1572868
  60.1 8.9 %copy-start.5 = (f32[31,256]{1,0:T(8,128)S(1)}, f32[31,256]{1,0:T(8,128)}, u32[]{:S(2)}) copy-start(f32[31,256]{1,0:T(8,128)} %taps.5) | copy-start | bytes 95236
  74.2 31.2 %all-to-all-start.2 = ((bf16[64,8,896]{2,1,0:T(8,128)(2,1)}), bf16[64,8,896]{2,1,0:T(8,128)(2,1)S(1)}, u32[]{:S(2)}, u32[]{:S(2)}) async-start(bf16[64,8,896]{2,1,0:T(8,128)(2,1)} %get-tuple-element.77), calls=%async_computation.2 | async-start | bytes 1835008 | tf_op jit(solution)/shard_map/all_to_all | solution.py:447
  80.6 8.7 %collective-permute-start.1 = (bf16[256,256]{1,0:T(8,128)(2,1)S(1)}, bf16[256,256]{1,0:T(8,128)(2,1)S(1)}, u32[]{:S(2)}, u32[]{:S(2)}) collective-permute-start(bf16[256,256]{1,0:T(8,128)(2,1)S(1)} %get-tuple-element.78), channel_id=1, source_target_pairs={{0,1},{1,2},{2,3},{3,0},{4,5},{5,6},{6,7},{7,4},{8,9},{9,10},{10,1... | collective-permute-start | bytes 393224 | tf_op jit(solution)/shard_map/ppermute | solution.py:456
  83.0 8.4 %collective-permute-start.2 = (bf16[256,256]{1,0:T(8,128)(2,1)S(1)}, bf16[256,256]{1,0:T(8,128)(2,1)S(1)}, u32[]{:S(2)}, u32[]{:S(2)}) collective-permute-start(bf16[256,256]{1,0:T(8,128)(2,1)S(1)} %get-tuple-element.80), channel_id=1, source_target_pairs={{0,2},{1,3},{2,0},{3,1},{4,6},{5,7},{6,4},{7,5},{8,10},{9,11},{10,... | collective-permute-start | bytes 393224 | tf_op jit(solution)/shard_map/ppermute | solution.py:456
  87.3 8.1 %collective-permute-start.3 = (bf16[256,256]{1,0:T(8,128)(2,1)S(1)}, bf16[256,256]{1,0:T(8,128)(2,1)S(1)}, u32[]{:S(2)}, u32[]{:S(2)}) collective-permute-start(bf16[256,256]{1,0:T(8,128)(2,1)S(1)} %get-tuple-element.82), channel_id=1, source_target_pairs={{0,3},{1,0},{2,1},{3,2},{4,7},{5,4},{6,5},{7,6},{8,11},{9,8},{10,9... | collective-permute-start | bytes 393224 | tf_op jit(solution)/shard_map/ppermute | solution.py:456

commit v6 on v5

--- a/solution.py
+++ b/solution.py
@@ -137,14 +137,13 @@
     pay[...] = jnp.broadcast_to(both[None], pay.shape)
 
 
-def known_sums(ones_sum, conv_sum, conv_out, buf, work, h, rows, first, live):
-    count = TAPS
-    embed(work, h, jnp.where(live, 1.0, 0.0), first)
-    tap_sums(ones_sum, work[h, pl.ds(PAD, rows + PAD), :], buf, h, count, rows)
-    embed(work, h, conv_out[:, lanes(h)], first)
-    tap_sums(conv_sum, work[h, pl.ds(PAD, rows + PAD), :], buf, h, count, rows)
-    ones_sum[count : count + 1, lanes(h)] = jnp.zeros((1, LANES), F32)
-    conv_sum[count : count + 1, lanes(h)] = jnp.zeros((1, LANES), F32)
+def live_taps(split, end, rows):
+    dims = (TAPS + 1, rows + 3 * PAD)
+    tap = lax.broadcasted_iota(jnp.int32, dims, 0)
+    at = lax.broadcasted_iota(jnp.int32, dims, 1) - tap + TAPS // 2
+    one = (at >= PAD) & (at < PAD + split)
+    two = (at >= 2 * PAD + split) & (at < 2 * PAD + end)
+    return jnp.where(one | two, 1.0, 0.0).astype(BF16)
 
 
 def side_kernel(
@@ -153,13 +152,17 @@
 ):
     rows, channels = conv_out.shape
     first, live = own_masks(len_ref, rows)
+    marks = live_taps(len_ref[0, 0], len_ref[0, 0] + len_ref[0, 1], rows)
     pre[...] = jnp.dot(frames[...], proj[...], preferred_element_type=F32)
     hid[...] = jnp.dot(grad_out[...], proj_out[...], preferred_element_type=F32)
     for h in range(channels // LANES):
         cols = lanes(h)
         value[:, cols], sig[:, cols], _ = gated(pre, live, h, channels)
         grad_hidden[:, cols] = jnp.where(live, hid[:, cols], 0.0)
-        known_sums(ones_sum, conv_sum, conv_out, buf, work, h, rows, first, live)
+        ones_sum[:, cols] = jnp.dot(marks, buf[h].astype(BF16), preferred_element_type=F32)
+        embed(work, h, conv_out[:, cols], first)
+        tap_sums(conv_sum, work[h, pl.ds(PAD, rows + PAD), :], buf, h, TAPS, rows)
+        conv_sum[TAPS : TAPS + 1, cols] = jnp.zeros((1, LANES), F32)
     total = jnp.sum(counts[...].astype(F32), axis=1, keepdims=True) * BLOCK
     params[0:1] = gain[...]
     params[1:2] = shift[...]
@@ -168,8 +171,8 @@
 
 
 def mirror_kernel(
-    given, proj, proj_out, taps,
-    value, sig, grad_hidden, ones_sum, conv_sum, conv_out, buf, ends, pre, hid, work,
+    given, proj, proj_out, taps, stats, params,
+    value, sig, grad_hidden, conv_out, hidden, ends, pre, hid, buf,
 ):
     rows, channels = conv_out.shape
     spans = given[2 * rows : 2 * rows + 16, :LANES].astype(F32)[0:1]
@@ -179,6 +182,7 @@
     ends[1:2] = jnp.broadcast_to(end, (1, LANES))
     ends[2:] = jnp.zeros((6, LANES), F32)
     first, live = row_masks(ends[0:1], ends[1:2], rows)
+    mean, inv_std = stats[0:1], stats[1:2]
     pre[...] = jnp.dot(given[:rows], proj[...], preferred_element_type=F32)
     hid[...] = jnp.dot(given[rows : 2 * rows], proj_out[...], preferred_element_type=F32)
     for h in range(channels // LANES):
@@ -187,63 +191,69 @@
         embed(buf, h, glu, first)
         conv_out[:, cols] = jnp.where(live, conv(buf, h, taps, rows, first, 1), 0.0)
         grad_hidden[:, cols] = jnp.where(live, hid[:, cols], 0.0)
-        known_sums(ones_sum, conv_sum, conv_out, buf, work, h, rows, first, live)
+        _, scaled, s = batch_norm(conv_out, mean, inv_std, params, cols)
+        hidden[:, cols] = jnp.where(live, scaled * s, 0.0).astype(BF16)
 
 
 def norm_kernel(
-    len_ref, ends, got, params, conv_a, conv_b, hid_a, hid_b, buf_a, buf_b,
-    ones_a, ones_b, conv_sum_a, conv_sum_b,
-    hidden, stats, pay, work, sums, hids, bufs, sems,
+    len_ref, got, params, conv_out, grad_hidden, buf, ones_sum, conv_sum,
+    hidden, stats, sums, work,
 ):
-    rows, channels = conv_a.shape
+    rows, channels = conv_out.shape
     count = TAPS
-    copies = fetches((hid_a, hid_b, buf_a, buf_b), (hids.at[0], hids.at[1], bufs.at[0], bufs.at[1]), sems)
+    first, live = own_masks(len_ref, rows)
     total = params[2:3]
     found = tree_sum(got[...])
     mean = found[0:1] / total
     inv_std = lax.rsqrt(found[1:2] / total - mean * mean + 1e-05)
     stats[0:1] = mean
     stats[1:2] = inv_std
-    sums[1] = ones_a[...] + ones_b[...]
-    sums[2] = conv_sum_a[...] + conv_sum_b[...]
-    for copy in copies:
-        copy.wait()
-    heads = []
+    base = 3 * (count + 1)
+    sums[count + 1 : 2 * (count + 1)] = ones_sum[...]
+    sums[2 * (count + 1) : base] = conv_sum[...]
+    sums[base + 2 :] = jnp.zeros((6, channels), F32)
     for h in range(channels // LANES):
         cols = lanes(h)
-        head = []
-        for part, conv_out in enumerate((conv_a, conv_b)):
-            masks = own_masks(len_ref, rows) if part == 0 else row_masks(ends[0:1], ends[1:2], rows)
-            first, live = masks
-            norm, scaled, s = batch_norm(conv_out, mean, inv_std, params, cols)
-            hidden[part * rows : (part + 1) * rows, cols] = jnp.where(live, scaled * s, 0.0).astype(BF16)
-            grad = hids[part, :, cols] * swish_slope(scaled, s)
-            head.append((jnp.sum(grad, axis=0, keepdims=True), jnp.sum(grad * norm, axis=0, keepdims=True)))
-            embed(work, h, grad, first)
-            out = sums.at[0] if part == 0 else sums.at[3]
-            tap_sums(out, work[h, pl.ds(PAD, rows + PAD), :], bufs.at[part], h, count, rows)
-            out[count : count + 1, cols] = jnp.zeros((1, LANES), F32)
-        heads.append([a + b for a, b in zip(*head)])
-    sums[0] = sums[0] + sums[3]
-    (s0, q0), (s1, q1) = heads
-    tile = jnp.concatenate([s0, s1, q0, q1, jnp.zeros((4, LANES), F32)], axis=0)
+        norm, scaled, s = batch_norm(conv_out, mean, inv_std, params, cols)
+        hidden[:, cols] = jnp.where(live, scaled * s, 0.0).astype(BF16)
+        grad = grad_hidden[:, cols] * swish_slope(scaled, s)
+        sums[base : base + 1, cols] = jnp.sum(grad, axis=0, keepdims=True)
+        sums[base + 1 : base + 2, cols] = jnp.sum(grad * norm, axis=0, keepdims=True)
+        embed(work, h, grad, first)
+        tap_sums(sums, work[h, pl.ds(PAD, rows + PAD), :], buf, h, count, rows)
+        sums[count : count + 1, cols] = jnp.zeros((1, LANES), F32)
+
+
+def spread_kernel(own, other, pay, sums):
+    sums[...] = own[...] + other[...]
+    count = pay.shape[0] // 2
+    base = 3 * count
+    tile = jnp.concatenate(
+        [sums[base + i : base + i + 1, lanes(h)] for i in range(2) for h in range(2)]
+        + [jnp.zeros((4, LANES), F32)],
+        axis=0,
+    )
     pay[...] = jnp.broadcast_to(tile[None], pay.shape)
     for j in range(pay.shape[0]):
         for i in range(3):
-            pay[j, 4 + i : 5 + i, :] = sums[i, j // 2 : j // 2 + 1, lanes(j % 2)]
+            at = i * count + j // 2
+            pay[j, 4 + i : 5 + i, :] = sums[at : at + 1, lanes(j % 2)]
 
 
 def back_kernel(
     len_ref, half_ref, ends, got, params, stats, conv_a, conv_b, taps,
-    hid_a, hid_b, value_a, value_b, sig_a, sig_b, left_in, rows_in,
+    hid_a, hid_b, value_a, value_b, sig_a, sig_b, left_a, left_b, rows_in,
     own_pre, shift_grad, gain_grad, pay, work, grad_pre, hids, values, sigs, left, out_rows, sems,
 ):
     rows, channels = conv_a.shape
     width = 2 * channels
     peers, rows_dev, _ = pay.shape
     copies = fetches(
-        (hid_a, hid_b, value_a, value_b, sig_a, sig_b, left_in, rows_in),
-        (hids.at[0], hids.at[1], values.at[0], values.at[1], sigs.at[0], sigs.at[1], left, out_rows),
+        (hid_a, hid_b, value_a, value_b, sig_a, sig_b, left_a, left_b, rows_in),
+        (
+            hids.at[0], hids.at[1], values.at[0], values.at[1], sigs.at[0], sigs.at[1],
+            left.at[0], left.at[1], out_rows,
+        ),
         sems,
     )
     total = params[2:3]
@@ -280,9 +290,10 @@
     own_pre[...] = grad_pre[:rows]
     which = jnp.full((1, LANES), half_ref[0], jnp.int32)
     depth = jnp.where(which == 0, slices[0], slices[1]).astype(BF16)
-    copies[6].wait()
-    copies[7].wait()
-    total = jnp.dot(left[...], grad_pre[...], preferred_element_type=F32)
+    for copy in copies[6:]:
+        copy.wait()
+    total = jnp.dot(left[0], grad_pre[:rows], preferred_element_type=F32)
+    total = total + jnp.dot(left[1], grad_pre[rows:], preferred_element_type=F32)
     pay[:, :, :width] = total.reshape(peers, rows_dev, width).astype(BF16)
     pay[:, :, width : width + channels] = out_rows[...]
     pay[:, :, width + channels :] = jnp.broadcast_to(depth[None], (peers, rows_dev, LANES))
@@ -297,8 +308,10 @@
         out[...] = term.astype(BF16)
 
 
-def rows_kernel(left, right, out):
-    out[...] = jnp.dot(left[...], right[...], preferred_element_type=F32).astype(BF16)
+def rows_kernel(left_a, left_b, right_a, right_b, out):
+    total = jnp.dot(left_a[...], right_a[...], preferred_element_type=F32)
+    total = total + jnp.dot(left_b[...], right_b[...], preferred_element_type=F32)
+    out[...] = total.astype(BF16)
 
 
 def last_kernel(got, in_rows, out_rows, depth):
@@ -317,13 +330,10 @@
         depth[j // 2 : j // 2 + 1, lanes(j % 2)] = got[j, 0:1, width + more :].astype(F32)
 
 
-def core_rows(x, other, core):
+def core_rows(x, core):
     frames, width = x.shape
-    halves = []
-    for part in (x, other):
-        rows = part.T.reshape(width // 16, 2, 8, frames)
-        halves.append(lax.dynamic_index_in_dim(rows, core, 1, keepdims=False).reshape(width // 2, frames))
-    return jnp.concatenate(halves, axis=1)
+    rows = x.T.reshape(width // 16, 2, 8, frames)
+    return lax.dynamic_index_in_dim(rows, core, 1, keepdims=False).reshape(width // 2, frames)
 
 
 def swap_cores(x):
@@ -371,7 +381,7 @@
         (
             hbm_shape((rows, channels)),
             hbm_shape((rows, channels)),
-            hbm_shape((rows, channels)),
+            full,
             shape(tap_shape),
             shape(tap_shape),
             shape((8, channels)),
@@ -379,45 +389,46 @@
         [SM, HB, HB, HB, HB, VM, VM, HB, HB, HB],
         [wide, square, work],
     )(lengths, frames, proj, grad_out, proj_out, conv_a, buf_a, gain_row, shift_row, counts_row)
-    value_b, sig_b, hid_b, ones_b, conv_sum_b, conv_b, buf_b, ends = call(
+    late = lax.optimization_barrier((frames, grad_out, params))
+    left_in_a = core_rows(late[0], core)
+    left_out_a = core_rows(late[1], core)
+    got, left_in_a, left_out_a = lax.optimization_barrier((got, left_in_a, left_out_a))
+
+    hidden_a, stats, sums = call(
+        norm_kernel,
+        (
+            shape((rows, channels), BF16),
+            shape((2, channels)),
+            shape((3 * (count + 1) + 8, channels)),
+        ),
+        [SM] + [VM] * 7,
+        [work],
+    )(lengths, got, params, conv_a, hid_a, buf_a, ones_a, conv_sum_a)
+    (pay,) = call(
+        spread_kernel, (hbm_shape((chips, 8, LANES)),), [VM, VM], [pltpu.VMEM((3 * (count + 1) + 8, channels), F32)]
+    )(sums, swap_cores(sums))
+    got = lax.all_to_all(pay, YZ, 0, 0)
+
+    given = after(given, pay)
+    value_b, sig_b, hid_b, conv_b, hidden_b, ends = call(
         mirror_kernel,
         (
             hbm_shape((rows, channels)),
             hbm_shape((rows, channels)),
             hbm_shape((rows, channels)),
-            shape(tap_shape),
-            shape(tap_shape),
             full,
-            hbm_shape(buf_shape),
+            shape((rows, channels), BF16),
             shape((8, LANES)),
         ),
-        [HB, HB, HB, HB],
+        [HB, HB, HB, HB, VM, VM],
         [wide, square, work],
-    )(given, proj, proj_out, taps)
-
-    hidden, stats, pay = call(
-        norm_kernel,
-        (
-            shape((2 * rows, channels), BF16),
-            shape((2, channels)),
-            hbm_shape((chips, 8, LANES)),
-        ),
-        [SM] + [VM] * 5 + [AN] * 4 + [VM] * 4,
-        [
-            work,
-            pltpu.VMEM((4,) + tap_shape, F32),
-            pltpu.VMEM((2, rows, channels), F32),
-            pltpu.VMEM((2,) + buf_shape, F32),
-            pltpu.SemaphoreType.DMA((4,)),
-        ],
-    )(lengths, ends, got, params, conv_a, conv_b, hid_a, hid_b, buf_a, buf_b, ones_a, ones_b, conv_sum_a, conv_sum_b)
-    got = lax.all_to_all(pay, YZ, 0, 0)
-
-    given, frames, grad_out, _ = lax.optimization_barrier((given, frames, grad_out, pay))
-    left_in = core_rows(frames, given[:rows], core)
-    left_out = core_rows(grad_out, given[rows : 2 * rows], core)
-    (out_rows,) = call(rows_kernel, (hbm_shape((width // 2, channels), BF16),), [HB, VM])(left_out, hidden)
-    got, out_rows, left_in = lax.optimization_barrier((got, out_rows, left_in))
+    )(given, proj, proj_out, taps, stats, params)
+    left_in_b = core_rows(given[:rows], core)
+    left_out_b = core_rows(given[rows : 2 * rows], core)
+    (out_rows,) = call(rows_kernel, (hbm_shape((width // 2, channels), BF16),), [HB, HB, VM, VM])(
+        left_out_a, left_out_b, hidden_a, hidden_b
+    )
+    got, out_rows, left_in_a, left_in_b = lax.optimization_barrier((got, out_rows, left_in_a, left_in_b))
     out_rows = out_rows.reshape(chips, rows_dev, channels)
 
     half = (chip % 2).astype(jnp.int32).reshape(1)
@@ -429,20 +440,20 @@
             hbm_shape((1, channels)),
             hbm_shape((chips, rows_dev, 3 * channels + LANES), BF16),
         ),
-        [SM, SM] + [VM] * 7 + [AN] * 8,
+        [SM, SM] + [VM] * 7 + [AN] * 9,
         [
             work,
             pltpu.VMEM((2 * rows, 2 * channels), BF16),
             pltpu.VMEM((2, rows, channels), F32),
             pltpu.VMEM((2, rows, channels), F32),
             pltpu.VMEM((2, rows, channels), F32),
-            pltpu.VMEM((width // 2, 2 * rows), BF16),
+            pltpu.VMEM((2, width // 2, rows), BF16),
             pltpu.VMEM((chips, rows_dev, channels), BF16),
-            pltpu.SemaphoreType.DMA((8,)),
+            pltpu.SemaphoreType.DMA((9,)),
         ],
     )(
         lengths, half, ends, got, params, stats, conv_a, conv_b, taps,
-        hid_a, hid_b, value_a, value_b, sig_a, sig_b, left_in, out_rows,
+        hid_a, hid_b, value_a, value_b, sig_a, sig_b, left_in_a, left_in_b, out_rows,
     )
     got = lax.all_to_all(pay, YZ, 0, 0)
 

time: 108 us -> 107 us (level)
  waiting for transfers between devices: 27.9 us -> 32.3 us
  Pallas kernels: 26.7 us -> 22.6 us
  other arithmetic: 3.53 us -> 1.8 us
  local copies, waits for them, and re-layouts: 5.74 us -> 6.84 us
    pallas_call x8 -> x9, Pallas kernels: 26.7 us -> 22.6 us  [run(): return kernel(*held)]
    all_to_all x1, waiting for transfers between devices: 4.44 us -> 8.51 us  [shards(): got = lax.all_to_all(pay, DP, 0, 0)]
    all_to_all x2, starting transfers between devices: 12.9 us -> 10.5 us  [shards(): got = lax.all_to_all(pay, YZ, 0, 0)]
    reshape x2 -> x3, local copies, waits for them, and re-layouts: 0.08 us -> 2.29 us  [core_rows(): lax.dynamic_index_in_dim(rows, core, 1, keepdims=False)]
    ppermute x1 -> x2, starting transfers between devices: 1.91 us -> 3.83 us  [swap_cores(): return lax.ppermute(x, 'core', [(0, 1), (1, 0)])]
    concatenate x2 -> x0, other arithmetic: 1.7 us -> none  [core_rows(): return jnp.concatenate(halves, axis=1)]
    ppermute x1 -> x2, waiting for transfers between devices: 0.01 us -> 1.28 us  [swap_cores(): return lax.ppermute(x, 'core', [(0, 1), (1, 0)])]
    unnamed x27 -> x19, local copies, waits for them, and re-layouts: 3.19 us -> 2.47 us
  transfers between devices with their start and end apart: 7 -> 8, of which waited for: 5 -> 6; matrix products, arithmetic and copies ran while one was open for 5% -> 5% of each run, Pallas kernels for 13% -> 13%
where the time goes in v6:
time: 107 us; the launch traced here: 105 us
  starting transfers between devices  40.9 us (38%)
  waiting for transfers between devices  32.3 us (30%)
  Pallas kernels  22.6 us (21%)
  local copies, waits for them, and re-layouts  6.84 us (6%)
  other arithmetic  1.8 us (2%)
    pallas_call x9, Pallas kernels, run(): return kernel(*held)  22.6 us
    all_to_all x1, starting transfers between devices, shards(): got = lax.all_to_all(pay, DP, 0, 0)  17.9 us
    all_to_all x2, waiting for transfers between devices, shards(): got = lax.all_to_all(pay, YZ, 0, 0)  16.4 us
    all_to_all x2, starting transfers between devices, shards(): got = lax.all_to_all(pay, YZ, 0, 0)  10.5 us
    ppermute x3, starting transfers between devices, shards(): lax.ppermute(after(part, pay), 'mp', [(i, (i + d) % groups) for i in rang...  8.63 us
    all_to_all x1, waiting for transfers between devices, shards(): got = lax.all_to_all(pay, DP, 0, 0)  8.51 us
    ppermute x3, waiting for transfers between devices, shards(): lax.ppermute(after(part, pay), 'mp', [(i, (i + d) % groups) for i in rang...  6.14 us
    ppermute x2, starting transfers between devices, swap_cores(): return lax.ppermute(x, 'core', [(0, 1), (1, 0)])  3.83 us
  transfers between devices with their start and end apart: 8, of which 6 were waited for; matrix products, arithmetic and copies ran while one was open for 5% of the time, Pallas kernels for 13%

profile of v6, /device:TPU:6, one launch (start us, length us, event | category | flops | bytes accessed | tf_op | source)
XLA Modules:
  0.0 105.4 jit_solution(7963960251489556847)
XLA Ops:
  0.6 0.0 copy-start.8
  0.6 0.0 copy-start.4
  0.7 0.0 copy-start.1
  0.7 1.5 %copy.23 = bf16[128,8,2,256]{3,1,2,0:T(8,128)(2,1)S(1)} copy(bf16[128,8,2,256]{3,2,1,0:T(2,128)(2,1)} %bitcast.38) | data formatting | bytes 2097152
  2.2 0.0 copy-done.8
  2.2 0.0 copy-start
  2.2 0.0 copy-start.6
  2.2 0.0 copy-done.4
  2.2 0.0 copy-done.1
  2.2 2.8 %shard_map.136 = (f32[256,256]{1,0:T(8,128)S(1)}, f32[2,304,128]{2,1,0:T(8,128)S(1)}, f32[128,2,256]{2,1,0:T(2,128)}) custom-call(s32[1,2]{1,0:T(1,128)} %len_ref.7, bf16[256,1024]{1,0:T(8,128)(2,1)S(1)} %copy-done.1, bf16[1024,512]{1,0:T(8,128)(2,1)S(1)} %bitcast.30, f32[31,256]{1,0:T(8,128)S(1)} %copy-done.4), custom_call_target="tpu_custom_call" | custom-call | tf_op jit(solution)/shard_map/pallas_call | solution.py:34
  5.0 0.0 copy-done.6
  5.0 1.1 %fusion.1 = bf16[528,1024]{1,0:T(8,128)(2,1)} fusion(bf16[1,2]{1,0:T(2,128)(2,1)S(1)} %convert_element_type.20, bf16[256,1024]{1,0:T(8,128)(2,1)S(1)} %copy-done.6, bf16[256,1024]{1,0:T(8,128)(2,1)S(1)} %copy-done.1), kind=kLoop, calls=%fused_computation.2 | loop fusion | flops 4325376 | bytes 2129924 | tf_op jit(solution)/shard_map/concatenate | solution.py:377
  6.1 0.0 copy-done
  6.1 1.9 %collective-permute-start = (bf16[528,1024]{1,0:T(8,128)(2,1)}, bf16[528,1024]{1,0:T(8,128)(2,1)}, u32[]{:S(2)}, u32[]{:S(2)}) collective-permute-start(bf16[528,1024]{1,0:T(8,128)(2,1)} %fusion.1), channel_id=1, source_target_pairs={{0,4},{4,0},{1,5},{5,1},{2,6},{6,2},{3,7},{7,3},{8,12},{12,8},{9,1... | collective-permute-start | bytes 3244040 | tf_op jit(solution)/shard_map/ppermute | solution.py:340
  8.0 17.9 %all-to-all-start = ((f32[128,2,256]{2,1,0:T(2,128)}), f32[128,2,256]{2,1,0:T(2,128)S(1)}, u32[]{:S(2)}, u32[]{:S(2)}) async-start(f32[128,2,256]{2,1,0:T(2,128)} %get-tuple-element.49), calls=%async_computation | async-start | bytes 524288 | tf_op jit(solution)/shard_map/all_to_all | solution.py:374
  26.0 0.0 copy-start.7
  26.0 3.8 %shard_map.137 = (f32[256,256]{1,0:T(8,128)}, f32[256,256]{1,0:T(8,128)}, f32[256,256]{1,0:T(8,128)S(1)}, f32[32,256]{1,0:T(8,128)S(1)}, f32[32,256]{1,0:T(8,128)S(1)}, /*index=5*/f32[8,256]{1,0:T(8,128)S(1)}) custom-call(s32[1,2]{1,0:T(1,128)} %len_ref.7, bf16[256,1024]{1,0:T(8,128)(2,1)} %frames.3, bf16[1024,512]{1,0:T(8,128)(2,1)} %bitcast.31, ...), custom_call_target="tpu_custom_call" | custom-call | tf_op jit(solution)/shard_map/pallas_call | solution.py:34
  29.7 0.2 copy.20
  29.9 0.9 copy-done.2
  30.9 0.2 copy.19
  31.1 0.7 dynamic-slice_bitcast_fusion.2.left_a
  31.8 0.7 dynamic-slice_bitcast_fusion.3.left_a
  32.5 8.5 %all-to-all-done.got = f32[128,2,256]{2,1,0:T(2,128)S(1)} async-done(((f32[128,2,256]{2,1,0:T(2,128)}), f32[128,2,256]{2,1,0:T(2,128)S(1)}, u32[]{:S(2)}, u32[]{:S(2)}) %all-to-all-start) | async-done | bytes 262176 | tf_op jit(solution)/shard_map/all_to_all | solution.py:374
  41.0 1.8 %shard_map.138 = (bf16[256,256]{1,0:T(8,128)(2,1)S(1)}, f32[2,256]{1,0:T(2,128)S(1)}, f32[104,256]{1,0:T(8,128)S(1)}) custom-call(s32[1,2]{1,0:T(1,128)} %len_ref.7, f32[128,2,256]{2,1,0:T(2,128)S(1)} %all-to-all-done.got, f32[8,256]{1,0:T(8,128)S(1)} %get-tuple-element.53.params, f32[256,256]{1,0:T(8,128)S(1)} %get-tuple-element.51.conv_out.conv_a, ...), custom_call_target="tpu_custom_call" | custom-call | tf_op jit(solution)/shard_map/pallas_call | solution.py:34
  42.8 1.9 %collective-permute-start.1 = (f32[104,256]{1,0:T(8,128)S(1)}, f32[104,256]{1,0:T(8,128)S(1)}, u32[]{:S(2)}, u32[]{:S(2)}) collective-permute-start(f32[104,256]{1,0:T(8,128)S(1)} %get-tuple-element.60.own), channel_id=1, source_target_pairs={{0,4},{4,0},{1,5},{5,1},{2,6},{6,2},{3,7},{7,3},{8,12},{12,8},{9,1... | collective-permute-start | bytes 319496 | tf_op jit(solution)/shard_map/ppermute | solution.py:340
  44.8 1.3 %collective-permute-done.1.other = f32[104,256]{1,0:T(8,128)S(1)} collective-permute-done((f32[104,256]{1,0:T(8,128)S(1)}, f32[104,256]{1,0:T(8,128)S(1)}, u32[]{:S(2)}, u32[]{:S(2)}) %collective-permute-start.1) | collective-permute-done | bytes 106528 | tf_op jit(solution)/shard_map/ppermute | solution.py:340
  46.0 0.8 shard_map.139
  46.9 4.8 %all-to-all-start.1 = ((f32[64,8,128]{2,1,0:T(8,128)}), f32[64,8,128]{2,1,0:T(8,128)S(1)}, u32[]{:S(2)}, u32[]{:S(2)}) async-start(f32[64,8,128]{2,1,0:T(8,128)} %shard_map.139), calls=%async_computation.1 | async-start | bytes 524288 | tf_op jit(solution)/shard_map/all_to_all | solution.py:410
  51.7 0.0 collective-permute-done.given
  51.7 1.3 %slice_bitcast_fusion = (bf16[1024,256]{0,1:T(8,128)(2,1)S(1)}, bf16[1024,256]{0,1:T(8,128)(2,1)S(1)}) fusion(bf16[528,1024]{1,0:T(8,128)(2,1)} %collective-permute-done.given), kind=kLoop, calls=%fused_computation.3 | loop fusion | bytes 2097152 | tf_op jit(solution)/shard_map/transpose | solution.py:335
  53.0 0.2 copy.21
  53.2 0.2 copy.22
  53.4 3.7 %shard_map.140 = (f32[256,256]{1,0:T(8,128)}, f32[256,256]{1,0:T(8,128)}, f32[256,256]{1,0:T(8,128)}, f32[256,256]{1,0:T(8,128)S(1)}, bf16[256,256]{1,0:T(8,128)(2,1)S(1)}, /*index=5*/f32[8,128]{1,0:T(8,128)S(1)}) custom-call(bf16[528,1024]{1,0:T(8,128)(2,1)} %collective-permute-done.given, bf16[1024,512]{1,0:T(8,128)(2,1)} %bitcast.32, ...), custom_call_target="tpu_custom_call" | custom-call | tf_op jit(solution)/shard_map/pallas_call | solution.py:34
  57.1 0.8 dynamic-slice_bitcast_fusion
  57.9 2.0 %shard_map.141 = bf16[512,256]{1,0:T(8,128)(2,1)} custom-call(bf16[512,256]{1,0:T(8,128)(2,1)} %dynamic-slice_bitcast_fusion.2.left_a, bf16[512,256]{1,0:T(8,128)(2,1)} %get-tuple-element.95.left_b, bf16[256,256]{1,0:T(8,128)(2,1)S(1)} %get-tuple-element.65.right_a, bf16[256,256]{1,0:T(8,128)(2,1)S(1)} %get-tuple-element.66.right_b), custom_call_target="tpu_custom_call" | custom-call | tf_op jit(solution)/shard_map/pallas_call | solution.py:34
  60.0 6.8 %all-to-all-done.1.got = f32[64,8,128]{2,1,0:T(8,128)S(1)} async-done(((f32[64,8,128]{2,1,0:T(8,128)}), f32[64,8,128]{2,1,0:T(8,128)S(1)}, u32[]{:S(2)}, u32[]{:S(2)}) %all-to-all-start.1) | async-done | bytes 262176 | tf_op jit(solution)/shard_map/all_to_all | solution.py:410
  66.8 5.2 %shard_map.142 = (bf16[256,512]{1,0:T(8,128)(2,1)S(1)}, f32[1,256]{1,0:T(1,128)}, f32[1,256]{1,0:T(1,128)}, bf16[64,8,896]{2,1,0:T(8,128)(2,1)}) custom-call(s32[1,2]{1,0:T(1,128)} %len_ref.7, s32[1]{0:T(128)} %bitcast.1.half_ref, f32[8,128]{1,0:T(8,128)S(1)} %get-tuple-element.63.ends, f32[64,8,128]{2,1,0:T(8,128)S(1)} %all-to-all-done.1.got, ...), custom_call_target="tpu_custom_call" | custom-call | tf_op jit(solution)/shard_map/pallas_call | solution.py:34
  72.0 5.7 %all-to-all-start.2 = ((bf16[64,8,896]{2,1,0:T(8,128)(2,1)}), bf16[64,8,896]{2,1,0:T(8,128)(2,1)S(1)}, u32[]{:S(2)}, u32[]{:S(2)}) async-start(bf16[64,8,896]{2,1,0:T(8,128)(2,1)} %get-tuple-element.81), calls=%async_computation.2 | async-start | bytes 1835008 | tf_op jit(solution)/shard_map/all_to_all | solution.py:458
  77.8 1.7 %shard_map.143 = (bf16[256,256]{1,0:T(8,128)(2,1)S(1)}, bf16[256,256]{1,0:T(8,128)(2,1)S(1)}, bf16[256,256]{1,0:T(8,128)(2,1)S(1)}, bf16[256,256]{1,0:T(8,128)(2,1)S(1)}) custom-call(s32[1]{0:T(128)} %bitcast.mp_ref, bf16[256,512]{1,0:T(8,128)(2,1)S(1)} %get-tuple-element.78.grad_pre, bf16[1024,512]{1,0:T(8,128)(2,1)} %bitcast.33), custom_call_target="tpu_custom_call" | custom-call | tf_op jit(solution)/shard_map/pallas_call | solution.py:34
  79.5 2.4 %collective-permute-start.2 = (bf16[256,256]{1,0:T(8,128)(2,1)S(1)}, bf16[256,256]{1,0:T(8,128)(2,1)S(1)}, u32[]{:S(2)}, u32[]{:S(2)}) collective-permute-start(bf16[256,256]{1,0:T(8,128)(2,1)S(1)} %get-tuple-element.82), channel_id=1, source_target_pairs={{0,1},{1,2},{2,3},{3,0},{4,5},{5,6},{6,7},{7,4},{8,9},{9,10},{10,1... | collective-permute-start | bytes 393224 | tf_op jit(solution)/shard_map/ppermute | solution.py:467
  81.9 4.3 %collective-permute-start.3 = (bf16[256,256]{1,0:T(8,128)(2,1)S(1)}, bf16[256,256]{1,0:T(8,128)(2,1)S(1)}, u32[]{:S(2)}, u32[]{:S(2)}) collective-permute-start(bf16[256,256]{1,0:T(8,128)(2,1)S(1)} %get-tuple-element.84), channel_id=1, source_target_pairs={{0,2},{1,3},{2,0},{3,1},{4,6},{5,7},{6,4},{7,5},{8,10},{9,11},{10,... | collective-permute-start | bytes 393224 | tf_op jit(solution)/shard_map/ppermute | solution.py:467
  86.2 1.9 %collective-permute-start.4 = (bf16[256,256]{1,0:T(8,128)(2,1)S(1)}, bf16[256,256]{1,0:T(8,128)(2,1)S(1)}, u32[]{:S(2)}, u32[]{:S(2)}) collective-permute-start(bf16[256,256]{1,0:T(8,128)(2,1)S(1)} %get-tuple-element.86), channel_id=1, source_target_pairs={{0,3},{1,0},{2,1},{3,2},{4,7},{5,4},{6,5},{7,6},{8,11},{9,8},{10,9... | collective-permute-start | bytes 393224 | tf_op jit(solution)/shard_map/ppermute | solution.py:467
  88.1 0.0 collective-permute-done.2
  88.1 2.1 %collective-permute-done.3 = bf16[256,256]{1,0:T(8,128)(2,1)S(1)} collective-permute-done((bf16[256,256]{1,0:T(8,128)(2,1)S(1)}, bf16[256,256]{1,0:T(8,128)(2,1)S(1)}, u32[]{:S(2)}, u32[]{:S(2)}) %collective-permute-start.3) | collective-permute-done | bytes 131104 | tf_op jit(solution)/shard_map/ppermute | solution.py:467
  90.2 4.0 %collective-permute-done.4 = bf16[256,256]{1,0:T(8,128)(2,1)S(1)} collective-permute-done((bf16[256,256]{1,0:T(8,128)(2,1)S(1)}, bf16[256,256]{1,0:T(8,128)(2,1)S(1)}, u32[]{:S(2)}, u32[]{:S(2)}) %collective-permute-start.4) | collective-permute-done | bytes 131104 | tf_op jit(solution)/shard_map/ppermute | solution.py:467
  94.3 0.7 add_convert_fusion
  95.0 9.6 %all-to-all-done.2.got = bf16[64,8,896]{2,1,0:T(8,128)(2,1)S(1)} async-done(((bf16[64,8,896]{2,1,0:T(8,128)(2,1)}), bf16[64,8,896]{2,1,0:T(8,128)(2,1)S(1)}, u32[]{:S(2)}, u32[]{:S(2)}) %all-to-all-start.2) | async-done | bytes 917536 | tf_op jit(solution)/shard_map/all_to_all | solution.py:458
  104.6 0.8 shard_map.144
  (7 shorter events, 0.0 us)
Async XLA Ops:
  0.6 1.6 %copy-start.8 = (s32[1,2]{1,0:T(1,128)S(1)}, s32[1,2]{1,0:T(1,128)}, u32[]{:S(2)}) copy-start(s32[1,2]{1,0:T(1,128)} %len_ref.7) | copy-start | bytes 28
  0.6 1.6 %copy-start.4 = (f32[31,256]{1,0:T(8,128)S(1)}, f32[31,256]{1,0:T(8,128)}, u32[]{:S(2)}) copy-start(f32[31,256]{1,0:T(8,128)} %taps.5) | copy-start | bytes 95236
  0.7 1.6 %copy-start.1 = (bf16[256,1024]{1,0:T(8,128)(2,1)S(1)}, bf16[256,1024]{1,0:T(8,128)(2,1)}, u32[]{:S(2)}) copy-start(bf16[256,1024]{1,0:T(8,128)(2,1)} %frames.3) | copy-start | bytes 1572868
  2.2 3.9 %copy-start = (bf16[128,8,2,256]{3,1,2,0:T(8,128)(2,1)}, bf16[128,8,2,256]{3,1,2,0:T(8,128)(2,1)S(1)}, u32[]{:S(2)}) copy-start(bf16[128,8,2,256]{3,1,2,0:T(8,128)(2,1)S(1)} %copy.23) | copy-start | bytes 3145732
  2.2 2.8 %copy-start.6 = (bf16[256,1024]{1,0:T(8,128)(2,1)S(1)}, bf16[256,1024]{1,0:T(8,128)(2,1)}, u32[]{:S(2)}) copy-start(bf16[256,1024]{1,0:T(8,128)(2,1)} %grad_out.1) | copy-start | bytes 1572868
  6.1 45.6 %collective-permute-start = (bf16[528,1024]{1,0:T(8,128)(2,1)}, bf16[528,1024]{1,0:T(8,128)(2,1)}, u32[]{:S(2)}, u32[]{:S(2)}) collective-permute-start(bf16[528,1024]{1,0:T(8,128)(2,1)} %fusion.1), channel_id=1, source_target_pairs={{0,4},{4,0},{1,5},{5,1},{2,6},{6,2},{3,7},{7,3},{8,12},{12,8},{9,1... | collective-permute-start | bytes 3244040 | tf_op jit(solution)/shard_map/ppermute | solution.py:340
  8.0 33.0 %all-to-all-start = ((f32[128,2,256]{2,1,0:T(2,128)}), f32[128,2,256]{2,1,0:T(2,128)S(1)}, u32[]{:S(2)}, u32[]{:S(2)}) async-start(f32[128,2,256]{2,1,0:T(2,128)} %get-tuple-element.49), calls=%async_computation | async-start | bytes 524288 | tf_op jit(solution)/shard_map/all_to_all | solution.py:374
  26.0 3.8 %copy-start.7 = (bf16[256,1024]{1,0:T(8,128)(2,1)S(1)}, bf16[256,1024]{1,0:T(8,128)(2,1)}, u32[]{:S(2)}) copy-start(bf16[256,1024]{1,0:T(8,128)(2,1)} %grad_out.1) | copy-start | bytes 1572868
  29.7 11.3 %copy-start.3 = (f32[256,256]{1,0:T(8,128)}, f32[256,256]{1,0:T(8,128)S(1)}, u32[]{:S(2)}) copy-start(f32[256,256]{1,0:T(8,128)S(1)} %get-tuple-element.57.grad_hidden.hid_a) | copy-start | bytes 786436
  29.7 1.1 %copy-start.2 = (bf16[256,1024]{1,0:T(8,128)(2,1)S(1)}, bf16[256,1024]{1,0:T(8,128)(2,1)}, u32[]{:S(2)}) copy-start(bf16[256,1024]{1,0:T(8,128)(2,1)} %frames.3) | copy-start | bytes 1572868
  42.8 3.2 %collective-permute-start.1 = (f32[104,256]{1,0:T(8,128)S(1)}, f32[104,256]{1,0:T(8,128)S(1)}, u32[]{:S(2)}, u32[]{:S(2)}) collective-permute-start(f32[104,256]{1,0:T(8,128)S(1)} %get-tuple-element.60.own), channel_id=1, source_target_pairs={{0,4},{4,0},{1,5},{5,1},{2,6},{6,2},{3,7},{7,3},{8,12},{12,8},{9,1... | collective-permute-start | bytes 319496 | tf_op jit(solution)/shard_map/ppermute | solution.py:340
  46.9 19.9 %all-to-all-start.1 = ((f32[64,8,128]{2,1,0:T(8,128)}), f32[64,8,128]{2,1,0:T(8,128)S(1)}, u32[]{:S(2)}, u32[]{:S(2)}) async-start(f32[64,8,128]{2,1,0:T(8,128)} %shard_map.139), calls=%async_computation.1 | async-start | bytes 524288 | tf_op jit(solution)/shard_map/all_to_all | solution.py:410
  57.1 9.7 %copy-start.5 = (f32[31,256]{1,0:T(8,128)S(1)}, f32[31,256]{1,0:T(8,128)}, u32[]{:S(2)}) copy-start(f32[31,256]{1,0:T(8,128)} %taps.5) | copy-start | bytes 95236
  72.0 32.6 %all-to-all-start.2 = ((bf16[64,8,896]{2,1,0:T(8,128)(2,1)}), bf16[64,8,896]{2,1,0:T(8,128)(2,1)S(1)}, u32[]{:S(2)}, u32[]{:S(2)}) async-start(bf16[64,8,896]{2,1,0:T(8,128)(2,1)} %get-tuple-element.81), calls=%async_computation.2 | async-start | bytes 1835008 | tf_op jit(solution)/shard_map/all_to_all | solution.py:458
  79.5 8.7 %collective-permute-start.2 = (bf16[256,256]{1,0:T(8,128)(2,1)S(1)}, bf16[256,256]{1,0:T(8,128)(2,1)S(1)}, u32[]{:S(2)}, u32[]{:S(2)}) collective-permute-start(bf16[256,256]{1,0:T(8,128)(2,1)S(1)} %get-tuple-element.82), channel_id=1, source_target_pairs={{0,1},{1,2},{2,3},{3,0},{4,5},{5,6},{6,7},{7,4},{8,9},{9,10},{10,1... | collective-permute-start | bytes 393224 | tf_op jit(solution)/shard_map/ppermute | solution.py:467
  81.9 8.4 %collective-permute-start.3 = (bf16[256,256]{1,0:T(8,128)(2,1)S(1)}, bf16[256,256]{1,0:T(8,128)(2,1)S(1)}, u32[]{:S(2)}, u32[]{:S(2)}) collective-permute-start(bf16[256,256]{1,0:T(8,128)(2,1)S(1)} %get-tuple-element.84), channel_id=1, source_target_pairs={{0,2},{1,3},{2,0},{3,1},{4,6},{5,7},{6,4},{7,5},{8,10},{9,11},{10,... | collective-permute-start | bytes 393224 | tf_op jit(solution)/shard_map/ppermute | solution.py:467
  86.2 8.1 %collective-permute-start.4 = (bf16[256,256]{1,0:T(8,128)(2,1)S(1)}, bf16[256,256]{1,0:T(8,128)(2,1)S(1)}, u32[]{:S(2)}, u32[]{:S(2)}) collective-permute-start(bf16[256,256]{1,0:T(8,128)(2,1)S(1)} %get-tuple-element.86), channel_id=1, source_target_pairs={{0,3},{1,0},{2,1},{3,2},{4,7},{5,4},{6,5},{7,6},{8,11},{9,8},{10,9... | collective-permute-start | bytes 393224 | tf_op jit(solution)/shard_map/ppermute | solution.py:467

commit v7 on v6

--- a/solution.py
+++ b/solution.py
@@ -21,9 +21,13 @@
 NT = (((1,), (1,)), ((), ()))
 
 
-def call(body, outs, ins, scratch=()):
+def call(body, outs, ins, scratch=(), out_specs=None):
     kernel = pl.pallas_call(
-        body, out_shape=outs, in_specs=ins, out_specs=tuple(VM for _ in outs), scratch_shapes=list(scratch)
+        body,
+        out_shape=outs,
+        in_specs=ins,
+        out_specs=out_specs or tuple(VM for _ in outs),
+        scratch_shapes=list(scratch),
     )
 
     def run(*args):
@@ -118,13 +122,29 @@
     return value, sig, jnp.where(live, value * sig, 0.0).astype(BF16).astype(F32)
 
 
-def forward_kernel(len_ref, frames, proj, taps, conv_out, buf, pay, pre):
+def forward_kernel(
+    len_ref, frames, proj, taps, raw_frames, raw_grad,
+    conv_out, buf, pay, value_out, sig_out, given, pre, value, sig, spans, sems,
+):
     rows, channels = conv_out.shape
     first, live = own_masks(len_ref, rows)
+    lane = lax.broadcasted_iota(jnp.int32, spans.shape, 1)
+    spans[...] = jnp.where(
+        lane == 0, len_ref[0, 0].astype(F32), jnp.where(lane == 1, len_ref[0, 1].astype(F32), 0.0)
+    ).astype(BF16)
+    copies = fetches(
+        (raw_frames, raw_grad, spans),
+        (given.at[pl.ds(0, rows)], given.at[pl.ds(rows, rows)], given.at[pl.ds(2 * rows, 16)]),
+        sems,
+    )
     pre[...] = jnp.dot(frames[...], proj[...], preferred_element_type=F32)
+    glus = []
+    for h in range(channels // LANES):
+        value[:, lanes(h)], sig[:, lanes(h)], glu = gated(pre, live, h, channels)
+        glus.append(glu)
+    copies += fetches((value, sig), (value_out, sig_out), sems.at[pl.ds(3, 2)])
     sums = []
-    for h in range(channels // LANES):
-        _, _, glu = gated(pre, live, h, channels)
+    for h, glu in enumerate(glus):
         embed(buf, h, glu, first)
         out = jnp.where(live, conv(buf, h, taps, rows, first, 1), 0.0)
         conv_out[:, lanes(h)] = out
@@ -135,6 +155,8 @@
         )
     both = jnp.concatenate(sums, axis=1)
     pay[...] = jnp.broadcast_to(both[None], pay.shape)
+    for copy in copies:
+        copy.wait()
 
 
 def live_taps(split, end, rows):
@@ -147,17 +169,15 @@
 
 
 def side_kernel(
-    len_ref, frames, proj, grad_out, proj_out, conv_out, buf, gain, shift, counts,
-    value, sig, grad_hidden, ones_sum, conv_sum, params, pre, hid, work,
+    len_ref, grad_out, proj_out, conv_out, buf, gain, shift, counts,
+    grad_hidden, ones_sum, conv_sum, params, hid, work,
 ):
     rows, channels = conv_out.shape
     first, live = own_masks(len_ref, rows)
     marks = live_taps(len_ref[0, 0], len_ref[0, 0] + len_ref[0, 1], rows)
-    pre[...] = jnp.dot(frames[...], proj[...], preferred_element_type=F32)
     hid[...] = jnp.dot(grad_out[...], proj_out[...], preferred_element_type=F32)
     for h in range(channels // LANES):
         cols = lanes(h)
-        value[:, cols], sig[:, cols], _ = gated(pre, live, h, channels)
         grad_hidden[:, cols] = jnp.where(live, hid[:, cols], 0.0)
         ones_sum[:, cols] = jnp.dot(marks, buf[h].astype(BF16), preferred_element_type=F32)
         embed(work, h, conv_out[:, cols], first)
@@ -259,9 +279,7 @@
     total = params[2:3]
     sums = tree_sum(got[...])
     mean, inv_std = stats[0:1], stats[1:2]
-    copies[0].wait()
-    copies[1].wait()
-    slices = []
+    slices, scales, means = [], [], []
     for h in range(channels // LANES):
         cols = lanes(h)
         s, q = sums[h : h + 1], sums[2 + h : 3 + h]
@@ -269,12 +287,20 @@
         gain_grad[:, cols] = q
         scale = params[0:1, cols] * inv_std[:, cols]
         s, q = s / total[:, cols], q / total[:, cols]
-        for part, conv_out in enumerate((conv_a, conv_b)):
-            masks = own_masks(len_ref, rows) if part == 0 else row_masks(ends[0:1], ends[1:2], rows)
-            first, live = masks
-            span = slice(part * rows, (part + 1) * rows)
+        own, ones, cv = sums[4:5], sums[5:6], sums[6:7]
+        slices.append(scale * (own - s * ones - q * inv_std[:, cols] * (cv - mean[:, cols] * ones)))
+        scales.append(scale)
+        means.append((s, q))
+    for part, conv_out in enumerate((conv_a, conv_b)):
+        masks = own_masks(len_ref, rows) if part == 0 else row_masks(ends[0:1], ends[1:2], rows)
+        first, live = masks
+        span = slice(part * rows, (part + 1) * rows)
+        copies[part].wait()
+        for h in range(channels // LANES):
+            cols = lanes(h)
+            s, q = means[h]
             norm, scaled, swish = batch_norm(conv_out, mean, inv_std, params, cols)
-            grad = scale * (hids[part, :, cols] * swish_slope(scaled, swish) - s - norm * q)
+            grad = scales[h] * (hids[part, :, cols] * swish_slope(scaled, swish) - s - norm * q)
             embed(work, h, jnp.where(live, grad, 0.0), first)
             glu = jnp.where(live, conv(work, h, taps, rows, first, -1), 0.0)
             if h == 0:
@@ -285,15 +311,13 @@
             grad_pre[span, channels + h * LANES : channels + (h + 1) * LANES] = (
                 glu * v * g * (1.0 - g)
             ).astype(BF16)
-        own, ones, cv = sums[4:5], sums[5:6], sums[6:7]
-        slices.append(scale * (own - s * ones - q * inv_std[:, cols] * (cv - mean[:, cols] * ones)))
+        copies[6 + part].wait()
+        term = jnp.dot(left[part], grad_pre[span], preferred_element_type=F32)
+        total = term if part == 0 else total + term
     own_pre[...] = grad_pre[:rows]
     which = jnp.full((1, LANES), half_ref[0], jnp.int32)
     depth = jnp.where(which == 0, slices[0], slices[1]).astype(BF16)
-    for copy in copies[6:]:
-        copy.wait()
-    total = jnp.dot(left[0], grad_pre[:rows], preferred_element_type=F32)
-    total = total + jnp.dot(left[1], grad_pre[rows:], preferred_element_type=F32)
+    copies[8].wait()
     pay[:, :, :width] = total.reshape(peers, rows_dev, width).astype(BF16)
     pay[:, :, width : width + channels] = out_rows[...]
     pay[:, :, width + channels :] = jnp.broadcast_to(depth[None], (peers, rows_dev, LANES))
@@ -368,27 +392,34 @@
     gain_row = bn_gain.reshape(1, channels)
     shift_row = bn_shift.reshape(1, channels)
 
-    conv_a, buf_a, pay = call(
-        forward_kernel, (full, shape(buf_shape), hbm_shape((peers, 2, channels))), [SM, VM, VM, VM], [wide]
-    )(lengths, frames, proj, taps)
+    conv_a, buf_a, pay, value_a, sig_a, given = call(
+        forward_kernel,
+        (
+            full,
+            shape(buf_shape),
+            hbm_shape((peers, 2, channels)),
+            hbm_shape((rows, channels)),
+            hbm_shape((rows, channels)),
+            hbm_shape((2 * rows + 16, width), BF16),
+        ),
+        [SM, VM, VM, VM, AN, AN],
+        [wide, square, square, pltpu.VMEM((16, width), BF16), pltpu.SemaphoreType.DMA((5,))],
+        out_specs=(VM, VM, VM, AN, AN, AN),
+    )(lengths, frames, proj, taps, frames, grad_out)
     got = lax.all_to_all(pay, DP, 0, 0)
 
-    spans = jnp.pad(lengths.astype(BF16), ((0, 15), (0, width - lengths.shape[1])))
-    given = after(jnp.concatenate([frames, grad_out, spans], axis=0), pay)
     given = swap_cores(given)
-    value_a, sig_a, hid_a, ones_a, conv_sum_a, params = call(
+    hid_a, ones_a, conv_sum_a, params = call(
         side_kernel,
         (
-            hbm_shape((rows, channels)),
-            hbm_shape((rows, channels)),
             full,
             shape(tap_shape),
             shape(tap_shape),
             shape((8, channels)),
         ),
-        [SM, HB, HB, HB, HB, VM, VM, HB, HB, HB],
-        [wide, square, work],
-    )(lengths, frames, proj, grad_out, proj_out, conv_a, buf_a, gain_row, shift_row, counts_row)
+        [SM, HB, HB, VM, VM, HB, HB, HB],
+        [square, work],
+    )(lengths, grad_out, proj_out, conv_a, buf_a, gain_row, shift_row, counts_row)
     late = lax.optimization_barrier((frames, grad_out, params))
     left_in_a = core_rows(late[0], core)
     left_out_a = core_rows(late[1], core)
@@ -405,7 +436,10 @@
         [work],
     )(lengths, got, params, conv_a, hid_a, buf_a, ones_a, conv_sum_a)
     (pay,) = call(
-        spread_kernel, (hbm_shape((chips, 8, LANES)),), [VM, VM], [pltpu.VMEM((3 * (count + 1) + 8, channels), F32)]
+        spread_kernel,
+        (hbm_shape((chips, 8, LANES)),),
+        [VM, VM],
+        [pltpu.VMEM((3 * (count + 1) + 8, channels), F32)],
     )(sums, swap_cores(sums))
     got = lax.all_to_all(pay, YZ, 0, 0)
 

time: 107 us -> 121 us (1.13)
  Pallas kernels: 22.6 us -> 36.9 us
  waiting for transfers between devices: 32.3 us -> 34.7 us
    pallas_call x9, Pallas kernels: 22.6 us -> 36.9 us  [run(): return kernel(*held)]
    all_to_all x1, waiting for transfers between devices: 8.51 us -> 10.7 us  [shards(): got = lax.all_to_all(pay, DP, 0, 0)]
    unnamed x19 -> x13, local copies, waits for them, and re-layouts: 2.47 us -> 1.54 us
  transfers between devices with their start and end apart: 8 -> 8, of which waited for: 6 -> 6; matrix products, arithmetic and copies ran while one was open for 5% -> 4% of each run, Pallas kernels for 13% -> 10%
where the time goes in v7:
time: 121 us; the launch traced here: 120 us
  starting transfers between devices  40.8 us (34%)
  Pallas kernels  36.9 us (30%)
  waiting for transfers between devices  34.7 us (29%)
  local copies, waits for them, and re-layouts  5.88 us (5%)
    pallas_call x9, Pallas kernels, run(): return kernel(*held)  36.9 us
    all_to_all x1, starting transfers between devices, shards(): got = lax.all_to_all(pay, DP, 0, 0)  18.1 us
    all_to_all x2, waiting for transfers between devices, shards(): got = lax.all_to_all(pay, YZ, 0, 0)  16.6 us
    all_to_all x1, waiting for transfers between devices, shards(): got = lax.all_to_all(pay, DP, 0, 0)  10.7 us
    all_to_all x2, starting transfers between devices, shards(): got = lax.all_to_all(pay, YZ, 0, 0)  10.3 us
    ppermute x3, starting transfers between devices, shards(): lax.ppermute(after(part, pay), 'mp', [(i, (i + d) % groups) for i in rang...  8.64 us
    ppermute x3, waiting for transfers between devices, shards(): lax.ppermute(after(part, pay), 'mp', [(i, (i + d) % groups) for i in rang...  6.14 us
    ppermute x2, starting transfers between devices, swap_cores(): return lax.ppermute(x, 'core', [(0, 1), (1, 0)])  3.84 us
  transfers between devices with their start and end apart: 8, of which 6 were waited for; matrix products, arithmetic and copies ran while one was open for 4% of the time, Pallas kernels for 10%

profile of v7, /device:TPU:6, one launch (start us, length us, event | category | flops | bytes accessed | tf_op | source)
XLA Modules:
  0.0 119.9 jit_solution(12706326091510607214)
XLA Ops:
  0.6 0.0 copy-start.3
  0.6 0.0 copy-start.1
  0.7 1.5 %copy.23 = bf16[128,8,2,256]{3,1,2,0:T(8,128)(2,1)S(1)} copy(bf16[128,8,2,256]{3,2,1,0:T(2,128)(2,1)} %bitcast.37) | data formatting | bytes 2097152
  2.2 0.0 copy-start
  2.2 0.0 copy-done.3
  2.2 0.0 copy-done.1
  2.2 18.4 %shard_map.136 = (f32[256,256]{1,0:T(8,128)S(1)}, f32[2,304,128]{2,1,0:T(8,128)S(1)}, f32[128,2,256]{2,1,0:T(2,128)}, f32[256,256]{1,0:T(8,128)}, f32[256,256]{1,0:T(8,128)}, /*index=5*/bf16[528,1024]{1,0:T(8,128)(2,1)}) custom-call(s32[1,2]{1,0:T(1,128)} %len_ref.7, bf16[256,1024]{1,0:T(8,128)(2,1)S(1)} %copy-done.1, bf16[1024,512]{1,0:T(8,128)(2,1)S(1)} %bitcast.30, ...), custom_call_target="tpu_custom_call" | custom-call | tf_op jit(solution)/shard_map/pallas_call | solution.py:38
  20.6 0.0 copy-done
  20.6 1.9 %collective-permute-start = (bf16[528,1024]{1,0:T(8,128)(2,1)}, bf16[528,1024]{1,0:T(8,128)(2,1)}, u32[]{:S(2)}, u32[]{:S(2)}) collective-permute-start(bf16[528,1024]{1,0:T(8,128)(2,1)} %get-tuple-element.49), channel_id=1, source_target_pairs={{0,4},{4,0},{1,5},{5,1},{2,6},{6,2},{3,7},{7,3},{8,12},{12,8},{9,1... | collective-permute-start | bytes 3244040 | tf_op jit(solution)/shard_map/ppermute | solution.py:364
  22.5 0.0 copy-start.5
  22.5 18.1 %all-to-all-start = ((f32[128,2,256]{2,1,0:T(2,128)}), f32[128,2,256]{2,1,0:T(2,128)S(1)}, u32[]{:S(2)}, u32[]{:S(2)}) async-start(f32[128,2,256]{2,1,0:T(2,128)} %get-tuple-element.50), calls=%async_computation | async-start | bytes 524288 | tf_op jit(solution)/shard_map/all_to_all | solution.py:409
  40.6 2.5 %shard_map.137 = (f32[256,256]{1,0:T(8,128)S(1)}, f32[32,256]{1,0:T(8,128)S(1)}, f32[32,256]{1,0:T(8,128)S(1)}, f32[8,256]{1,0:T(8,128)S(1)}) custom-call(s32[1,2]{1,0:T(1,128)} %len_ref.7, bf16[256,1024]{1,0:T(8,128)(2,1)} %grad_out.1, bf16[1024,256]{1,0:T(8,128)(2,1)} %proj_out.3, f32[256,256]{1,0:T(8,128)S(1)} %get-tuple-element.51.conv_out.conv_a, ...), custom_call_target="tpu_custom_call" | custom-call | tf_op jit(solution)/shard_map/pallas_call | solution.py:38
  43.2 0.0 copy-start.2
  43.2 0.0 copy-done.5
  43.2 0.2 copy.20
  43.4 0.2 copy.19
  43.6 0.7 dynamic-slice_bitcast_fusion.2.left_a
  44.3 0.7 dynamic-slice_bitcast_fusion.3.left_a
  45.0 10.7 %all-to-all-done.got = f32[128,2,256]{2,1,0:T(2,128)S(1)} async-done(((f32[128,2,256]{2,1,0:T(2,128)}), f32[128,2,256]{2,1,0:T(2,128)S(1)}, u32[]{:S(2)}, u32[]{:S(2)}) %all-to-all-start) | async-done | bytes 262176 | tf_op jit(solution)/shard_map/all_to_all | solution.py:409
  55.7 0.0 copy-done.2
  55.7 1.8 %shard_map.138 = (bf16[256,256]{1,0:T(8,128)(2,1)S(1)}, f32[2,256]{1,0:T(2,128)S(1)}, f32[104,256]{1,0:T(8,128)S(1)}) custom-call(s32[1,2]{1,0:T(1,128)} %len_ref.7, f32[128,2,256]{2,1,0:T(2,128)S(1)} %all-to-all-done.got, f32[8,256]{1,0:T(8,128)S(1)} %get-tuple-element.53.params, f32[256,256]{1,0:T(8,128)S(1)} %get-tuple-element.51.conv_out.conv_a, ...), custom_call_target="tpu_custom_call" | custom-call | tf_op jit(solution)/shard_map/pallas_call | solution.py:38
  57.5 1.9 %collective-permute-start.1 = (f32[104,256]{1,0:T(8,128)S(1)}, f32[104,256]{1,0:T(8,128)S(1)}, u32[]{:S(2)}, u32[]{:S(2)}) collective-permute-start(f32[104,256]{1,0:T(8,128)S(1)} %get-tuple-element.60.own), channel_id=1, source_target_pairs={{0,4},{4,0},{1,5},{5,1},{2,6},{6,2},{3,7},{7,3},{8,12},{12,8},{9,1... | collective-permute-start | bytes 319496 | tf_op jit(solution)/shard_map/ppermute | solution.py:364
  59.4 1.3 %collective-permute-done.1.other = f32[104,256]{1,0:T(8,128)S(1)} collective-permute-done((f32[104,256]{1,0:T(8,128)S(1)}, f32[104,256]{1,0:T(8,128)S(1)}, u32[]{:S(2)}, u32[]{:S(2)}) %collective-permute-start.1) | collective-permute-done | bytes 106528 | tf_op jit(solution)/shard_map/ppermute | solution.py:364
  60.7 0.8 shard_map.139
  61.5 4.6 %all-to-all-start.1 = ((f32[64,8,128]{2,1,0:T(8,128)}), f32[64,8,128]{2,1,0:T(8,128)S(1)}, u32[]{:S(2)}, u32[]{:S(2)}) async-start(f32[64,8,128]{2,1,0:T(8,128)} %shard_map.139), calls=%async_computation.1 | async-start | bytes 524288 | tf_op jit(solution)/shard_map/all_to_all | solution.py:444
  66.1 0.0 collective-permute-done.given
  66.1 1.3 %slice_bitcast_fusion = (bf16[1024,256]{0,1:T(8,128)(2,1)S(1)}, bf16[1024,256]{0,1:T(8,128)(2,1)S(1)}) fusion(bf16[528,1024]{1,0:T(8,128)(2,1)} %collective-permute-done.given), kind=kLoop, calls=%fused_computation | loop fusion | bytes 2097152 | tf_op jit(solution)/shard_map/transpose | solution.py:359
  67.4 0.2 copy.21
  67.6 0.2 copy.22
  67.8 3.7 %shard_map.140 = (f32[256,256]{1,0:T(8,128)}, f32[256,256]{1,0:T(8,128)}, f32[256,256]{1,0:T(8,128)}, f32[256,256]{1,0:T(8,128)S(1)}, bf16[256,256]{1,0:T(8,128)(2,1)S(1)}, /*index=5*/f32[8,128]{1,0:T(8,128)S(1)}) custom-call(bf16[528,1024]{1,0:T(8,128)(2,1)} %collective-permute-done.given, bf16[1024,512]{1,0:T(8,128)(2,1)} %bitcast.31, ...), custom_call_target="tpu_custom_call" | custom-call | tf_op jit(solution)/shard_map/pallas_call | solution.py:38
  71.5 0.0 copy-start.4
  71.5 0.8 dynamic-slice_bitcast_fusion
  72.4 2.0 %shard_map.141 = bf16[512,256]{1,0:T(8,128)(2,1)} custom-call(bf16[512,256]{1,0:T(8,128)(2,1)} %dynamic-slice_bitcast_fusion.2.left_a, bf16[512,256]{1,0:T(8,128)(2,1)} %get-tuple-element.95.left_b, bf16[256,256]{1,0:T(8,128)(2,1)S(1)} %get-tuple-element.65.right_a, bf16[256,256]{1,0:T(8,128)(2,1)S(1)} %get-tuple-element.66.right_b), custom_call_target="tpu_custom_call" | custom-call | tf_op jit(solution)/shard_map/pallas_call | solution.py:38
  74.4 7.0 %all-to-all-done.1.got = f32[64,8,128]{2,1,0:T(8,128)S(1)} async-done(((f32[64,8,128]{2,1,0:T(8,128)}), f32[64,8,128]{2,1,0:T(8,128)S(1)}, u32[]{:S(2)}, u32[]{:S(2)}) %all-to-all-start.1) | async-done | bytes 262176 | tf_op jit(solution)/shard_map/all_to_all | solution.py:444
  81.4 0.0 copy-done.4
  81.4 5.2 %shard_map.142 = (bf16[256,512]{1,0:T(8,128)(2,1)S(1)}, f32[1,256]{1,0:T(1,128)}, f32[1,256]{1,0:T(1,128)}, bf16[64,8,896]{2,1,0:T(8,128)(2,1)}) custom-call(s32[1,2]{1,0:T(1,128)} %len_ref.7, s32[1]{0:T(128)} %bitcast.1.half_ref, f32[8,128]{1,0:T(8,128)S(1)} %get-tuple-element.63.ends, f32[64,8,128]{2,1,0:T(8,128)S(1)} %all-to-all-done.1.got, ...), custom_call_target="tpu_custom_call" | custom-call | tf_op jit(solution)/shard_map/pallas_call | solution.py:38
  86.6 5.7 %all-to-all-start.2 = ((bf16[64,8,896]{2,1,0:T(8,128)(2,1)}), bf16[64,8,896]{2,1,0:T(8,128)(2,1)S(1)}, u32[]{:S(2)}, u32[]{:S(2)}) async-start(bf16[64,8,896]{2,1,0:T(8,128)(2,1)} %get-tuple-element.81), calls=%async_computation.2 | async-start | bytes 1835008 | tf_op jit(solution)/shard_map/all_to_all | solution.py:492
  92.3 1.7 %shard_map.143 = (bf16[256,256]{1,0:T(8,128)(2,1)S(1)}, bf16[256,256]{1,0:T(8,128)(2,1)S(1)}, bf16[256,256]{1,0:T(8,128)(2,1)S(1)}, bf16[256,256]{1,0:T(8,128)(2,1)S(1)}) custom-call(s32[1]{0:T(128)} %bitcast.mp_ref, bf16[256,512]{1,0:T(8,128)(2,1)S(1)} %get-tuple-element.78.grad_pre, bf16[1024,512]{1,0:T(8,128)(2,1)} %bitcast.32), custom_call_target="tpu_custom_call" | custom-call | tf_op jit(solution)/shard_map/pallas_call | solution.py:38
  94.0 2.4 %collective-permute-start.2 = (bf16[256,256]{1,0:T(8,128)(2,1)S(1)}, bf16[256,256]{1,0:T(8,128)(2,1)S(1)}, u32[]{:S(2)}, u32[]{:S(2)}) collective-permute-start(bf16[256,256]{1,0:T(8,128)(2,1)S(1)} %get-tuple-element.82), channel_id=1, source_target_pairs={{0,1},{1,2},{2,3},{3,0},{4,5},{5,6},{6,7},{7,4},{8,9},{9,10},{10,1... | collective-permute-start | bytes 393224 | tf_op jit(solution)/shard_map/ppermute | solution.py:501
  96.4 4.3 %collective-permute-start.3 = (bf16[256,256]{1,0:T(8,128)(2,1)S(1)}, bf16[256,256]{1,0:T(8,128)(2,1)S(1)}, u32[]{:S(2)}, u32[]{:S(2)}) collective-permute-start(bf16[256,256]{1,0:T(8,128)(2,1)S(1)} %get-tuple-element.84), channel_id=1, source_target_pairs={{0,2},{1,3},{2,0},{3,1},{4,6},{5,7},{6,4},{7,5},{8,10},{9,11},{10,... | collective-permute-start | bytes 393224 | tf_op jit(solution)/shard_map/ppermute | solution.py:501
  100.8 1.9 %collective-permute-start.4 = (bf16[256,256]{1,0:T(8,128)(2,1)S(1)}, bf16[256,256]{1,0:T(8,128)(2,1)S(1)}, u32[]{:S(2)}, u32[]{:S(2)}) collective-permute-start(bf16[256,256]{1,0:T(8,128)(2,1)S(1)} %get-tuple-element.86), channel_id=1, source_target_pairs={{0,3},{1,0},{2,1},{3,2},{4,7},{5,4},{6,5},{7,6},{8,11},{9,8},{10,9... | collective-permute-start | bytes 393224 | tf_op jit(solution)/shard_map/ppermute | solution.py:501
  102.7 0.0 collective-permute-done.2
  102.7 2.1 %collective-permute-done.3 = bf16[256,256]{1,0:T(8,128)(2,1)S(1)} collective-permute-done((bf16[256,256]{1,0:T(8,128)(2,1)S(1)}, bf16[256,256]{1,0:T(8,128)(2,1)S(1)}, u32[]{:S(2)}, u32[]{:S(2)}) %collective-permute-start.3) | collective-permute-done | bytes 131104 | tf_op jit(solution)/shard_map/ppermute | solution.py:501
  104.8 4.1 %collective-permute-done.4 = bf16[256,256]{1,0:T(8,128)(2,1)S(1)} collective-permute-done((bf16[256,256]{1,0:T(8,128)(2,1)S(1)}, bf16[256,256]{1,0:T(8,128)(2,1)S(1)}, u32[]{:S(2)}, u32[]{:S(2)}) %collective-permute-start.4) | collective-permute-done | bytes 131104 | tf_op jit(solution)/shard_map/ppermute | solution.py:501
  108.8 0.7 add_convert_fusion
  109.6 9.6 %all-to-all-done.2.got = bf16[64,8,896]{2,1,0:T(8,128)(2,1)S(1)} async-done(((bf16[64,8,896]{2,1,0:T(8,128)(2,1)}), bf16[64,8,896]{2,1,0:T(8,128)(2,1)S(1)}, u32[]{:S(2)}, u32[]{:S(2)}) %all-to-all-start.2) | async-done | bytes 917536 | tf_op jit(solution)/shard_map/all_to_all | solution.py:492
  119.2 0.8 shard_map.144
Async XLA Ops:
  0.6 1.5 %copy-start.3 = (f32[31,256]{1,0:T(8,128)S(1)}, f32[31,256]{1,0:T(8,128)}, u32[]{:S(2)}) copy-start(f32[31,256]{1,0:T(8,128)} %taps.5) | copy-start | bytes 95236
  0.6 1.5 %copy-start.1 = (bf16[256,1024]{1,0:T(8,128)(2,1)S(1)}, bf16[256,1024]{1,0:T(8,128)(2,1)}, u32[]{:S(2)}) copy-start(bf16[256,1024]{1,0:T(8,128)(2,1)} %raw_frames.1) | copy-start | bytes 1572868
  2.2 18.4 %copy-start = (bf16[128,8,2,256]{3,1,2,0:T(8,128)(2,1)}, bf16[128,8,2,256]{3,1,2,0:T(8,128)(2,1)S(1)}, u32[]{:S(2)}) copy-start(bf16[128,8,2,256]{3,1,2,0:T(8,128)(2,1)S(1)} %copy.23) | copy-start | bytes 3145732
  20.6 45.5 %collective-permute-start = (bf16[528,1024]{1,0:T(8,128)(2,1)}, bf16[528,1024]{1,0:T(8,128)(2,1)}, u32[]{:S(2)}, u32[]{:S(2)}) collective-permute-start(bf16[528,1024]{1,0:T(8,128)(2,1)} %get-tuple-element.49), channel_id=1, source_target_pairs={{0,4},{4,0},{1,5},{5,1},{2,6},{6,2},{3,7},{7,3},{8,12},{12,8},{9,1... | collective-permute-start | bytes 3244040 | tf_op jit(solution)/shard_map/ppermute | solution.py:364
  22.5 20.6 %copy-start.5 = (bf16[256,1024]{1,0:T(8,128)(2,1)S(1)}, bf16[256,1024]{1,0:T(8,128)(2,1)}, u32[]{:S(2)}) copy-start(bf16[256,1024]{1,0:T(8,128)(2,1)} %grad_out.1) | copy-start | bytes 1572868
  22.5 33.1 %all-to-all-start = ((f32[128,2,256]{2,1,0:T(2,128)}), f32[128,2,256]{2,1,0:T(2,128)S(1)}, u32[]{:S(2)}, u32[]{:S(2)}) async-start(f32[128,2,256]{2,1,0:T(2,128)} %get-tuple-element.50), calls=%async_computation | async-start | bytes 524288 | tf_op jit(solution)/shard_map/all_to_all | solution.py:409
  43.2 12.5 %copy-start.2 = (f32[256,256]{1,0:T(8,128)}, f32[256,256]{1,0:T(8,128)S(1)}, u32[]{:S(2)}) copy-start(f32[256,256]{1,0:T(8,128)S(1)} %get-tuple-element.57.grad_hidden.hid_a) | copy-start | bytes 786436
  57.5 3.2 %collective-permute-start.1 = (f32[104,256]{1,0:T(8,128)S(1)}, f32[104,256]{1,0:T(8,128)S(1)}, u32[]{:S(2)}, u32[]{:S(2)}) collective-permute-start(f32[104,256]{1,0:T(8,128)S(1)} %get-tuple-element.60.own), channel_id=1, source_target_pairs={{0,4},{4,0},{1,5},{5,1},{2,6},{6,2},{3,7},{7,3},{8,12},{12,8},{9,1... | collective-permute-start | bytes 319496 | tf_op jit(solution)/shard_map/ppermute | solution.py:364
  61.5 19.9 %all-to-all-start.1 = ((f32[64,8,128]{2,1,0:T(8,128)}), f32[64,8,128]{2,1,0:T(8,128)S(1)}, u32[]{:S(2)}, u32[]{:S(2)}) async-start(f32[64,8,128]{2,1,0:T(8,128)} %shard_map.139), calls=%async_computation.1 | async-start | bytes 524288 | tf_op jit(solution)/shard_map/all_to_all | solution.py:444
  71.5 9.9 %copy-start.4 = (f32[31,256]{1,0:T(8,128)S(1)}, f32[31,256]{1,0:T(8,128)}, u32[]{:S(2)}) copy-start(f32[31,256]{1,0:T(8,128)} %taps.5) | copy-start | bytes 95236
  86.6 32.6 %all-to-all-start.2 = ((bf16[64,8,896]{2,1,0:T(8,128)(2,1)}), bf16[64,8,896]{2,1,0:T(8,128)(2,1)S(1)}, u32[]{:S(2)}, u32[]{:S(2)}) async-start(bf16[64,8,896]{2,1,0:T(8,128)(2,1)} %get-tuple-element.81), calls=%async_computation.2 | async-start | bytes 1835008 | tf_op jit(solution)/shard_map/all_to_all | solution.py:492
  94.0 8.7 %collective-permute-start.2 = (bf16[256,256]{1,0:T(8,128)(2,1)S(1)}, bf16[256,256]{1,0:T(8,128)(2,1)S(1)}, u32[]{:S(2)}, u32[]{:S(2)}) collective-permute-start(bf16[256,256]{1,0:T(8,128)(2,1)S(1)} %get-tuple-element.82), channel_id=1, source_target_pairs={{0,1},{1,2},{2,3},{3,0},{4,5},{5,6},{6,7},{7,4},{8,9},{9,10},{10,1... | collective-permute-start | bytes 393224 | tf_op jit(solution)/shard_map/ppermute | solution.py:501
  96.4 8.4 %collective-permute-start.3 = (bf16[256,256]{1,0:T(8,128)(2,1)S(1)}, bf16[256,256]{1,0:T(8,128)(2,1)S(1)}, u32[]{:S(2)}, u32[]{:S(2)}) collective-permute-start(bf16[256,256]{1,0:T(8,128)(2,1)S(1)} %get-tuple-element.84), channel_id=1, source_target_pairs={{0,2},{1,3},{2,0},{3,1},{4,6},{5,7},{6,4},{7,5},{8,10},{9,11},{10,... | collective-permute-start | bytes 393224 | tf_op jit(solution)/shard_map/ppermute | solution.py:501
  100.8 8.1 %collective-permute-start.4 = (bf16[256,256]{1,0:T(8,128)(2,1)S(1)}, bf16[256,256]{1,0:T(8,128)(2,1)S(1)}, u32[]{:S(2)}, u32[]{:S(2)}) collective-permute-start(bf16[256,256]{1,0:T(8,128)(2,1)S(1)} %get-tuple-element.86), channel_id=1, source_target_pairs={{0,3},{1,0},{2,1},{3,2},{4,7},{5,4},{6,5},{7,6},{8,11},{9,8},{10,9... | collective-permute-start | bytes 393224 | tf_op jit(solution)/shard_map/ppermute | solution.py:501

commit v8 on v7

--- a/solution.py
+++ b/solution.py
@@ -23,11 +23,7 @@
 
 def call(body, outs, ins, scratch=(), out_specs=None):
     kernel = pl.pallas_call(
-        body,
-        out_shape=outs,
-        in_specs=ins,
-        out_specs=out_specs or tuple(VM for _ in outs),
-        scratch_shapes=list(scratch),
+        body, out_shape=outs, in_specs=ins, out_specs=out_specs or tuple(VM for _ in outs), scratch_shapes=list(scratch)
     )
 
     def run(*args):
@@ -123,8 +119,8 @@
 
 
 def forward_kernel(
-    len_ref, frames, proj, taps, raw_frames, raw_grad,
-    conv_out, buf, pay, value_out, sig_out, given, pre, value, sig, spans, sems,
+    len_ref, frames, proj, taps, raw_grad,
+    conv_out, buf, pay, value_out, sig_out, given, pre, value, sig, spans, grad, sems,
 ):
     rows, channels = conv_out.shape
     first, live = own_masks(len_ref, rows)
@@ -132,20 +128,17 @@
     spans[...] = jnp.where(
         lane == 0, len_ref[0, 0].astype(F32), jnp.where(lane == 1, len_ref[0, 1].astype(F32), 0.0)
     ).astype(BF16)
+    (inward,) = fetches((raw_grad,), (grad,), sems)
     copies = fetches(
-        (raw_frames, raw_grad, spans),
-        (given.at[pl.ds(0, rows)], given.at[pl.ds(rows, rows)], given.at[pl.ds(2 * rows, 16)]),
-        sems,
+        (frames, spans), (given.at[pl.ds(0, rows)], given.at[pl.ds(2 * rows, 16)]), sems.at[pl.ds(1, 2)]
     )
     pre[...] = jnp.dot(frames[...], proj[...], preferred_element_type=F32)
-    glus = []
     for h in range(channels // LANES):
         value[:, lanes(h)], sig[:, lanes(h)], glu = gated(pre, live, h, channels)
-        glus.append(glu)
+        embed(buf, h, glu, first)
     copies += fetches((value, sig), (value_out, sig_out), sems.at[pl.ds(3, 2)])
     sums = []
-    for h, glu in enumerate(glus):
-        embed(buf, h, glu, first)
+    for h in range(channels // LANES):
         out = jnp.where(live, conv(buf, h, taps, rows, first, 1), 0.0)
         conv_out[:, lanes(h)] = out
         sums.append(
@@ -153,6 +146,9 @@
                 [jnp.sum(out, axis=0, keepdims=True), jnp.sum(out * out, axis=0, keepdims=True)], axis=0
             )
         )
+        if h == 0:
+            inward.wait()
+            copies += fetches((grad,), (given.at[pl.ds(rows, rows)],), sems.at[pl.ds(5, 1)])
     both = jnp.concatenate(sums, axis=1)
     pay[...] = jnp.broadcast_to(both[None], pay.shape)
     for copy in copies:
@@ -402,10 +398,17 @@
             hbm_shape((rows, channels)),
             hbm_shape((2 * rows + 16, width), BF16),
         ),
-        [SM, VM, VM, VM, AN, AN],
-        [wide, square, square, pltpu.VMEM((16, width), BF16), pltpu.SemaphoreType.DMA((5,))],
+        [SM, VM, VM, VM, AN],
+        [
+            wide,
+            square,
+            square,
+            pltpu.VMEM((16, width), BF16),
+            pltpu.VMEM((rows, width), BF16),
+            pltpu.SemaphoreType.DMA((6,)),
+        ],
         out_specs=(VM, VM, VM, AN, AN, AN),
-    )(lengths, frames, proj, taps, frames, grad_out)
+    )(lengths, frames, proj, taps, grad_out)
     got = lax.all_to_all(pay, DP, 0, 0)
 
     given = swap_cores(given)
@@ -436,10 +439,7 @@
         [work],
     )(lengths, got, params, conv_a, hid_a, buf_a, ones_a, conv_sum_a)
     (pay,) = call(
-        spread_kernel,
-        (hbm_shape((chips, 8, LANES)),),
-        [VM, VM],
-        [pltpu.VMEM((3 * (count + 1) + 8, channels), F32)],
+        spread_kernel, (hbm_shape((chips, 8, LANES)),), [VM, VM], [pltpu.VMEM((3 * (count + 1) + 8, channels), F32)]
     )(sums, swap_cores(sums))
     got = lax.all_to_all(pay, YZ, 0, 0)
 
@@ -459,7 +459,7 @@
     )(given, proj, proj_out, taps, stats, params)
     left_in_b = core_rows(given[:rows], core)
     left_out_b = core_rows(given[rows : 2 * rows], core)
-    (out_rows,) = call(rows_kernel, (hbm_shape((width // 2, channels), BF16),), [HB, HB, VM, VM])(
+    (out_rows,) = call(rows_kernel, (hbm_shape((width // 2, channels), BF16),), [HB, VM, VM, VM])(
         left_out_a, left_out_b, hidden_a, hidden_b
     )
     got, out_rows, left_in_a, left_in_b = lax.optimization_barrier((got, out_rows, left_in_a, left_in_b))

time: 121 us -> 106 us (0.88)
  Pallas kernels: 36.9 us -> 21.9 us
    pallas_call x9, Pallas kernels: 36.9 us -> 21.9 us  [run(): return kernel(*held)]
  transfers between devices with their start and end apart: 8 -> 8, of which waited for: 6 -> 6; matrix products, arithmetic and copies ran while one was open for 4% -> 5% of each run, Pallas kernels for 10% -> 12%
where the time goes in v8:
time: 106 us; the launch traced here: 105 us
  starting transfers between devices  40.5 us (38%)
  waiting for transfers between devices  34.8 us (33%)
  Pallas kernels  21.9 us (21%)
  local copies, waits for them, and re-layouts  5.8 us (5%)
    pallas_call x9, Pallas kernels, run(): return kernel(*held)  21.9 us
    all_to_all x1, starting transfers between devices, shards(): got = lax.all_to_all(pay, DP, 0, 0)  17.9 us
    all_to_all x2, waiting for transfers between devices, shards(): got = lax.all_to_all(pay, YZ, 0, 0)  16.8 us
    all_to_all x1, waiting for transfers between devices, shards(): got = lax.all_to_all(pay, DP, 0, 0)  10.6 us
    all_to_all x2, starting transfers between devices, shards(): got = lax.all_to_all(pay, YZ, 0, 0)  10.1 us
    ppermute x3, starting transfers between devices, shards(): lax.ppermute(after(part, pay), 'mp', [(i, (i + d) % groups) for i in rang...  8.62 us
    ppermute x3, waiting for transfers between devices, shards(): lax.ppermute(after(part, pay), 'mp', [(i, (i + d) % groups) for i in rang...  6.14 us
    ppermute x2, starting transfers between devices, swap_cores(): return lax.ppermute(x, 'core', [(0, 1), (1, 0)])  3.84 us
  transfers between devices with their start and end apart: 8, of which 6 were waited for; matrix products, arithmetic and copies ran while one was open for 5% of the time, Pallas kernels for 12%

profile of v8, /device:TPU:6, one launch (start us, length us, event | category | flops | bytes accessed | tf_op | source)
XLA Modules:
  0.0 104.7 jit_solution(9333821120797973409)
XLA Ops:
  0.6 0.0 copy-start.3
  0.6 0.0 copy-start.1
  0.7 1.5 %copy.23 = bf16[128,8,2,256]{3,1,2,0:T(8,128)(2,1)S(1)} copy(bf16[128,8,2,256]{3,2,1,0:T(2,128)(2,1)} %bitcast.37) | data formatting | bytes 2097152
  2.2 0.0 copy-start
  2.2 0.0 copy-done.3
  2.2 0.0 copy-done.1
  2.2 3.5 %shard_map.136 = (f32[256,256]{1,0:T(8,128)S(1)}, f32[2,304,128]{2,1,0:T(8,128)S(1)}, f32[128,2,256]{2,1,0:T(2,128)}, f32[256,256]{1,0:T(8,128)}, f32[256,256]{1,0:T(8,128)}, /*index=5*/bf16[528,1024]{1,0:T(8,128)(2,1)}) custom-call(s32[1,2]{1,0:T(1,128)} %len_ref.7, bf16[256,1024]{1,0:T(8,128)(2,1)S(1)} %copy-done.1, bf16[1024,512]{1,0:T(8,128)(2,1)S(1)} %bitcast.30, ...), custom_call_target="tpu_custom_call" | custom-call | tf_op jit(solution)/shard_map/pallas_call | solution.py:34
  5.7 1.9 %collective-permute-start = (bf16[528,1024]{1,0:T(8,128)(2,1)}, bf16[528,1024]{1,0:T(8,128)(2,1)}, u32[]{:S(2)}, u32[]{:S(2)}) collective-permute-start(bf16[528,1024]{1,0:T(8,128)(2,1)} %get-tuple-element.49), channel_id=1, source_target_pairs={{0,4},{4,0},{1,5},{5,1},{2,6},{6,2},{3,7},{7,3},{8,12},{12,8},{9,1... | collective-permute-start | bytes 3244040 | tf_op jit(solution)/shard_map/ppermute | solution.py:360
  7.6 0.0 copy-done
  7.6 17.9 %all-to-all-start = ((f32[128,2,256]{2,1,0:T(2,128)}), f32[128,2,256]{2,1,0:T(2,128)S(1)}, u32[]{:S(2)}, u32[]{:S(2)}) async-start(f32[128,2,256]{2,1,0:T(2,128)} %get-tuple-element.50), calls=%async_computation | async-start | bytes 524288 | tf_op jit(solution)/shard_map/all_to_all | solution.py:412
  25.5 0.0 copy-start.5
  25.5 2.6 %shard_map.137 = (f32[256,256]{1,0:T(8,128)S(1)}, f32[32,256]{1,0:T(8,128)S(1)}, f32[32,256]{1,0:T(8,128)S(1)}, f32[8,256]{1,0:T(8,128)S(1)}) custom-call(s32[1,2]{1,0:T(1,128)} %len_ref.7, bf16[256,1024]{1,0:T(8,128)(2,1)} %grad_out.1, bf16[1024,256]{1,0:T(8,128)(2,1)} %proj_out.3, f32[256,256]{1,0:T(8,128)S(1)} %get-tuple-element.51.conv_out.conv_a, ...), custom_call_target="tpu_custom_call" | custom-call | tf_op jit(solution)/shard_map/pallas_call | solution.py:34
  28.1 0.0 copy-start.2
  28.2 0.0 copy-done.5
  28.2 0.2 copy.20
  28.4 0.2 copy.19
  28.6 0.7 dynamic-slice_bitcast_fusion.2.left_a
  29.3 0.7 dynamic-slice_bitcast_fusion.3.left_a
  30.0 10.6 %all-to-all-done.got = f32[128,2,256]{2,1,0:T(2,128)S(1)} async-done(((f32[128,2,256]{2,1,0:T(2,128)}), f32[128,2,256]{2,1,0:T(2,128)S(1)}, u32[]{:S(2)}, u32[]{:S(2)}) %all-to-all-start) | async-done | bytes 262176 | tf_op jit(solution)/shard_map/all_to_all | solution.py:412
  40.6 0.0 copy-done.2
  40.6 1.8 %shard_map.138 = (bf16[256,256]{1,0:T(8,128)(2,1)S(1)}, f32[2,256]{1,0:T(2,128)S(1)}, f32[104,256]{1,0:T(8,128)S(1)}) custom-call(s32[1,2]{1,0:T(1,128)} %len_ref.7, f32[128,2,256]{2,1,0:T(2,128)S(1)} %all-to-all-done.got, f32[8,256]{1,0:T(8,128)S(1)} %get-tuple-element.53.params, f32[256,256]{1,0:T(8,128)S(1)} %get-tuple-element.51.conv_out.conv_a, ...), custom_call_target="tpu_custom_call" | custom-call | tf_op jit(solution)/shard_map/pallas_call | solution.py:34
  42.4 1.9 %collective-permute-start.1 = (f32[104,256]{1,0:T(8,128)S(1)}, f32[104,256]{1,0:T(8,128)S(1)}, u32[]{:S(2)}, u32[]{:S(2)}) collective-permute-start(f32[104,256]{1,0:T(8,128)S(1)} %get-tuple-element.60.own), channel_id=1, source_target_pairs={{0,4},{4,0},{1,5},{5,1},{2,6},{6,2},{3,7},{7,3},{8,12},{12,8},{9,1... | collective-permute-start | bytes 319496 | tf_op jit(solution)/shard_map/ppermute | solution.py:360
  44.3 1.3 %collective-permute-done.1.other = f32[104,256]{1,0:T(8,128)S(1)} collective-permute-done((f32[104,256]{1,0:T(8,128)S(1)}, f32[104,256]{1,0:T(8,128)S(1)}, u32[]{:S(2)}, u32[]{:S(2)}) %collective-permute-start.1) | collective-permute-done | bytes 106528 | tf_op jit(solution)/shard_map/ppermute | solution.py:360
  45.6 0.8 shard_map.139
  46.4 4.6 %all-to-all-start.1 = ((f32[64,8,128]{2,1,0:T(8,128)}), f32[64,8,128]{2,1,0:T(8,128)S(1)}, u32[]{:S(2)}, u32[]{:S(2)}) async-start(f32[64,8,128]{2,1,0:T(8,128)} %shard_map.139), calls=%async_computation.1 | async-start | bytes 524288 | tf_op jit(solution)/shard_map/all_to_all | solution.py:444
  51.0 0.0 collective-permute-done.given
  51.1 1.3 %slice_bitcast_fusion = (bf16[1024,256]{0,1:T(8,128)(2,1)S(1)}, bf16[1024,256]{0,1:T(8,128)(2,1)S(1)}) fusion(bf16[528,1024]{1,0:T(8,128)(2,1)} %collective-permute-done.given), kind=kLoop, calls=%fused_computation | loop fusion | bytes 2097152 | tf_op jit(solution)/shard_map/transpose | solution.py:355
  52.3 0.2 copy.21
  52.5 0.2 copy.22
  52.7 3.7 %shard_map.140 = (f32[256,256]{1,0:T(8,128)}, f32[256,256]{1,0:T(8,128)}, f32[256,256]{1,0:T(8,128)}, f32[256,256]{1,0:T(8,128)S(1)}, bf16[256,256]{1,0:T(8,128)(2,1)S(1)}, /*index=5*/f32[8,128]{1,0:T(8,128)S(1)}) custom-call(bf16[528,1024]{1,0:T(8,128)(2,1)} %collective-permute-done.given, bf16[1024,512]{1,0:T(8,128)(2,1)} %bitcast.31, ...), custom_call_target="tpu_custom_call" | custom-call | tf_op jit(solution)/shard_map/pallas_call | solution.py:34
  56.5 0.0 copy-start.4
  56.5 0.7 dynamic-slice_bitcast_fusion
  57.2 1.9 %shard_map.141 = bf16[512,256]{1,0:T(8,128)(2,1)} custom-call(bf16[512,256]{1,0:T(8,128)(2,1)} %dynamic-slice_bitcast_fusion.2.left_a, bf16[512,256]{1,0:T(8,128)(2,1)S(1)} %get-tuple-element.95.left_b, bf16[256,256]{1,0:T(8,128)(2,1)S(1)} %get-tuple-element.65.right_a, bf16[256,256]{1,0:T(8,128)(2,1)S(1)} %get-tuple-element.66.right_b), custom_call_target="tpu_custom_call" | custom-call | tf_op jit(solution)/shard_map/pallas_call | solution.py:34
  59.1 7.2 %all-to-all-done.1.got = f32[64,8,128]{2,1,0:T(8,128)S(1)} async-done(((f32[64,8,128]{2,1,0:T(8,128)}), f32[64,8,128]{2,1,0:T(8,128)S(1)}, u32[]{:S(2)}, u32[]{:S(2)}) %all-to-all-start.1) | async-done | bytes 262176 | tf_op jit(solution)/shard_map/all_to_all | solution.py:444
  66.3 0.0 copy-done.4
  66.3 5.2 %shard_map.142 = (bf16[256,512]{1,0:T(8,128)(2,1)S(1)}, f32[1,256]{1,0:T(1,128)}, f32[1,256]{1,0:T(1,128)}, bf16[64,8,896]{2,1,0:T(8,128)(2,1)}) custom-call(s32[1,2]{1,0:T(1,128)} %len_ref.7, s32[1]{0:T(128)} %bitcast.1.half_ref, f32[8,128]{1,0:T(8,128)S(1)} %get-tuple-element.63.ends, f32[64,8,128]{2,1,0:T(8,128)S(1)} %all-to-all-done.1.got, ...), custom_call_target="tpu_custom_call" | custom-call | tf_op jit(solution)/shard_map/pallas_call | solution.py:34
  71.5 5.5 %all-to-all-start.2 = ((bf16[64,8,896]{2,1,0:T(8,128)(2,1)}), bf16[64,8,896]{2,1,0:T(8,128)(2,1)S(1)}, u32[]{:S(2)}, u32[]{:S(2)}) async-start(bf16[64,8,896]{2,1,0:T(8,128)(2,1)} %get-tuple-element.81), calls=%async_computation.2 | async-start | bytes 1835008 | tf_op jit(solution)/shard_map/all_to_all | solution.py:492
  77.1 1.7 %shard_map.143 = (bf16[256,256]{1,0:T(8,128)(2,1)S(1)}, bf16[256,256]{1,0:T(8,128)(2,1)S(1)}, bf16[256,256]{1,0:T(8,128)(2,1)S(1)}, bf16[256,256]{1,0:T(8,128)(2,1)S(1)}) custom-call(s32[1]{0:T(128)} %bitcast.mp_ref, bf16[256,512]{1,0:T(8,128)(2,1)S(1)} %get-tuple-element.78.grad_pre, bf16[1024,512]{1,0:T(8,128)(2,1)} %bitcast.32), custom_call_target="tpu_custom_call" | custom-call | tf_op jit(solution)/shard_map/pallas_call | solution.py:34
  78.8 2.4 %collective-permute-start.2 = (bf16[256,256]{1,0:T(8,128)(2,1)S(1)}, bf16[256,256]{1,0:T(8,128)(2,1)S(1)}, u32[]{:S(2)}, u32[]{:S(2)}) collective-permute-start(bf16[256,256]{1,0:T(8,128)(2,1)S(1)} %get-tuple-element.82), channel_id=1, source_target_pairs={{0,1},{1,2},{2,3},{3,0},{4,5},{5,6},{6,7},{7,4},{8,9},{9,10},{10,1... | collective-permute-start | bytes 393224 | tf_op jit(solution)/shard_map/ppermute | solution.py:501
  81.2 4.3 %collective-permute-start.3 = (bf16[256,256]{1,0:T(8,128)(2,1)S(1)}, bf16[256,256]{1,0:T(8,128)(2,1)S(1)}, u32[]{:S(2)}, u32[]{:S(2)}) collective-permute-start(bf16[256,256]{1,0:T(8,128)(2,1)S(1)} %get-tuple-element.84), channel_id=1, source_target_pairs={{0,2},{1,3},{2,0},{3,1},{4,6},{5,7},{6,4},{7,5},{8,10},{9,11},{10,... | collective-permute-start | bytes 393224 | tf_op jit(solution)/shard_map/ppermute | solution.py:501
  85.5 1.9 %collective-permute-start.4 = (bf16[256,256]{1,0:T(8,128)(2,1)S(1)}, bf16[256,256]{1,0:T(8,128)(2,1)S(1)}, u32[]{:S(2)}, u32[]{:S(2)}) collective-permute-start(bf16[256,256]{1,0:T(8,128)(2,1)S(1)} %get-tuple-element.86), channel_id=1, source_target_pairs={{0,3},{1,0},{2,1},{3,2},{4,7},{5,4},{6,5},{7,6},{8,11},{9,8},{10,9... | collective-permute-start | bytes 393224 | tf_op jit(solution)/shard_map/ppermute | solution.py:501
  87.4 0.0 collective-permute-done.2
  87.4 2.1 %collective-permute-done.3 = bf16[256,256]{1,0:T(8,128)(2,1)S(1)} collective-permute-done((bf16[256,256]{1,0:T(8,128)(2,1)S(1)}, bf16[256,256]{1,0:T(8,128)(2,1)S(1)}, u32[]{:S(2)}, u32[]{:S(2)}) %collective-permute-start.3) | collective-permute-done | bytes 131104 | tf_op jit(solution)/shard_map/ppermute | solution.py:501
  89.5 4.0 %collective-permute-done.4 = bf16[256,256]{1,0:T(8,128)(2,1)S(1)} collective-permute-done((bf16[256,256]{1,0:T(8,128)(2,1)S(1)}, bf16[256,256]{1,0:T(8,128)(2,1)S(1)}, u32[]{:S(2)}, u32[]{:S(2)}) %collective-permute-start.4) | collective-permute-done | bytes 131104 | tf_op jit(solution)/shard_map/ppermute | solution.py:501
  93.6 0.7 add_convert_fusion
  94.3 9.6 %all-to-all-done.2.got = bf16[64,8,896]{2,1,0:T(8,128)(2,1)S(1)} async-done(((bf16[64,8,896]{2,1,0:T(8,128)(2,1)}), bf16[64,8,896]{2,1,0:T(8,128)(2,1)S(1)}, u32[]{:S(2)}, u32[]{:S(2)}) %all-to-all-start.2) | async-done | bytes 917536 | tf_op jit(solution)/shard_map/all_to_all | solution.py:492
  103.9 0.8 shard_map.144
Async XLA Ops:
  0.6 1.5 %copy-start.3 = (f32[31,256]{1,0:T(8,128)S(1)}, f32[31,256]{1,0:T(8,128)}, u32[]{:S(2)}) copy-start(f32[31,256]{1,0:T(8,128)} %taps.5) | copy-start | bytes 95236
  0.6 1.5 %copy-start.1 = (bf16[256,1024]{1,0:T(8,128)(2,1)S(1)}, bf16[256,1024]{1,0:T(8,128)(2,1)}, u32[]{:S(2)}) copy-start(bf16[256,1024]{1,0:T(8,128)(2,1)} %frames.1) | copy-start | bytes 1572868
  2.2 5.4 %copy-start = (bf16[128,8,2,256]{3,1,2,0:T(8,128)(2,1)}, bf16[128,8,2,256]{3,1,2,0:T(8,128)(2,1)S(1)}, u32[]{:S(2)}) copy-start(bf16[128,8,2,256]{3,1,2,0:T(8,128)(2,1)S(1)} %copy.23) | copy-start | bytes 3145732
  5.7 45.4 %collective-permute-start = (bf16[528,1024]{1,0:T(8,128)(2,1)}, bf16[528,1024]{1,0:T(8,128)(2,1)}, u32[]{:S(2)}, u32[]{:S(2)}) collective-permute-start(bf16[528,1024]{1,0:T(8,128)(2,1)} %get-tuple-element.49), channel_id=1, source_target_pairs={{0,4},{4,0},{1,5},{5,1},{2,6},{6,2},{3,7},{7,3},{8,12},{12,8},{9,1... | collective-permute-start | bytes 3244040 | tf_op jit(solution)/shard_map/ppermute | solution.py:360
  7.6 33.0 %all-to-all-start = ((f32[128,2,256]{2,1,0:T(2,128)}), f32[128,2,256]{2,1,0:T(2,128)S(1)}, u32[]{:S(2)}, u32[]{:S(2)}) async-start(f32[128,2,256]{2,1,0:T(2,128)} %get-tuple-element.50), calls=%async_computation | async-start | bytes 524288 | tf_op jit(solution)/shard_map/all_to_all | solution.py:412
  25.5 2.6 %copy-start.5 = (bf16[256,1024]{1,0:T(8,128)(2,1)S(1)}, bf16[256,1024]{1,0:T(8,128)(2,1)}, u32[]{:S(2)}) copy-start(bf16[256,1024]{1,0:T(8,128)(2,1)} %grad_out.1) | copy-start | bytes 1572868
  28.1 12.5 %copy-start.2 = (f32[256,256]{1,0:T(8,128)}, f32[256,256]{1,0:T(8,128)S(1)}, u32[]{:S(2)}) copy-start(f32[256,256]{1,0:T(8,128)S(1)} %get-tuple-element.57.grad_hidden.hid_a) | copy-start | bytes 786436
  42.4 3.2 %collective-permute-start.1 = (f32[104,256]{1,0:T(8,128)S(1)}, f32[104,256]{1,0:T(8,128)S(1)}, u32[]{:S(2)}, u32[]{:S(2)}) collective-permute-start(f32[104,256]{1,0:T(8,128)S(1)} %get-tuple-element.60.own), channel_id=1, source_target_pairs={{0,4},{4,0},{1,5},{5,1},{2,6},{6,2},{3,7},{7,3},{8,12},{12,8},{9,1... | collective-permute-start | bytes 319496 | tf_op jit(solution)/shard_map/ppermute | solution.py:360
  46.4 19.9 %all-to-all-start.1 = ((f32[64,8,128]{2,1,0:T(8,128)}), f32[64,8,128]{2,1,0:T(8,128)S(1)}, u32[]{:S(2)}, u32[]{:S(2)}) async-start(f32[64,8,128]{2,1,0:T(8,128)} %shard_map.139), calls=%async_computation.1 | async-start | bytes 524288 | tf_op jit(solution)/shard_map/all_to_all | solution.py:444
  56.5 9.9 %copy-start.4 = (f32[31,256]{1,0:T(8,128)S(1)}, f32[31,256]{1,0:T(8,128)}, u32[]{:S(2)}) copy-start(f32[31,256]{1,0:T(8,128)} %taps.5) | copy-start | bytes 95236
  71.5 32.4 %all-to-all-start.2 = ((bf16[64,8,896]{2,1,0:T(8,128)(2,1)}), bf16[64,8,896]{2,1,0:T(8,128)(2,1)S(1)}, u32[]{:S(2)}, u32[]{:S(2)}) async-start(bf16[64,8,896]{2,1,0:T(8,128)(2,1)} %get-tuple-element.81), calls=%async_computation.2 | async-start | bytes 1835008 | tf_op jit(solution)/shard_map/all_to_all | solution.py:492
  78.8 8.6 %collective-permute-start.2 = (bf16[256,256]{1,0:T(8,128)(2,1)S(1)}, bf16[256,256]{1,0:T(8,128)(2,1)S(1)}, u32[]{:S(2)}, u32[]{:S(2)}) collective-permute-start(bf16[256,256]{1,0:T(8,128)(2,1)S(1)} %get-tuple-element.82), channel_id=1, source_target_pairs={{0,1},{1,2},{2,3},{3,0},{4,5},{5,6},{6,7},{7,4},{8,9},{9,10},{10,1... | collective-permute-start | bytes 393224 | tf_op jit(solution)/shard_map/ppermute | solution.py:501
  81.2 8.4 %collective-permute-start.3 = (bf16[256,256]{1,0:T(8,128)(2,1)S(1)}, bf16[256,256]{1,0:T(8,128)(2,1)S(1)}, u32[]{:S(2)}, u32[]{:S(2)}) collective-permute-start(bf16[256,256]{1,0:T(8,128)(2,1)S(1)} %get-tuple-element.84), channel_id=1, source_target_pairs={{0,2},{1,3},{2,0},{3,1},{4,6},{5,7},{6,4},{7,5},{8,10},{9,11},{10,... | collective-permute-start | bytes 393224 | tf_op jit(solution)/shard_map/ppermute | solution.py:501
  85.5 8.1 %collective-permute-start.4 = (bf16[256,256]{1,0:T(8,128)(2,1)S(1)}, bf16[256,256]{1,0:T(8,128)(2,1)S(1)}, u32[]{:S(2)}, u32[]{:S(2)}) collective-permute-start(bf16[256,256]{1,0:T(8,128)(2,1)S(1)} %get-tuple-element.86), channel_id=1, source_target_pairs={{0,3},{1,0},{2,1},{3,2},{4,7},{5,4},{6,5},{7,6},{8,11},{9,8},{10,9... | collective-permute-start | bytes 393224 | tf_op jit(solution)/shard_map/ppermute | solution.py:501

commit v9 on v8

--- a/solution.py
+++ b/solution.py
@@ -23,7 +23,11 @@
 
 def call(body, outs, ins, scratch=(), out_specs=None):
     kernel = pl.pallas_call(
-        body, out_shape=outs, in_specs=ins, out_specs=out_specs or tuple(VM for _ in outs), scratch_shapes=list(scratch)
+        body,
+        out_shape=outs,
+        in_specs=ins,
+        out_specs=out_specs or tuple(VM for _ in outs),
+        scratch_shapes=list(scratch),
     )
 
     def run(*args):
@@ -187,8 +191,8 @@
 
 
 def mirror_kernel(
-    given, proj, proj_out, taps, stats, params,
-    value, sig, grad_hidden, conv_out, hidden, ends, pre, hid, buf,
+    given, proj, proj_out, taps, stats, params, left_a, left_b, hidden_a,
+    value, sig, grad_hidden, conv_out, out_rows, ends, pre, hid, buf, hidden,
 ):
     rows, channels = conv_out.shape
     spans = given[2 * rows : 2 * rows + 16, :LANES].astype(F32)[0:1]
@@ -209,6 +213,9 @@
         grad_hidden[:, cols] = jnp.where(live, hid[:, cols], 0.0)
         _, scaled, s = batch_norm(conv_out, mean, inv_std, params, cols)
         hidden[:, cols] = jnp.where(live, scaled * s, 0.0).astype(BF16)
+    total = jnp.dot(left_a[...], hidden_a[...], preferred_element_type=F32)
+    total = total + jnp.dot(left_b[...], hidden[...], preferred_element_type=F32)
+    out_rows[...] = total.astype(BF16)
 
 
 def norm_kernel(
@@ -291,12 +298,14 @@
         masks = own_masks(len_ref, rows) if part == 0 else row_masks(ends[0:1], ends[1:2], rows)
         first, live = masks
         span = slice(part * rows, (part + 1) * rows)
-        copies[part].wait()
         for h in range(channels // LANES):
             cols = lanes(h)
             s, q = means[h]
             norm, scaled, swish = batch_norm(conv_out, mean, inv_std, params, cols)
-            grad = scales[h] * (hids[part, :, cols] * swish_slope(scaled, swish) - s - norm * q)
+            slope = swish_slope(scaled, swish)
+            if h == 0:
+                copies[part].wait()
+            grad = scales[h] * (hids[part, :, cols] * slope - s - norm * q)
             embed(work, h, jnp.where(live, grad, 0.0), first)
             glu = jnp.where(live, conv(work, h, taps, rows, first, -1), 0.0)
             if h == 0:
@@ -326,12 +335,6 @@
         at = pl.multiple_of(lax.rem(mp_ref[0] + d, groups) * width, width)
         term = lax.dot_general(grad_pre[...], proj[pl.ds(at, width), :], NT, preferred_element_type=F32)
         out[...] = term.astype(BF16)
-
-
-def rows_kernel(left_a, left_b, right_a, right_b, out):
-    total = jnp.dot(left_a[...], right_a[...], preferred_element_type=F32)
-    total = total + jnp.dot(left_b[...], right_b[...], preferred_element_type=F32)
-    out[...] = total.astype(BF16)
 
 
 def last_kernel(got, in_rows, out_rows, depth):
@@ -439,29 +442,29 @@
         [work],
     )(lengths, got, params, conv_a, hid_a, buf_a, ones_a, conv_sum_a)
     (pay,) = call(
-        spread_kernel, (hbm_shape((chips, 8, LANES)),), [VM, VM], [pltpu.VMEM((3 * (count + 1) + 8, channels), F32)]
+        spread_kernel,
+        (hbm_shape((chips, 8, LANES)),),
+        [VM, VM],
+        [pltpu.VMEM((3 * (count + 1) + 8, channels), F32)],
     )(sums, swap_cores(sums))
     got = lax.all_to_all(pay, YZ, 0, 0)
 
     given = after(given, pay)
-    value_b, sig_b, hid_b, conv_b, hidden_b, ends = call(
+    left_in_b = core_rows(given[:rows], core)
+    left_out_b = core_rows(given[rows : 2 * rows], core)
+    value_b, sig_b, hid_b, conv_b, out_rows, ends = call(
         mirror_kernel,
         (
             hbm_shape((rows, channels)),
             hbm_shape((rows, channels)),
             hbm_shape((rows, channels)),
             full,
-            shape((rows, channels), BF16),
+            hbm_shape((width // 2, channels), BF16),
             shape((8, LANES)),
         ),
-        [HB, HB, HB, HB, VM, VM],
-        [wide, square, work],
-    )(given, proj, proj_out, taps, stats, params)
-    left_in_b = core_rows(given[:rows], core)
-    left_out_b = core_rows(given[rows : 2 * rows], core)
-    (out_rows,) = call(rows_kernel, (hbm_shape((width // 2, channels), BF16),), [HB, VM, VM, VM])(
-        left_out_a, left_out_b, hidden_a, hidden_b
-    )
+        [HB, HB, HB, HB, VM, VM, HB, VM, VM],
+        [wide, square, work, pltpu.VMEM((rows, channels), BF16)],
+    )(given, proj, proj_out, taps, stats, params, left_out_a, left_out_b, hidden_a)
     got, out_rows, left_in_a, left_in_b = lax.optimization_barrier((got, out_rows, left_in_a, left_in_b))
     out_rows = out_rows.reshape(chips, rows_dev, channels)
 

time: 106 us -> 105 us (level)
  Pallas kernels: 21.9 us -> 20.5 us
    ppermute x3, waiting for transfers between devices: 6.14 us -> 3.5 us  [shards(): lax.ppermute(after(part, pay), 'mp', [(i, (i + d) % groups) for i in rang...]
    all_to_all x2, waiting for transfers between devices: 16.8 us -> 19.3 us  [shards(): got = lax.all_to_all(pay, YZ, 0, 0)]
    pallas_call x9 -> x8, Pallas kernels: 21.9 us -> 20.5 us  [run(): return kernel(*held)]
    ppermute x3, starting transfers between devices: 8.62 us -> 9.76 us  [shards(): lax.ppermute(after(part, pay), 'mp', [(i, (i + d) % groups) for i in rang...]
  transfers between devices with their start and end apart: 8 -> 8, of which waited for: 6 -> 6; matrix products, arithmetic and copies ran while one was open for 5% -> 4% of each run, Pallas kernels for 12% -> 11%
where the time goes in v9:
time: 105 us; the launch traced here: 103 us
  starting transfers between devices  40.8 us (39%)
  waiting for transfers between devices  35.3 us (34%)
  Pallas kernels  20.5 us (20%)
  local copies, waits for them, and re-layouts  5.2 us (5%)
    pallas_call x8, Pallas kernels, run(): return kernel(*held)  20.5 us
    all_to_all x2, waiting for transfers between devices, shards(): got = lax.all_to_all(pay, YZ, 0, 0)  19.3 us
    all_to_all x1, starting transfers between devices, shards(): got = lax.all_to_all(pay, DP, 0, 0)  17.9 us
    all_to_all x1, waiting for transfers between devices, shards(): got = lax.all_to_all(pay, DP, 0, 0)  11.2 us
    ppermute x3, starting transfers between devices, shards(): lax.ppermute(after(part, pay), 'mp', [(i, (i + d) % groups) for i in rang...  9.76 us
    all_to_all x2, starting transfers between devices, shards(): got = lax.all_to_all(pay, YZ, 0, 0)  9.26 us
    ppermute x2, starting transfers between devices, swap_cores(): return lax.ppermute(x, 'core', [(0, 1), (1, 0)])  3.84 us
    ppermute x3, waiting for transfers between devices, shards(): lax.ppermute(after(part, pay), 'mp', [(i, (i + d) % groups) for i in rang...  3.5 us
  transfers between devices with their start and end apart: 8, of which 6 were waited for; matrix products, arithmetic and copies ran while one was open for 4% of the time, Pallas kernels for 11%

profile of v9, /device:TPU:6, one launch (start us, length us, event | category | flops | bytes accessed | tf_op | source)
XLA Modules:
  0.0 103.3 jit_solution(9812552701224142519)
XLA Ops:
  0.6 0.0 copy-start.3
  0.6 0.0 copy-start.1
  0.7 1.5 %copy.23 = bf16[128,8,2,256]{3,1,2,0:T(8,128)(2,1)S(1)} copy(bf16[128,8,2,256]{3,2,1,0:T(2,128)(2,1)} %bitcast.37) | data formatting | bytes 2097152
  2.2 0.0 copy-start
  2.2 0.0 copy-done.3
  2.2 0.0 copy-done.1
  2.2 3.5 %shard_map.136 = (f32[256,256]{1,0:T(8,128)S(1)}, f32[2,304,128]{2,1,0:T(8,128)S(1)}, f32[128,2,256]{2,1,0:T(2,128)}, f32[256,256]{1,0:T(8,128)}, f32[256,256]{1,0:T(8,128)}, /*index=5*/bf16[528,1024]{1,0:T(8,128)(2,1)}) custom-call(s32[1,2]{1,0:T(1,128)} %len_ref.7, bf16[256,1024]{1,0:T(8,128)(2,1)S(1)} %copy-done.1, bf16[1024,512]{1,0:T(8,128)(2,1)S(1)} %bitcast.30, ...), custom_call_target="tpu_custom_call" | custom-call | tf_op jit(solution)/shard_map/pallas_call | solution.py:38
  5.7 1.9 %collective-permute-start = (bf16[528,1024]{1,0:T(8,128)(2,1)}, bf16[528,1024]{1,0:T(8,128)(2,1)}, u32[]{:S(2)}, u32[]{:S(2)}) collective-permute-start(bf16[528,1024]{1,0:T(8,128)(2,1)} %get-tuple-element.49), channel_id=1, source_target_pairs={{0,4},{4,0},{1,5},{5,1},{2,6},{6,2},{3,7},{7,3},{8,12},{12,8},{9,1... | collective-permute-start | bytes 3244040 | tf_op jit(solution)/shard_map/ppermute | solution.py:363
  7.6 0.0 copy-done
  7.6 17.9 %all-to-all-start = ((f32[128,2,256]{2,1,0:T(2,128)}), f32[128,2,256]{2,1,0:T(2,128)S(1)}, u32[]{:S(2)}, u32[]{:S(2)}) async-start(f32[128,2,256]{2,1,0:T(2,128)} %get-tuple-element.50), calls=%async_computation | async-start | bytes 524288 | tf_op jit(solution)/shard_map/all_to_all | solution.py:415
  25.5 0.0 copy-start.5
  25.6 2.6 %shard_map.137 = (f32[256,256]{1,0:T(8,128)S(1)}, f32[32,256]{1,0:T(8,128)S(1)}, f32[32,256]{1,0:T(8,128)S(1)}, f32[8,256]{1,0:T(8,128)S(1)}) custom-call(s32[1,2]{1,0:T(1,128)} %len_ref.7, bf16[256,1024]{1,0:T(8,128)(2,1)} %grad_out.1, bf16[1024,256]{1,0:T(8,128)(2,1)} %proj_out.3, f32[256,256]{1,0:T(8,128)S(1)} %get-tuple-element.51.conv_out.conv_a, ...), custom_call_target="tpu_custom_call" | custom-call | tf_op jit(solution)/shard_map/pallas_call | solution.py:38
  28.2 0.0 copy-start.2
  28.2 0.2 copy.19
  28.4 0.0 copy-done.5
  28.4 0.2 copy.20
  28.6 0.8 dynamic-slice_bitcast_fusion.2
  29.4 11.2 %all-to-all-done.got = f32[128,2,256]{2,1,0:T(2,128)S(1)} async-done(((f32[128,2,256]{2,1,0:T(2,128)}), f32[128,2,256]{2,1,0:T(2,128)S(1)}, u32[]{:S(2)}, u32[]{:S(2)}) %all-to-all-start) | async-done | bytes 262176 | tf_op jit(solution)/shard_map/all_to_all | solution.py:415
  40.6 0.0 copy-done.2
  40.6 1.8 %shard_map.138 = (bf16[256,256]{1,0:T(8,128)(2,1)S(1)}, f32[2,256]{1,0:T(2,128)S(1)}, f32[104,256]{1,0:T(8,128)S(1)}) custom-call(s32[1,2]{1,0:T(1,128)} %len_ref.7, f32[128,2,256]{2,1,0:T(2,128)S(1)} %all-to-all-done.got, f32[8,256]{1,0:T(8,128)S(1)} %get-tuple-element.53.params, f32[256,256]{1,0:T(8,128)S(1)} %get-tuple-element.51.conv_out.conv_a, ...), custom_call_target="tpu_custom_call" | custom-call | tf_op jit(solution)/shard_map/pallas_call | solution.py:38
  42.4 1.9 %collective-permute-start.1 = (f32[104,256]{1,0:T(8,128)S(1)}, f32[104,256]{1,0:T(8,128)S(1)}, u32[]{:S(2)}, u32[]{:S(2)}) collective-permute-start(f32[104,256]{1,0:T(8,128)S(1)} %get-tuple-element.60.own), channel_id=1, source_target_pairs={{0,4},{4,0},{1,5},{5,1},{2,6},{6,2},{3,7},{7,3},{8,12},{12,8},{9,1... | collective-permute-start | bytes 319496 | tf_op jit(solution)/shard_map/ppermute | solution.py:363
  44.4 1.3 %collective-permute-done.1.other = f32[104,256]{1,0:T(8,128)S(1)} collective-permute-done((f32[104,256]{1,0:T(8,128)S(1)}, f32[104,256]{1,0:T(8,128)S(1)}, u32[]{:S(2)}, u32[]{:S(2)}) %collective-permute-start.1) | collective-permute-done | bytes 106528 | tf_op jit(solution)/shard_map/ppermute | solution.py:363
  45.6 0.8 shard_map.139
  46.4 4.6 %all-to-all-start.1 = ((f32[64,8,128]{2,1,0:T(8,128)}), f32[64,8,128]{2,1,0:T(8,128)S(1)}, u32[]{:S(2)}, u32[]{:S(2)}) async-start(f32[64,8,128]{2,1,0:T(8,128)} %shard_map.139), calls=%async_computation.1 | async-start | bytes 524288 | tf_op jit(solution)/shard_map/all_to_all | solution.py:450
  51.1 0.0 collective-permute-done.given
  51.1 1.3 %slice_bitcast_fusion = (bf16[1024,256]{0,1:T(8,128)(2,1)S(1)}, bf16[1024,256]{0,1:T(8,128)(2,1)S(1)}) fusion(bf16[528,1024]{1,0:T(8,128)(2,1)} %collective-permute-done.given), kind=kLoop, calls=%fused_computation | loop fusion | bytes 2097152 | tf_op jit(solution)/shard_map/transpose | solution.py:358
  52.3 0.2 copy.22
  52.6 0.2 copy.21
  52.8 0.0 copy-start.4
  52.8 4.1 %shard_map.140 = (f32[256,256]{1,0:T(8,128)}, f32[256,256]{1,0:T(8,128)}, f32[256,256]{1,0:T(8,128)}, f32[256,256]{1,0:T(8,128)S(1)}, bf16[512,256]{1,0:T(8,128)(2,1)}, /*index=5*/f32[8,128]{1,0:T(8,128)S(1)}) custom-call(bf16[528,1024]{1,0:T(8,128)(2,1)} %collective-permute-done.given, bf16[1024,512]{1,0:T(8,128)(2,1)} %bitcast.31, ...), custom_call_target="tpu_custom_call" | custom-call | tf_op jit(solution)/shard_map/pallas_call | solution.py:38
  57.0 0.7 dynamic-slice_bitcast_fusion.left_b
  57.7 8.7 %all-to-all-done.1.got = f32[64,8,128]{2,1,0:T(8,128)S(1)} async-done(((f32[64,8,128]{2,1,0:T(8,128)}), f32[64,8,128]{2,1,0:T(8,128)S(1)}, u32[]{:S(2)}, u32[]{:S(2)}) %all-to-all-start.1) | async-done | bytes 262176 | tf_op jit(solution)/shard_map/all_to_all | solution.py:450
  66.3 0.0 copy-done.4
  66.4 5.2 %shard_map.141 = (bf16[256,512]{1,0:T(8,128)(2,1)S(1)}, f32[1,256]{1,0:T(1,128)}, f32[1,256]{1,0:T(1,128)}, bf16[64,8,896]{2,1,0:T(8,128)(2,1)}) custom-call(s32[1,2]{1,0:T(1,128)} %len_ref.7, s32[1]{0:T(128)} %bitcast.1.half_ref, f32[8,128]{1,0:T(8,128)S(1)} %get-tuple-element.65.ends, f32[64,8,128]{2,1,0:T(8,128)S(1)} %all-to-all-done.1.got, ...), custom_call_target="tpu_custom_call" | custom-call | tf_op jit(solution)/shard_map/pallas_call | solution.py:38
  71.6 4.7 %all-to-all-start.2 = ((bf16[64,8,896]{2,1,0:T(8,128)(2,1)}), bf16[64,8,896]{2,1,0:T(8,128)(2,1)S(1)}, u32[]{:S(2)}, u32[]{:S(2)}) async-start(bf16[64,8,896]{2,1,0:T(8,128)(2,1)} %get-tuple-element.81), calls=%async_computation.2 | async-start | bytes 1835008 | tf_op jit(solution)/shard_map/all_to_all | solution.py:495
  76.2 1.7 %shard_map.142 = (bf16[256,256]{1,0:T(8,128)(2,1)S(1)}, bf16[256,256]{1,0:T(8,128)(2,1)S(1)}, bf16[256,256]{1,0:T(8,128)(2,1)S(1)}, bf16[256,256]{1,0:T(8,128)(2,1)S(1)}) custom-call(s32[1]{0:T(128)} %bitcast.mp_ref, bf16[256,512]{1,0:T(8,128)(2,1)S(1)} %get-tuple-element.78.grad_pre, bf16[1024,512]{1,0:T(8,128)(2,1)} %bitcast.32), custom_call_target="tpu_custom_call" | custom-call | tf_op jit(solution)/shard_map/pallas_call | solution.py:38
  77.9 2.7 %collective-permute-start.4 = (bf16[256,256]{1,0:T(8,128)(2,1)S(1)}, bf16[256,256]{1,0:T(8,128)(2,1)S(1)}, u32[]{:S(2)}, u32[]{:S(2)}) collective-permute-start(bf16[256,256]{1,0:T(8,128)(2,1)S(1)} %get-tuple-element.86), channel_id=1, source_target_pairs={{0,3},{1,0},{2,1},{3,2},{4,7},{5,4},{6,5},{7,6},{8,11},{9,8},{10,9... | collective-permute-start | bytes 393224 | tf_op jit(solution)/shard_map/ppermute | solution.py:504
  80.7 3.0 %collective-permute-start.3 = (bf16[256,256]{1,0:T(8,128)(2,1)S(1)}, bf16[256,256]{1,0:T(8,128)(2,1)S(1)}, u32[]{:S(2)}, u32[]{:S(2)}) collective-permute-start(bf16[256,256]{1,0:T(8,128)(2,1)S(1)} %get-tuple-element.84), channel_id=1, source_target_pairs={{0,2},{1,3},{2,0},{3,1},{4,6},{5,7},{6,4},{7,5},{8,10},{9,11},{10,... | collective-permute-start | bytes 393224 | tf_op jit(solution)/shard_map/ppermute | solution.py:504
  83.7 4.0 %collective-permute-start.2 = (bf16[256,256]{1,0:T(8,128)(2,1)S(1)}, bf16[256,256]{1,0:T(8,128)(2,1)S(1)}, u32[]{:S(2)}, u32[]{:S(2)}) collective-permute-start(bf16[256,256]{1,0:T(8,128)(2,1)S(1)} %get-tuple-element.82), channel_id=1, source_target_pairs={{0,1},{1,2},{2,3},{3,0},{4,5},{5,6},{6,7},{7,4},{8,9},{9,10},{10,1... | collective-permute-start | bytes 393224 | tf_op jit(solution)/shard_map/ppermute | solution.py:504
  87.7 0.0 collective-permute-done.4
  87.7 1.3 %collective-permute-done.3 = bf16[256,256]{1,0:T(8,128)(2,1)S(1)} collective-permute-done((bf16[256,256]{1,0:T(8,128)(2,1)S(1)}, bf16[256,256]{1,0:T(8,128)(2,1)S(1)}, u32[]{:S(2)}, u32[]{:S(2)}) %collective-permute-start.3) | collective-permute-done | bytes 131104 | tf_op jit(solution)/shard_map/ppermute | solution.py:504
  89.1 2.2 %collective-permute-done.2 = bf16[256,256]{1,0:T(8,128)(2,1)S(1)} collective-permute-done((bf16[256,256]{1,0:T(8,128)(2,1)S(1)}, bf16[256,256]{1,0:T(8,128)(2,1)S(1)}, u32[]{:S(2)}, u32[]{:S(2)}) %collective-permute-start.2) | collective-permute-done | bytes 131104 | tf_op jit(solution)/shard_map/ppermute | solution.py:504
  91.2 0.7 add_convert_fusion
  92.0 10.6 %all-to-all-done.2.got = bf16[64,8,896]{2,1,0:T(8,128)(2,1)S(1)} async-done(((bf16[64,8,896]{2,1,0:T(8,128)(2,1)}), bf16[64,8,896]{2,1,0:T(8,128)(2,1)S(1)}, u32[]{:S(2)}, u32[]{:S(2)}) %all-to-all-start.2) | async-done | bytes 917536 | tf_op jit(solution)/shard_map/all_to_all | solution.py:495
  102.6 0.8 shard_map.143
  (1 shorter events, 0.0 us)
Async XLA Ops:
  0.6 1.5 %copy-start.3 = (f32[31,256]{1,0:T(8,128)S(1)}, f32[31,256]{1,0:T(8,128)}, u32[]{:S(2)}) copy-start(f32[31,256]{1,0:T(8,128)} %taps.5) | copy-start | bytes 95236
  0.6 1.5 %copy-start.1 = (bf16[256,1024]{1,0:T(8,128)(2,1)S(1)}, bf16[256,1024]{1,0:T(8,128)(2,1)}, u32[]{:S(2)}) copy-start(bf16[256,1024]{1,0:T(8,128)(2,1)} %frames.1) | copy-start | bytes 1572868
  2.2 5.4 %copy-start = (bf16[128,8,2,256]{3,1,2,0:T(8,128)(2,1)}, bf16[128,8,2,256]{3,1,2,0:T(8,128)(2,1)S(1)}, u32[]{:S(2)}) copy-start(bf16[128,8,2,256]{3,1,2,0:T(8,128)(2,1)S(1)} %copy.23) | copy-start | bytes 3145732
  5.7 45.4 %collective-permute-start = (bf16[528,1024]{1,0:T(8,128)(2,1)}, bf16[528,1024]{1,0:T(8,128)(2,1)}, u32[]{:S(2)}, u32[]{:S(2)}) collective-permute-start(bf16[528,1024]{1,0:T(8,128)(2,1)} %get-tuple-element.49), channel_id=1, source_target_pairs={{0,4},{4,0},{1,5},{5,1},{2,6},{6,2},{3,7},{7,3},{8,12},{12,8},{9,1... | collective-permute-start | bytes 3244040 | tf_op jit(solution)/shard_map/ppermute | solution.py:363
  7.6 33.0 %all-to-all-start = ((f32[128,2,256]{2,1,0:T(2,128)}), f32[128,2,256]{2,1,0:T(2,128)S(1)}, u32[]{:S(2)}, u32[]{:S(2)}) async-start(f32[128,2,256]{2,1,0:T(2,128)} %get-tuple-element.50), calls=%async_computation | async-start | bytes 524288 | tf_op jit(solution)/shard_map/all_to_all | solution.py:415
  25.5 2.8 %copy-start.5 = (bf16[256,1024]{1,0:T(8,128)(2,1)S(1)}, bf16[256,1024]{1,0:T(8,128)(2,1)}, u32[]{:S(2)}) copy-start(bf16[256,1024]{1,0:T(8,128)(2,1)} %grad_out.1) | copy-start | bytes 1572868
  28.2 12.5 %copy-start.2 = (f32[256,256]{1,0:T(8,128)}, f32[256,256]{1,0:T(8,128)S(1)}, u32[]{:S(2)}) copy-start(f32[256,256]{1,0:T(8,128)S(1)} %get-tuple-element.57.grad_hidden.hid_a) | copy-start | bytes 786436
  42.4 3.2 %collective-permute-start.1 = (f32[104,256]{1,0:T(8,128)S(1)}, f32[104,256]{1,0:T(8,128)S(1)}, u32[]{:S(2)}, u32[]{:S(2)}) collective-permute-start(f32[104,256]{1,0:T(8,128)S(1)} %get-tuple-element.60.own), channel_id=1, source_target_pairs={{0,4},{4,0},{1,5},{5,1},{2,6},{6,2},{3,7},{7,3},{8,12},{12,8},{9,1... | collective-permute-start | bytes 319496 | tf_op jit(solution)/shard_map/ppermute | solution.py:363
  46.4 19.9 %all-to-all-start.1 = ((f32[64,8,128]{2,1,0:T(8,128)}), f32[64,8,128]{2,1,0:T(8,128)S(1)}, u32[]{:S(2)}, u32[]{:S(2)}) async-start(f32[64,8,128]{2,1,0:T(8,128)} %shard_map.139), calls=%async_computation.1 | async-start | bytes 524288 | tf_op jit(solution)/shard_map/all_to_all | solution.py:450
  52.8 13.6 %copy-start.4 = (f32[31,256]{1,0:T(8,128)S(1)}, f32[31,256]{1,0:T(8,128)}, u32[]{:S(2)}) copy-start(f32[31,256]{1,0:T(8,128)} %taps.5) | copy-start | bytes 95236
  71.6 31.0 %all-to-all-start.2 = ((bf16[64,8,896]{2,1,0:T(8,128)(2,1)}), bf16[64,8,896]{2,1,0:T(8,128)(2,1)S(1)}, u32[]{:S(2)}, u32[]{:S(2)}) async-start(bf16[64,8,896]{2,1,0:T(8,128)(2,1)} %get-tuple-element.81), calls=%async_computation.2 | async-start | bytes 1835008 | tf_op jit(solution)/shard_map/all_to_all | solution.py:495
  77.9 9.8 %collective-permute-start.4 = (bf16[256,256]{1,0:T(8,128)(2,1)S(1)}, bf16[256,256]{1,0:T(8,128)(2,1)S(1)}, u32[]{:S(2)}, u32[]{:S(2)}) collective-permute-start(bf16[256,256]{1,0:T(8,128)(2,1)S(1)} %get-tuple-element.86), channel_id=1, source_target_pairs={{0,3},{1,0},{2,1},{3,2},{4,7},{5,4},{6,5},{7,6},{8,11},{9,8},{10,9... | collective-permute-start | bytes 393224 | tf_op jit(solution)/shard_map/ppermute | solution.py:504
  80.7 8.4 %collective-permute-start.3 = (bf16[256,256]{1,0:T(8,128)(2,1)S(1)}, bf16[256,256]{1,0:T(8,128)(2,1)S(1)}, u32[]{:S(2)}, u32[]{:S(2)}) collective-permute-start(bf16[256,256]{1,0:T(8,128)(2,1)S(1)} %get-tuple-element.84), channel_id=1, source_target_pairs={{0,2},{1,3},{2,0},{3,1},{4,6},{5,7},{6,4},{7,5},{8,10},{9,11},{10,... | collective-permute-start | bytes 393224 | tf_op jit(solution)/shard_map/ppermute | solution.py:504
  83.7 7.5 %collective-permute-start.2 = (bf16[256,256]{1,0:T(8,128)(2,1)S(1)}, bf16[256,256]{1,0:T(8,128)(2,1)S(1)}, u32[]{:S(2)}, u32[]{:S(2)}) collective-permute-start(bf16[256,256]{1,0:T(8,128)(2,1)S(1)} %get-tuple-element.82), channel_id=1, source_target_pairs={{0,1},{1,2},{2,3},{3,0},{4,5},{5,6},{6,7},{7,4},{8,9},{9,10},{10,1... | collective-permute-start | bytes 393224 | tf_op jit(solution)/shard_map/ppermute | solution.py:504
